TPU v7x, 256 devices: a whole 4x4x8 slice. The times are simulated.
256 devices in a mesh: dom: 64 (over y, z, core), mat: 4 (over x).
Axes of the slice: x: 4, y: 4, z: 8, core: 2. Of those that a mesh axis runs over, the one named last changes fastest.
Arguments:
- orbitals: bfloat16 [16384, 12, 32, 128], P('dom', None, 'mat')
- potential: float32 [256, 32, 128], P('dom', 'mat'), may hold values from -3 to 3
- centre_first: int32 [16384], P('dom'), may hold values from 0 to 3
- centre_second: int32 [16384], P('dom'), may hold values from 0 to 31
- centre_third: int32 [16384], P('dom'), may hold values from 0 to 127
- correlation_pairs: int32 [128, 5, 2], P('dom'), may hold values from 0 to 1, as said below
Outputs:
- gram_rows: float32 [5, 256, 16384], P(None, 'mat', 'dom')
- hamiltonian_rows: float32 [5, 256, 16384], P(None, 'mat', 'dom')
Inputs may be any that keep to these rules, and one draw needn't show every extreme that they name: correlation_pairs[g, k, b] refers to block b of the domain k - 2 away from block g's owner (wrapping); the pattern is symmetric between the two blocks, and every pair of blocks of one domain is 1.
All inputs are finite; a program needn't handle non-finite values.
Results may differ from a plain program's by a relative error of at most 0.00043.
Values may be sent and summed in bfloat16 or wider, within the bound.
A program may use at most 128 MiB of HBM per device.

v0:
```python
import jax
import jax.numpy as jnp
from jax import lax
from jax.sharding import PartitionSpec as P


def extended_2(array, sides, width):
    for axis, dim in sides:
        size, length = (lax.axis_size(axis), array.shape[dim])
        up = [(i, (i + 1) % size) for i in range(size)]
        down = [(j, i) for i, j in up]
        last = lax.slice_in_dim(array, length - width, length, axis=dim)
        first = lax.slice_in_dim(array, 0, width, axis=dim)
        before = lax.ppermute(last, axis, up)
        after = lax.ppermute(first, axis, down)
        array = jnp.concatenate([before, array, after], axis=dim)
    return array


def passed_along(block, axis, distance):
    devices = range(lax.axis_size(axis))
    route = [((i - distance) % len(devices), i) for i in devices]
    return lax.ppermute(block, axis, route)


def sphere_mask(
    centre_first,
    centre_second,
    centre_third,
    window_cells,
    patch_cells,
    second_cells,
    second_start,
    second_total,
    third_cells,
):
    planes = lax.iota(jnp.int32, window_cells)
    off_first = planes[None, :] - (patch_cells + centre_first[:, None])
    interior = (planes >= 1) & (planes <= window_cells - 2)
    second_coord = second_start + lax.iota(jnp.int32, second_cells)
    off_second = jnp.mod(second_coord[None, :] - centre_second[:, None], second_total)
    off_second = jnp.minimum(off_second, second_total - off_second)
    off_third = lax.iota(jnp.int32, third_cells)[None, :] - centre_third[:, None]
    radius = window_cells // 2
    distance = (
        (off_first * off_first)[:, :, None, None]
        + (off_second * off_second)[:, None, :, None]
        + (off_third * off_third)[:, None, None, :]
    )
    return (distance <= radius * radius) & interior[None, :, None, None]


def stencil(extended, potential_slab):
    centre_cells = extended[:, 1:-1, 1:-1, :].astype(jnp.float32)
    beside = extended[:, 2:, 1:-1, :].astype(jnp.float32) + extended[:, :-2, 1:-1, :].astype(
        jnp.float32
    )
    beside = (
        beside
        + extended[:, 1:-1, 2:, :].astype(jnp.float32)
        + extended[:, 1:-1, :-2, :].astype(jnp.float32)
    )
    third_padded = jnp.pad(centre_cells, ((0, 0), (0, 0), (0, 0), (1, 1)))
    beside = beside + third_padded[..., 2:] + third_padded[..., :-2]
    return 0.5 * (6.0 * centre_cells - beside) + potential_slab[None] * centre_cells


def pair_product(left, right):
    return lax.dot_general(
        left, right, (((1, 2, 3), (1, 2, 3)), ((), ())), preferred_element_type=jnp.float32
    )


def ring_scatter(full, axis):
    count = lax.axis_size("mat")
    me = lax.axis_index("mat")
    share = full.shape[axis] // count
    split = full.shape[-1] // 2
    halves = (full[..., :split], full[..., split:])
    forward = [(i, (i + 1) % count) for i in range(count)]
    backward = [((i + 1) % count, i) for i in range(count)]

    def chunk(values, index):
        return lax.dynamic_slice_in_dim(values, index * share, share, axis=axis)

    ahead = chunk(halves[0], lax.rem(me + count - 1, count))
    behind = chunk(halves[1], lax.rem(me + 1, count))
    for step in range(count - 1):
        ahead = lax.ppermute(ahead, "mat", forward)
        behind = lax.ppermute(behind, "mat", backward)
        ahead = ahead + chunk(halves[0], lax.rem(me + 2 * count - 2 - step, count))
        behind = behind + chunk(halves[1], lax.rem(me + 2 + step, count))
    return jnp.concatenate([ahead, behind], axis=-1)


def on_device(orbitals, potential, centre_first, centre_second, centre_third, correlation_pairs):
    block_orbs, window_cells, second_cells, third_cells = orbitals.shape
    patch_cells = potential.shape[0]
    local_blocks = correlation_pairs.shape[0]
    per_block = block_orbs // local_blocks
    mat_count = lax.axis_size("mat")
    second_start = lax.axis_index("mat") * second_cells
    inside = sphere_mask(
        centre_first,
        centre_second,
        centre_third,
        window_cells,
        patch_cells,
        second_cells,
        second_start,
        second_cells * mat_count,
        third_cells,
    )
    masked = jnp.where(inside, orbitals, jnp.zeros_like(orbitals))
    upper_start = 2 * patch_cells
    to_right = masked[:, upper_start - 1 : window_cells - 1]
    to_left = masked[:, 1 : patch_cells + 1]
    from_left = passed_along(to_right, "dom", 1)
    from_right = passed_along(to_left, "dom", -1)
    mat_size = lax.axis_size("mat")
    up = [(i, (i + 1) % mat_size) for i in range(mat_size)]
    down = [(j, i) for i, j in up]
    row_above = lax.ppermute(masked[:, :, second_cells - 1], "mat", up)
    row_below = lax.ppermute(masked[:, :, 0], "mat", down)
    rows_right = jnp.stack(
        [row_above[:, upper_start - 1 : window_cells - 1], row_below[:, upper_start - 1 : window_cells - 1]]
    )
    rows_left = jnp.stack([row_above[:, 1 : patch_cells + 1], row_below[:, 1 : patch_cells + 1]])
    rows_from_left = passed_along(rows_right, "dom", 1)
    rows_from_right = passed_along(rows_left, "dom", -1)

    def with_rows(planes, rows):
        return jnp.concatenate([rows[0][:, :, None], planes, rows[1][:, :, None]], axis=2)

    zero_plane = jnp.zeros_like(masked[:, :1])
    zero_rows = jnp.zeros((2, block_orbs, 1, third_cells), masked.dtype)
    own_ext = with_rows(
        masked[:, patch_cells - 1 : upper_start + 1],
        jnp.stack([row_above[:, patch_cells - 1 : upper_start + 1], row_below[:, patch_cells - 1 : upper_start + 1]]),
    )
    left_ext = with_rows(
        jnp.concatenate([from_left, zero_plane, zero_plane], axis=1),
        jnp.concatenate([rows_from_left, zero_rows, zero_rows], axis=2),
    )
    right_ext = with_rows(
        jnp.concatenate([zero_plane, zero_plane, from_right], axis=1),
        jnp.concatenate([zero_rows, zero_rows, rows_from_right], axis=2),
    )
    phi_slots = [
        jnp.concatenate([from_left[:, 1:], zero_plane], axis=1),
        masked[:, patch_cells:upper_start],
        jnp.concatenate([zero_plane, from_right[:, :-1]], axis=1),
    ]
    applied_slots = [
        stencil(ext, potential).astype(jnp.bfloat16) for ext in (left_ext, own_ext, right_ext)
    ]
    gram_full = jnp.stack(
        [jnp.stack([pair_product(phi_slots[a], phi_slots[b]) for b in range(3)], 1) for a in range(3)]
    )
    energy_full = jnp.stack(
        [
            jnp.stack([pair_product(applied_slots[a], phi_slots[b]) for b in range(3)], 1)
            for a in range(3)
        ]
    )
    col_count = block_orbs // mat_count

    def row_blocks(full):
        assembled = jnp.pad(full[:, :, 1], ((1, 1), (0, 0), (0, 0)))
        for slot_index, offset in ((0, -1), (2, 1)):
            arrived = passed_along(full[:, :, slot_index], "dom", offset)
            assembled = assembled + jnp.pad(arrived, ((2 - slot_index, slot_index), (0, 0), (0, 0)))
        return assembled

    both = jnp.stack([row_blocks(gram_full), row_blocks(energy_full)])
    gram_rows, energy_rows = ring_scatter(both, 2)
    columns = lax.axis_index("mat") * col_count + lax.iota(jnp.int32, col_count)
    block_ids = lax.iota(jnp.int32, local_blocks)
    column_pick = ((columns // per_block)[:, None] == block_ids[None, :]).astype(jnp.float32)
    row_pick = (
        (lax.iota(jnp.int32, block_orbs) // per_block)[:, None] == block_ids[None, :]
    ).astype(jnp.float32)
    select = jnp.einsum(
        "rkb,cb,ar->kca", correlation_pairs.astype(jnp.float32), column_pick, row_pick
    )
    return (gram_rows * select, energy_rows * select)


def solution(mesh):
    return jax.shard_map(
        on_device,
        mesh=mesh,
        in_specs=(
            P("dom", None, "mat", None),
            P("dom", "mat", None),
            P("dom"),
            P("dom"),
            P("dom"),
            P("dom", None, None),
        ),
        out_specs=(P(None, "mat", "dom"), P(None, "mat", "dom")),
        check_vma=False,
    )
```

profile of v0, /device:TPU:6, one launch (start us, length us, event | category | flops | bytes accessed | tf_op | source)
XLA Modules:
  0.0 142.5 jit_solution(17266053153387009928)
XLA Ops:
  2.9 5.9 %fusion.1 = bf16[256,12,8,128]{3,0,2,1:T(8,128)(2,1)S(1)} fusion(bf16[256,12,8,128]{3,2,1,0:T(8,128)(2,1)} %param.6, s32[256,128]{1,0:T(8,128)S(1)} %subtract_multiply_fusion, s32[256,12,8]{0,2,1:T(8,128)S(1)} %broadcast_add_fusion, pred[12]{0:T(512)(128)(4,1)S(1)} %compare_and_fusion), kind=kLoop, calls=%fused_computation.2 | loop fusion | flops 12582912 | bytes 12812300 | tf_op jit(solution)/shard_map/jit(_where)/select_n | solution.py:114
  9.0 2.3 %collective-permute-start.4 = (bf16[256,12,128]{2,0,1:T(8,128)(2,1)S(1)}, bf16[256,12,128]{2,0,1:T(8,128)(2,1)S(1)}, u32[]{:S(2)}, u32[]{:S(2)}) collective-permute-start(bf16[256,12,128]{2,0,1:T(8,128)(2,1)S(1)} %get-tuple-element.5), channel_id=1, source_target_pairs={{0,1},{1,2},{2,3},{3,0},{4,5},{5,6},{6,7},{7,4},{8,9},{9,10},{10,1... | collective-permute-start | bytes 2359304 | tf_op jit(solution)/shard_map/ppermute | solution.py:123
  12.7 7.0 %collective-permute-start.1 = (bf16[256,4,8,128]{3,0,2,1:T(8,128)(2,1)S(1)}, bf16[256,4,8,128]{3,0,2,1:T(8,128)(2,1)S(1)}, u32[]{:S(2)}, u32[]{:S(2)}) collective-permute-start(bf16[256,4,8,128]{3,0,2,1:T(8,128)(2,1)S(1)} %get-tuple-element.3), channel_id=1, source_target_pairs={{4,0},{8,4},{12,8},{16,12},{20,16},{24,20},{28,24},{32,28},{36,32}... | collective-permute-start | bytes 6291464 | tf_op jit(solution)/shard_map/ppermute | solution.py:23
  20.4 7.9 %collective-permute-done.4 = bf16[256,12,128]{2,0,1:T(8,128)(2,1)S(1)} collective-permute-done((bf16[256,12,128]{2,0,1:T(8,128)(2,1)S(1)}, bf16[256,12,128]{2,0,1:T(8,128)(2,1)S(1)}, u32[]{:S(2)}, u32[]{:S(2)}) %collective-permute-start.4) | collective-permute-done | bytes 786464 | tf_op jit(solution)/shard_map/ppermute | solution.py:123
  28.4 5.1 %collective-permute-done.5 = bf16[256,12,128]{2,0,1:T(8,128)(2,1)S(1)} collective-permute-done((bf16[256,12,128]{2,0,1:T(8,128)(2,1)S(1)}, bf16[256,12,128]{2,0,1:T(8,128)(2,1)S(1)}, u32[]{:S(2)}, u32[]{:S(2)}) %collective-permute-start.5) | collective-permute-done | bytes 786464 | tf_op jit(solution)/shard_map/ppermute | solution.py:124
  33.8 5.1 %collective-permute-start.7 = (bf16[2,256,4,128]{3,1,2,0:T(8,128)(2,1)S(1)}, bf16[2,256,4,128]{3,1,2,0:T(8,128)(2,1)S(1)}, u32[]{:S(2)}, u32[]{:S(2)}) collective-permute-start(bf16[2,256,4,128]{3,1,2,0:T(8,128)(2,1)S(1)} %pad_maximum_fusion.9), channel_id=1, source_target_pairs={{4,0},{8,4},{12,8},{16,12},{20,16},{24,20},{28,24},{32,28},{36,32}... | collective-permute-start | bytes 1572872 | tf_op jit(solution)/shard_map/ppermute | solution.py:23
  39.0 8.7 %collective-permute-done.6 = bf16[2,256,4,128]{3,1,2,0:T(8,128)(2,1)S(1)} collective-permute-done((bf16[2,256,4,128]{3,1,2,0:T(8,128)(2,1)S(1)}, bf16[2,256,4,128]{3,1,2,0:T(8,128)(2,1)S(1)}, u32[]{:S(2)}, u32[]{:S(2)}) %collective-permute-start.6) | collective-permute-done | bytes 524320 | tf_op jit(solution)/shard_map/ppermute | solution.py:23
  52.6 7.0 %fusion.7 = (bf16[256,4,8,128]{3,0,2,1:T(8,128)(2,1)S(1)}, bf16[256,4,8,128]{3,0,2,1:T(8,128)(2,1)}) fusion(f32[256,4,8,128]{3,0,2,1:T(8,128)S(1)} %slice_convert_fusion.1, bf16[256,4,8,128]{3,0,2,1:T(8,128)(2,1)S(1)} %collective-permute-done, bf16[256,6,8,128]{3,0,2,1:T(8,128)(2,1)S(1)} %concatenate.44, bf16[256,6,1,128]{3,0,2,1:T(8,128)(2,1)S(1)} %get-tuple-element.20, ...), kind=kLoop, calls=%fused_computation.14 | loop fusion | flops 35651584 | bytes 28852224 | tf_op jit(solution)/shard_map/convert_element_type | solution.py:155
  59.6 2.9 %fusion.51 = f32[256,1,256]{2,0,1:T(8,128)S(1)} fusion(bf16[256,4,8,128]{3,0,2,1:T(8,128)(2,1)} %get-tuple-element.24, bf16[256,3,8,128]{3,0,2,1:T(8,128)(2,1)} %slice.187), kind=kOutput, calls=%fused_computation.70 | convolution fusion | flops 536870912 | bytes 3932160 | tf_op jit(solution)/shard_map/dot_general | solution.py:69
  68.1 3.3 %fusion.19 = bf16[256,4,8,128]{3,0,2,1:T(8,128)(2,1)S(1)} fusion(f32[256,4,8,128]{3,0,2,1:T(8,128)S(1)} %slice_convert_fusion, bf16[256,4,8,128]{3,0,2,1:T(8,128)(2,1)S(1)} %collective-permute-done.1, bf16[256,6,8,128]{3,0,2,1:T(8,128)(2,1)S(1)} %concatenate.50, bf16[256,6,1,128]{3,0,2,1:T(8,128)(2,1)S(1)} %get-tuple-element.22, ...), kind=kLoop, calls=%fused_computation.26 | loop fusion | flops 17825792 | bytes 14434304 | tf_op jit(solution)/shard_map/convert_element_type | solution.py:155
  77.7 5.2 %collective-permute-start.8 = (f32[3,256,256]{2,1,0:T(8,128)}, f32[3,256,256]{2,1,0:T(8,128)}, u32[]{:S(2)}, u32[]{:S(2)}) collective-permute-start(f32[3,256,256]{2,1,0:T(8,128)} %get-tuple-element.9), channel_id=1, source_target_pairs={{4,0},{8,4},{12,8},{16,12},{20,16},{24,20},{28,24},{32,28},{36,32}... | collective-permute-start | bytes 2359304 | tf_op jit(solution)/shard_map/ppermute | solution.py:23
  87.6 5.1 %collective-permute-start.2 = (f32[3,256,256]{2,1,0:T(8,128)}, f32[3,256,256]{2,1,0:T(8,128)}, u32[]{:S(2)}, u32[]{:S(2)}) collective-permute-start(f32[3,256,256]{2,1,0:T(8,128)} %get-tuple-element.12), channel_id=1, source_target_pairs={{4,0},{8,4},{12,8},{16,12},{20,16},{24,20},{28,24},{32,28},{36,32}... | collective-permute-start | bytes 2359304 | tf_op jit(solution)/shard_map/ppermute | solution.py:23
  92.8 5.0 %collective-permute-done.9 = f32[3,256,256]{2,1,0:T(8,128)} collective-permute-done((f32[3,256,256]{2,1,0:T(8,128)S(1)}, f32[3,256,256]{2,1,0:T(8,128)}, u32[]{:S(2)}, u32[]{:S(2)}) %collective-permute-start.9) | collective-permute-done | bytes 786464 | tf_op jit(solution)/shard_map/ppermute | solution.py:23
  97.8 1.5 %add_bitcast_fusion = f32[1,5,256,256]{3,2,1,0:T(8,128)S(1)} fusion(f32[3,256,256]{2,1,0:T(8,128)} %collective-permute-done.9, f32[3,256,256]{2,1,0:T(8,128)} %collective-permute-done.8, f32[3,256,256]{2,1,0:T(8,128)S(1)} %get-tuple-element.7), kind=kLoop, calls=%fused_computation.64 | loop fusion | flops 655360 | bytes 3670016 | tf_op jit(solution)/shard_map/stack | solution.py:175
  99.3 3.2 %collective-permute-done.2 = f32[3,256,256]{2,1,0:T(8,128)} collective-permute-done((f32[3,256,256]{2,1,0:T(8,128)}, f32[3,256,256]{2,1,0:T(8,128)}, u32[]{:S(2)}, u32[]{:S(2)}) %collective-permute-start.2) | collective-permute-done | bytes 786464 | tf_op jit(solution)/shard_map/ppermute | solution.py:23
  102.5 5.2 %collective-permute-done.3 = f32[3,256,256]{2,1,0:T(8,128)} collective-permute-done((f32[3,256,256]{2,1,0:T(8,128)}, f32[3,256,256]{2,1,0:T(8,128)}, u32[]{:S(2)}, u32[]{:S(2)}) %collective-permute-start.3) | collective-permute-done | bytes 786464 | tf_op jit(solution)/shard_map/ppermute | solution.py:23
  107.7 1.5 %add_bitcast_fusion.1 = f32[1,5,256,256]{3,2,1,0:T(8,128)S(1)} fusion(f32[3,256,256]{2,1,0:T(8,128)} %collective-permute-done.3, f32[3,256,256]{2,1,0:T(8,128)} %collective-permute-done.2, f32[3,256,256]{2,1,0:T(8,128)S(1)} %get-tuple-element.10), kind=kLoop, calls=%fused_computation.65 | loop fusion | flops 655360 | bytes 3670016 | tf_op jit(solution)/shard_map/stack | solution.py:175
  110.5 1.8 %collective-permute-start.10 = (f32[2,5,64,128]{3,2,1,0:T(8,128)S(1)}, f32[2,5,64,128]{3,2,1,0:T(8,128)S(1)}, u32[]{:S(2)}, u32[]{:S(2)}) collective-permute-start(f32[2,5,64,128]{3,2,1,0:T(8,128)S(1)} %constant_dynamic-slice_fusion), channel_id=1, source_target_pairs={{0,1},{1,2},{2,3},{3,0},{4,5},{5,6},{6,7},{7,4},{8,9},{9,10},{10,1... | collective-permute-start | bytes 983048 | tf_op jit(solution)/shard_map/ppermute | solution.py:89
  112.7 4.9 %collective-permute-done.10 = f32[2,5,64,128]{3,2,1,0:T(8,128)S(1)} collective-permute-done((f32[2,5,64,128]{3,2,1,0:T(8,128)S(1)}, f32[2,5,64,128]{3,2,1,0:T(8,128)S(1)}, u32[]{:S(2)}, u32[]{:S(2)}) %collective-permute-start.10) | collective-permute-done | bytes 327712 | tf_op jit(solution)/shard_map/ppermute | solution.py:89
  118.7 3.8 %collective-permute-start.11 = (f32[2,5,64,128]{3,2,1,0:T(8,128)S(1)}, f32[2,5,64,128]{3,2,1,0:T(8,128)S(1)}, u32[]{:S(2)}, u32[]{:S(2)}) collective-permute-start(f32[2,5,64,128]{3,2,1,0:T(8,128)S(1)} %dynamic-slice_add_fusion.2), channel_id=1, source_target_pairs={{0,1},{1,2},{2,3},{3,0},{4,5},{5,6},{6,7},{7,4},{8,9},{9,10},{10,1... | collective-permute-start | bytes 983048 | tf_op jit(solution)/shard_map/ppermute | solution.py:89
  123.4 3.6 %collective-permute-done.11 = f32[2,5,64,128]{3,2,1,0:T(8,128)S(1)} collective-permute-done((f32[2,5,64,128]{3,2,1,0:T(8,128)S(1)}, f32[2,5,64,128]{3,2,1,0:T(8,128)S(1)}, u32[]{:S(2)}, u32[]{:S(2)}) %collective-permute-start.11) | collective-permute-done | bytes 327712 | tf_op jit(solution)/shard_map/ppermute | solution.py:89
  128.0 3.8 %collective-permute-start.12 = (f32[2,5,64,128]{3,2,1,0:T(8,128)S(1)}, f32[2,5,64,128]{3,2,1,0:T(8,128)S(1)}, u32[]{:S(2)}, u32[]{:S(2)}) collective-permute-start(f32[2,5,64,128]{3,2,1,0:T(8,128)S(1)} %dynamic-slice_add_fusion.1), channel_id=1, source_target_pairs={{0,1},{1,2},{2,3},{3,0},{4,5},{5,6},{6,7},{7,4},{8,9},{9,10},{10,1... | collective-permute-start | bytes 983048 | tf_op jit(solution)/shard_map/ppermute | solution.py:89
  133.1 3.3 %collective-permute-done.12 = f32[2,5,64,128]{3,2,1,0:T(8,128)S(1)} collective-permute-done((f32[2,5,64,128]{3,2,1,0:T(8,128)S(1)}, f32[2,5,64,128]{3,2,1,0:T(8,128)S(1)}, u32[]{:S(2)}, u32[]{:S(2)}) %collective-permute-start.12) | collective-permute-done | bytes 327712 | tf_op jit(solution)/shard_map/ppermute | solution.py:89
  137.4 4.0 %collective-permute-done.15 = f32[2,5,64,128]{3,2,1,0:T(8,128)S(1)} collective-permute-done((f32[2,5,64,128]{3,2,1,0:T(8,128)S(1)}, f32[2,5,64,128]{3,2,1,0:T(8,128)S(1)}, u32[]{:S(2)}, u32[]{:S(2)}) %collective-permute-start.15) | collective-permute-done | bytes 327712 | tf_op jit(solution)/shard_map/ppermute | solution.py:90
  (94 shorter events, 34.3 us)
Async XLA Ops:
  8.9 10.8 %copy-start = (bf16[256,12,8,128]{3,0,2,1:T(8,128)(2,1)}, bf16[256,12,8,128]{3,0,2,1:T(8,128)(2,1)S(1)}, u32[]{:S(2)}) copy-start(bf16[256,12,8,128]{3,0,2,1:T(8,128)(2,1)S(1)} %fusion.1) | copy-start | bytes 18874372
  9.0 19.4 %collective-permute-start.4 = (bf16[256,12,128]{2,0,1:T(8,128)(2,1)S(1)}, bf16[256,12,128]{2,0,1:T(8,128)(2,1)S(1)}, u32[]{:S(2)}, u32[]{:S(2)}) collective-permute-start(bf16[256,12,128]{2,0,1:T(8,128)(2,1)S(1)} %get-tuple-element.5), channel_id=1, source_target_pairs={{0,1},{1,2},{2,3},{3,0},{4,5},{5,6},{6,7},{7,4},{8,9},{9,10},{10,1... | collective-permute-start | bytes 2359304 | tf_op jit(solution)/shard_map/ppermute | solution.py:123
  12.5 36.4 %collective-permute-start = (bf16[256,4,8,128]{3,0,2,1:T(8,128)(2,1)S(1)}, bf16[256,4,8,128]{3,0,2,1:T(8,128)(2,1)S(1)}, u32[]{:S(2)}, u32[]{:S(2)}) collective-permute-start(bf16[256,4,8,128]{3,0,2,1:T(8,128)(2,1)S(1)} %get-tuple-element.4), channel_id=1, source_target_pairs={{252,0},{0,4},{4,8},{8,12},{12,16},{16,20},{20,24},{24,28},{28,32}... | collective-permute-start | bytes 6291464 | tf_op jit(solution)/shard_map/ppermute | solution.py:23
  12.6 20.9 %collective-permute-start.5 = (bf16[256,12,128]{2,0,1:T(8,128)(2,1)S(1)}, bf16[256,12,128]{2,0,1:T(8,128)(2,1)S(1)}, u32[]{:S(2)}, u32[]{:S(2)}) collective-permute-start(bf16[256,12,128]{2,0,1:T(8,128)(2,1)S(1)} %get-tuple-element.6), channel_id=1, source_target_pairs={{1,0},{2,1},{3,2},{0,3},{5,4},{6,5},{7,6},{4,7},{9,8},{10,9},{11,1... | collective-permute-start | bytes 2359304 | tf_op jit(solution)/shard_map/ppermute | solution.py:124
  12.7 52.9 %collective-permute-start.1 = (bf16[256,4,8,128]{3,0,2,1:T(8,128)(2,1)S(1)}, bf16[256,4,8,128]{3,0,2,1:T(8,128)(2,1)S(1)}, u32[]{:S(2)}, u32[]{:S(2)}) collective-permute-start(bf16[256,4,8,128]{3,0,2,1:T(8,128)(2,1)S(1)} %get-tuple-element.3), channel_id=1, source_target_pairs={{4,0},{8,4},{12,8},{16,12},{20,16},{24,20},{28,24},{32,28},{36,32}... | collective-permute-start | bytes 6291464 | tf_op jit(solution)/shard_map/ppermute | solution.py:23
  33.7 14.0 %collective-permute-start.6 = (bf16[2,256,4,128]{3,1,2,0:T(8,128)(2,1)S(1)}, bf16[2,256,4,128]{3,1,2,0:T(8,128)(2,1)S(1)}, u32[]{:S(2)}, u32[]{:S(2)}) collective-permute-start(bf16[2,256,4,128]{3,1,2,0:T(8,128)(2,1)S(1)} %pad_maximum_fusion.8), channel_id=1, source_target_pairs={{252,0},{0,4},{4,8},{8,12},{12,16},{16,20},{20,24},{24,28},{28,32}... | collective-permute-start | bytes 1572872 | tf_op jit(solution)/shard_map/ppermute | solution.py:23
  33.8 15.1 %collective-permute-start.7 = (bf16[2,256,4,128]{3,1,2,0:T(8,128)(2,1)S(1)}, bf16[2,256,4,128]{3,1,2,0:T(8,128)(2,1)S(1)}, u32[]{:S(2)}, u32[]{:S(2)}) collective-permute-start(bf16[2,256,4,128]{3,1,2,0:T(8,128)(2,1)S(1)} %pad_maximum_fusion.9), channel_id=1, source_target_pairs={{4,0},{8,4},{12,8},{16,12},{20,16},{24,20},{28,24},{32,28},{36,32}... | collective-permute-start | bytes 1572872 | tf_op jit(solution)/shard_map/ppermute | solution.py:23
  47.7 3.5 %slice-start = ((s8[6291456]{0:T(1024)(128)(4,1)}), s8[4194304]{0:T(1024)(128)(4,1)S(1)}, s32[]{:S(2)}) async-start(s8[6291456]{0:T(1024)(128)(4,1)} %bitcast.210), calls=%async_computation | async-start | bytes 8388608
  48.9 2.3 %slice-start.1 = ((s8[6291456]{0:T(1024)(128)(4,1)}), s8[2097152]{0:T(1024)(128)(4,1)S(1)}, s32[]{:S(2)}) async-start(s8[6291456]{0:T(1024)(128)(4,1)} %bitcast.210), calls=%async_computation.1 | async-start | bytes 4194304
  50.7 1.9 %slice-start.2 = ((bf16[256,12,8,128]{3,0,2,1:T(8,128)(2,1)}), bf16[256,6,8,128]{3,0,2,1:T(8,128)(2,1)S(1)}, s32[]{:S(2)}) async-start(bf16[256,12,8,128]{3,0,2,1:T(8,128)(2,1)} %copy-done), calls=%async_computation.2 | async-start | bytes 6291456 | tf_op jit(solution)/shard_map/slice | solution.py:138
  50.7 1.9 %copy-start.4 = (f32[4,8,128]{2,1,0:T(8,128)S(1)}, f32[4,8,128]{2,1,0:T(8,128)}, u32[]{:S(2)}) copy-start(f32[4,8,128]{2,1,0:T(8,128)} %param.7) | copy-start | bytes 49156
  59.6 2.9 %copy-start.3 = (bf16[256,3,8,128]{3,0,2,1:T(8,128)(2,1)S(1)}, bf16[256,3,8,128]{3,0,2,1:T(8,128)(2,1)}, u32[]{:S(2)}) copy-start(bf16[256,3,8,128]{3,0,2,1:T(8,128)(2,1)} %slice.187) | copy-start | bytes 4718596
  62.5 1.6 %copy-start.2 = (bf16[256,4,8,128]{3,0,2,1:T(8,128)(2,1)S(1)}, bf16[256,4,8,128]{3,0,2,1:T(8,128)(2,1)}, u32[]{:S(2)}) copy-start(bf16[256,4,8,128]{3,0,2,1:T(8,128)(2,1)} %get-tuple-element.24) | copy-start | bytes 6291460
  77.7 15.0 %collective-permute-start.8 = (f32[3,256,256]{2,1,0:T(8,128)}, f32[3,256,256]{2,1,0:T(8,128)}, u32[]{:S(2)}, u32[]{:S(2)}) collective-permute-start(f32[3,256,256]{2,1,0:T(8,128)} %get-tuple-element.9), channel_id=1, source_target_pairs={{4,0},{8,4},{12,8},{16,12},{20,16},{24,20},{28,24},{32,28},{36,32}... | collective-permute-start | bytes 2359304 | tf_op jit(solution)/shard_map/ppermute | solution.py:23
  83.0 14.8 %collective-permute-start.9 = (f32[3,256,256]{2,1,0:T(8,128)S(1)}, f32[3,256,256]{2,1,0:T(8,128)}, u32[]{:S(2)}, u32[]{:S(2)}) collective-permute-start(f32[3,256,256]{2,1,0:T(8,128)S(1)} %get-tuple-element.8), channel_id=1, source_target_pairs={{252,0},{0,4},{4,8},{8,12},{12,16},{16,20},{20,24},{24,28},{28,32}... | collective-permute-start | bytes 2359304 | tf_op jit(solution)/shard_map/ppermute | solution.py:23
  87.6 14.9 %collective-permute-start.2 = (f32[3,256,256]{2,1,0:T(8,128)}, f32[3,256,256]{2,1,0:T(8,128)}, u32[]{:S(2)}, u32[]{:S(2)}) collective-permute-start(f32[3,256,256]{2,1,0:T(8,128)} %get-tuple-element.12), channel_id=1, source_target_pairs={{4,0},{8,4},{12,8},{16,12},{20,16},{24,20},{28,24},{32,28},{36,32}... | collective-permute-start | bytes 2359304 | tf_op jit(solution)/shard_map/ppermute | solution.py:23
  92.7 15.1 %collective-permute-start.3 = (f32[3,256,256]{2,1,0:T(8,128)}, f32[3,256,256]{2,1,0:T(8,128)}, u32[]{:S(2)}, u32[]{:S(2)}) collective-permute-start(f32[3,256,256]{2,1,0:T(8,128)} %get-tuple-element.11), channel_id=1, source_target_pairs={{252,0},{0,4},{4,8},{8,12},{12,16},{16,20},{20,24},{24,28},{28,32}... | collective-permute-start | bytes 2359304 | tf_op jit(solution)/shard_map/ppermute | solution.py:23
  110.5 7.2 %collective-permute-start.10 = (f32[2,5,64,128]{3,2,1,0:T(8,128)S(1)}, f32[2,5,64,128]{3,2,1,0:T(8,128)S(1)}, u32[]{:S(2)}, u32[]{:S(2)}) collective-permute-start(f32[2,5,64,128]{3,2,1,0:T(8,128)S(1)} %constant_dynamic-slice_fusion), channel_id=1, source_target_pairs={{0,1},{1,2},{2,3},{3,0},{4,5},{5,6},{6,7},{7,4},{8,9},{9,10},{10,1... | collective-permute-start | bytes 983048 | tf_op jit(solution)/shard_map/ppermute | solution.py:89
  112.3 10.2 %collective-permute-start.13 = (f32[2,5,64,128]{3,2,1,0:T(8,128)S(1)}, f32[2,5,64,128]{3,2,1,0:T(8,128)S(1)}, u32[]{:S(2)}, u32[]{:S(2)}) collective-permute-start(f32[2,5,64,128]{3,2,1,0:T(8,128)S(1)} %fusion.96), channel_id=1, source_target_pairs={{1,0},{2,1},{3,2},{0,3},{5,4},{6,5},{7,6},{4,7},{9,8},{10,9},{11,1... | collective-permute-start | bytes 983048 | tf_op jit(solution)/shard_map/ppermute | solution.py:90
  112.7 10.5 %copy-start.5 = (s32[2,5,2]{1,2,0:T(2,128)S(1)}, s32[2,5,2]{1,2,0:T(2,128)}, u32[]{:S(2)}) copy-start(s32[2,5,2]{1,2,0:T(2,128)} %param.11) | copy-start | bytes 244
  118.7 8.4 %collective-permute-start.11 = (f32[2,5,64,128]{3,2,1,0:T(8,128)S(1)}, f32[2,5,64,128]{3,2,1,0:T(8,128)S(1)}, u32[]{:S(2)}, u32[]{:S(2)}) collective-permute-start(f32[2,5,64,128]{3,2,1,0:T(8,128)S(1)} %dynamic-slice_add_fusion.2), channel_id=1, source_target_pairs={{0,1},{1,2},{2,3},{3,0},{4,5},{5,6},{6,7},{7,4},{8,9},{9,10},{10,1... | collective-permute-start | bytes 983048 | tf_op jit(solution)/shard_map/ppermute | solution.py:89
  123.2 8.8 %collective-permute-start.14 = (f32[2,5,64,128]{3,2,1,0:T(8,128)}, f32[2,5,64,128]{3,2,1,0:T(8,128)}, u32[]{:S(2)}, u32[]{:S(2)}) collective-permute-start(f32[2,5,64,128]{3,2,1,0:T(8,128)} %fusion.98), channel_id=1, source_target_pairs={{1,0},{2,1},{3,2},{0,3},{5,4},{6,5},{7,6},{4,7},{9,8},{10,9},{11,1... | collective-permute-start | bytes 983048 | tf_op jit(solution)/shard_map/ppermute | solution.py:90
  128.0 8.4 %collective-permute-start.12 = (f32[2,5,64,128]{3,2,1,0:T(8,128)S(1)}, f32[2,5,64,128]{3,2,1,0:T(8,128)S(1)}, u32[]{:S(2)}, u32[]{:S(2)}) collective-permute-start(f32[2,5,64,128]{3,2,1,0:T(8,128)S(1)} %dynamic-slice_add_fusion.1), channel_id=1, source_target_pairs={{0,1},{1,2},{2,3},{3,0},{4,5},{5,6},{6,7},{7,4},{8,9},{9,10},{10,1... | collective-permute-start | bytes 983048 | tf_op jit(solution)/shard_map/ppermute | solution.py:89
  133.0 8.4 %collective-permute-start.15 = (f32[2,5,64,128]{3,2,1,0:T(8,128)S(1)}, f32[2,5,64,128]{3,2,1,0:T(8,128)S(1)}, u32[]{:S(2)}, u32[]{:S(2)}) collective-permute-start(f32[2,5,64,128]{3,2,1,0:T(8,128)S(1)} %fusion.100), channel_id=1, source_target_pairs={{1,0},{2,1},{3,2},{0,3},{5,4},{6,5},{7,6},{4,7},{9,8},{10,9},{11,1... | collective-permute-start | bytes 983048 | tf_op jit(solution)/shard_map/ppermute | solution.py:90
  (1 other events, 1.1 us)
where the time goes:
time: 143 us
  waiting for transfers between devices  52.4 us (37%)
  starting transfers between devices  34.7 us (24%)
  other arithmetic  29.3 us (20%)
  matrix products  16.3 us (11%)
  local copies, waits for them, and re-layouts  8.63 us (6%)
    ppermute x8, waiting for transfers between devices, passed_along(): return lax.ppermute(block, axis, route)  23.3 us
    ppermute x8, starting transfers between devices, passed_along(): return lax.ppermute(block, axis, route)  22.6 us
    dot_general x18, matrix products, pair_product(): lax.dot_general(left, right, (((1, 2, 3), (1, 2, 3)), ((), ())), preferre...  15 us
    ppermute x3, waiting for transfers between devices, ring_scatter(): ahead = lax.ppermute(ahead, 'mat', forward)  11.8 us
    convert_element_type x2, other arithmetic, on_device(): stencil(ext, potential).astype(jnp.bfloat16)  10.3 us
    ppermute x3, starting transfers between devices, ring_scatter(): ahead = lax.ppermute(ahead, 'mat', forward)  9.31 us
    ppermute x1, waiting for transfers between devices, on_device(): row_above = lax.ppermute(masked[:, :, second_cells - 1], 'mat', up)  7.94 us
    select_n x1, other arithmetic, on_device(): masked = jnp.where(inside, orbitals, jnp.zeros_like(orbitals))  5.94 us
  transfers between devices with their start and end apart: 16, of which 13 were waited for; matrix products, arithmetic and copies ran while one was open for 19% of the time, Pallas kernels for 0%

commit v1 on v0

--- a/solution.py
+++ b/solution.py
@@ -172,8 +172,8 @@
             assembled = assembled + jnp.pad(arrived, ((2 - slot_index, slot_index), (0, 0), (0, 0)))
         return assembled
 
-    both = jnp.stack([row_blocks(gram_full), row_blocks(energy_full)])
-    gram_rows, energy_rows = ring_scatter(both, 2)
+    gram_rows = ring_scatter(row_blocks(gram_full), 1)
+    energy_rows = ring_scatter(row_blocks(energy_full), 1)
     columns = lax.axis_index("mat") * col_count + lax.iota(jnp.int32, col_count)
     block_ids = lax.iota(jnp.int32, local_blocks)
     column_pick = ((columns // per_block)[:, None] == block_ids[None, :]).astype(jnp.float32)

time: 143 us -> 149 us (1.042)
  waiting for transfers between devices: 52.4 us -> 30.8 us
  starting transfers between devices: 34.7 us -> 49 us
  local copies, waits for them, and re-layouts: 8.63 us -> 15.6 us
  matrix products: 16.3 us -> 21.3 us
    ppermute x3 -> x6, waiting for transfers between devices: 11.8 us -> 0.02 us  [ring_scatter(): ahead = lax.ppermute(ahead, 'mat', forward)]
    ppermute x3 -> x6, starting transfers between devices: 9.31 us -> 20 us  [ring_scatter(): ahead = lax.ppermute(ahead, 'mat', forward)]
    dot_general x18, matrix products: 15 us -> 20 us  [pair_product(): lax.dot_general(left, right, (((1, 2, 3), (1, 2, 3)), ((), ())), preferre...]
    ppermute x8, waiting for transfers between devices: 23.3 us -> 19 us  [passed_along(): return lax.ppermute(block, axis, route)]
    ppermute x1, waiting for transfers between devices: 7.94 us -> 3.97 us  [on_device(): row_above = lax.ppermute(masked[:, :, second_cells - 1], 'mat', up)]
    convert_element_type x3, other arithmetic: 2.05 us -> 5.99 us  [stencil(): centre_cells = extended[:, 1:-1, 1:-1, :].astype(jnp.float32)]
    another operation x4 -> x0, other arithmetic: 3.17 us -> none  [on_device(): both = jnp.stack([row_blocks(gram_full), row_blocks(energy_full)])]
    add x0 -> x2, other arithmetic: none -> 3.05 us  [row_blocks(): assembled + jnp.pad(arrived, ((2 - slot_index, slot_index), (0, 0), (0, 0)))]
  transfers between devices with their start and end apart: 16 -> 22, of which waited for: 13 -> 8; matrix products, arithmetic and copies ran while one was open for 19% -> 22% of each run, Pallas kernels for 0% -> 0%
where the time goes in v1:
time: 149 us; the launch traced here: 147 us
  starting transfers between devices  49 us (33%)
  waiting for transfers between devices  30.8 us (21%)
  other arithmetic  29.3 us (20%)
  matrix products  21.3 us (14%)
  local copies, waits for them, and re-layouts  15.6 us (10%)
    ppermute x8, starting transfers between devices, passed_along(): return lax.ppermute(block, axis, route)  25.2 us
    dot_general x18, matrix products, pair_product(): lax.dot_general(left, right, (((1, 2, 3), (1, 2, 3)), ((), ())), preferre...  20 us
    ppermute x6, starting transfers between devices, ring_scatter(): ahead = lax.ppermute(ahead, 'mat', forward)  20 us
    ppermute x8, waiting for transfers between devices, passed_along(): return lax.ppermute(block, axis, route)  19 us
    convert_element_type x2, other arithmetic, on_device(): stencil(ext, potential).astype(jnp.bfloat16)  11 us
    convert_element_type x3, other arithmetic, stencil(): centre_cells = extended[:, 1:-1, 1:-1, :].astype(jnp.float32)  5.99 us
    select_n x1, other arithmetic, on_device(): masked = jnp.where(inside, orbitals, jnp.zeros_like(orbitals))  5.94 us
    ppermute x6, waiting for transfers between devices, ring_scatter(): behind = lax.ppermute(behind, 'mat', backward)  4.4 us
  transfers between devices with their start and end apart: 22, of which 8 were waited for; matrix products, arithmetic and copies ran while one was open for 22% of the time, Pallas kernels for 0%

profile of v1, /device:TPU:6, one launch (start us, length us, event | category | flops | bytes accessed | tf_op | source)
XLA Modules:
  0.0 147.3 jit_solution(15019229703771715190)
XLA Ops:
  2.9 5.9 %fusion.1 = bf16[256,12,8,128]{3,0,2,1:T(8,128)(2,1)S(1)} fusion(bf16[256,12,8,128]{3,2,1,0:T(8,128)(2,1)} %param.6, s32[256,128]{1,0:T(8,128)S(1)} %subtract_multiply_fusion, s32[256,12,8]{0,2,1:T(8,128)S(1)} %broadcast_add_fusion, pred[12]{0:T(512)(128)(4,1)S(1)} %compare_and_fusion), kind=kLoop, calls=%fused_computation.2 | loop fusion | flops 12582912 | bytes 12812300 | tf_op jit(solution)/shard_map/jit(_where)/select_n | solution.py:114
  11.2 3.6 %slice_convert_fusion.2 = (f32[256,4,8,128]{3,0,2,1:T(8,128)}, bf16[256,4,8,128]{3,0,2,1:T(8,128)(2,1)}, bf16[256,4,8,128]{3,0,2,1:T(8,128)(2,1)}) fusion(bf16[256,12,8,128]{3,0,2,1:T(8,128)(2,1)S(1)} %fusion.1), kind=kLoop, calls=%fused_computation.100 | loop fusion | flops 1048576 | bytes 14680064 | tf_op jit(solution)/shard_map/convert_element_type | solution.py:54
  14.8 7.5 %collective-permute-start.1 = (bf16[256,4,8,128]{3,0,2,1:T(8,128)(2,1)}, bf16[256,4,8,128]{3,0,2,1:T(8,128)(2,1)}, u32[]{:S(2)}, u32[]{:S(2)}) collective-permute-start(bf16[256,4,8,128]{3,0,2,1:T(8,128)(2,1)} %get-tuple-element.3), channel_id=1, source_target_pairs={{4,0},{8,4},{12,8},{16,12},{20,16},{24,20},{28,24},{32,28},{36,32}... | collective-permute-start | bytes 6291464 | tf_op jit(solution)/shard_map/ppermute | solution.py:23
  22.3 2.4 %collective-permute-start.10 = (bf16[256,12,128]{2,0,1:T(8,128)(2,1)}, bf16[256,12,128]{2,0,1:T(8,128)(2,1)}, u32[]{:S(2)}, u32[]{:S(2)}) collective-permute-start(bf16[256,12,128]{2,0,1:T(8,128)(2,1)} %get-tuple-element.5), channel_id=1, source_target_pairs={{0,1},{1,2},{2,3},{3,0},{4,5},{5,6},{6,7},{7,4},{8,9},{9,10},{10,1... | collective-permute-start | bytes 2359304 | tf_op jit(solution)/shard_map/ppermute | solution.py:123
  24.7 3.0 %convolution_bitcast_fusion.1 = f32[256,1,256]{2,0,1:T(8,128)S(1)} fusion(bf16[256,12,8,128]{3,0,2,1:T(8,128)(2,1)} %copy-done), kind=kOutput, calls=%fused_computation.64 | convolution fusion | flops 536870912 | bytes 8650752 | tf_op jit(solution)/shard_map/dot_general | solution.py:69
  27.7 3.4 %collective-permute-done.11 = bf16[256,12,128]{2,0,1:T(8,128)(2,1)S(1)} collective-permute-done((bf16[256,12,128]{2,0,1:T(8,128)(2,1)}, bf16[256,12,128]{2,0,1:T(8,128)(2,1)S(1)}, u32[]{:S(2)}, u32[]{:S(2)}) %collective-permute-start.11) | collective-permute-done | bytes 786464 | tf_op jit(solution)/shard_map/ppermute | solution.py:124
  31.1 4.0 %collective-permute-done.10 = bf16[256,12,128]{2,0,1:T(8,128)(2,1)} collective-permute-done((bf16[256,12,128]{2,0,1:T(8,128)(2,1)}, bf16[256,12,128]{2,0,1:T(8,128)(2,1)}, u32[]{:S(2)}, u32[]{:S(2)}) %collective-permute-start.10) | collective-permute-done | bytes 786464 | tf_op jit(solution)/shard_map/ppermute | solution.py:123
  36.2 7.5 %collective-permute-start.13 = (bf16[2,256,4,128]{3,1,2,0:T(8,128)(2,1)S(1)}, bf16[2,256,4,128]{3,1,2,0:T(8,128)(2,1)S(1)}, u32[]{:S(2)}, u32[]{:S(2)}) collective-permute-start(bf16[2,256,4,128]{3,1,2,0:T(8,128)(2,1)S(1)} %pad_maximum_fusion.9), channel_id=1, source_target_pairs={{4,0},{8,4},{12,8},{16,12},{20,16},{24,20},{28,24},{32,28},{36,32}... | collective-permute-start | bytes 1572872 | tf_op jit(solution)/shard_map/ppermute | solution.py:23
  44.9 6.7 %collective-permute-done.13 = bf16[2,256,4,128]{3,1,2,0:T(8,128)(2,1)S(1)} collective-permute-done((bf16[2,256,4,128]{3,1,2,0:T(8,128)(2,1)S(1)}, bf16[2,256,4,128]{3,1,2,0:T(8,128)(2,1)S(1)}, u32[]{:S(2)}, u32[]{:S(2)}) %collective-permute-start.13) | collective-permute-done | bytes 524320 | tf_op jit(solution)/shard_map/ppermute | solution.py:23
  51.7 7.6 %collective-permute-done.12 = bf16[2,256,4,128]{3,1,2,0:T(8,128)(2,1)S(1)} collective-permute-done((bf16[2,256,4,128]{3,1,2,0:T(8,128)(2,1)S(1)}, bf16[2,256,4,128]{3,1,2,0:T(8,128)(2,1)S(1)}, u32[]{:S(2)}, u32[]{:S(2)}) %collective-permute-start.12) | collective-permute-done | bytes 524320 | tf_op jit(solution)/shard_map/ppermute | solution.py:23
  60.9 2.7 %concatenate.54 = bf16[256,6,8,128]{3,0,2,1:T(8,128)(2,1)S(1)} pad(bf16[256,4,8,128]{3,0,2,1:T(8,128)(2,1)} %collective-permute-done.1, bf16[]{:T(256)} %constant.91.clone.1), padding=0_0x2_0x0_0x0_0 | pad | bytes 5242882 | tf_op jit(solution)/shard_map/concatenate | solution.py:146
  65.6 4.8 %fusion.19 = bf16[256,4,8,128]{3,0,2,1:T(8,128)(2,1)S(1)} fusion(f32[256,4,8,128]{3,0,2,1:T(8,128)S(1)} %slice_convert_fusion, bf16[256,4,8,128]{3,0,2,1:T(8,128)(2,1)} %collective-permute-done.1, bf16[256,6,8,128]{3,0,2,1:T(8,128)(2,1)S(1)} %concatenate.54, bf16[256,6,1,128]{3,0,2,1:T(8,128)(2,1)S(1)} %get-tuple-element.24, ...), kind=kLoop, calls=%fused_computation.26 | loop fusion | flops 17825792 | bytes 14434304 | tf_op jit(solution)/shard_map/convert_element_type | solution.py:155
  77.1 6.2 %fusion.7 = (bf16[256,4,8,128]{3,0,2,1:T(8,128)(2,1)S(1)}, bf16[256,4,8,128]{3,0,2,1:T(8,128)(2,1)S(1)}) fusion(f32[256,4,8,128]{3,0,2,1:T(8,128)S(1)} %slice_convert_fusion.1, bf16[256,4,8,128]{3,0,2,1:T(8,128)(2,1)S(1)} %collective-permute-done, bf16[256,6,8,128]{3,0,2,1:T(8,128)(2,1)S(1)} %concatenate.48, ...), kind=kLoop, calls=%fused_computation.14 | loop fusion | flops 35651584 | bytes 28852224 | tf_op jit(solution)/shard_map/convert_element_type | solution.py:155
  95.2 5.1 %collective-permute-start.14 = (f32[3,256,256]{2,1,0:T(8,128)}, f32[3,256,256]{2,1,0:T(8,128)}, u32[]{:S(2)}, u32[]{:S(2)}) collective-permute-start(f32[3,256,256]{2,1,0:T(8,128)} %get-tuple-element.9), channel_id=1, source_target_pairs={{4,0},{8,4},{12,8},{16,12},{20,16},{24,20},{28,24},{32,28},{36,32}... | collective-permute-start | bytes 2359304 | tf_op jit(solution)/shard_map/ppermute | solution.py:23
  102.5 2.2 %fusion.56 = f32[256,1,256]{2,0,1:T(8,128)S(1)} fusion(bf16[256,3,8,128]{3,0,2,1:T(8,128)(2,1)S(1)} %slice.195, bf16[256,4,8,128]{3,0,2,1:T(8,128)(2,1)} %collective-permute-done.1), kind=kOutput, calls=%fused_computation.69 | convolution fusion | flops 402653184 | bytes 3407872 | tf_op jit(solution)/shard_map/dot_general | solution.py:69
  107.5 5.1 %collective-permute-start.2 = (f32[3,256,256]{2,1,0:T(8,128)S(1)}, f32[3,256,256]{2,1,0:T(8,128)}, u32[]{:S(2)}, u32[]{:S(2)}) collective-permute-start(f32[3,256,256]{2,1,0:T(8,128)S(1)} %get-tuple-element.12), channel_id=1, source_target_pairs={{4,0},{8,4},{12,8},{16,12},{20,16},{24,20},{28,24},{32,28},{36,32}... | collective-permute-start | bytes 2359304 | tf_op jit(solution)/shard_map/ppermute | solution.py:23
  114.6 3.3 %collective-permute-start.16 = (f32[5,64,128]{2,1,0:T(8,128)S(1)}, f32[5,64,128]{2,1,0:T(8,128)S(1)}, u32[]{:S(2)}, u32[]{:S(2)}) collective-permute-start(f32[5,64,128]{2,1,0:T(8,128)S(1)} %constant_dynamic-slice_fusion.1), channel_id=1, source_target_pairs={{0,1},{1,2},{2,3},{3,0},{4,5},{5,6},{6,7},{7,4},{8,9},{9,10},{10,1... | collective-permute-start | bytes 491528 | tf_op jit(solution)/shard_map/ppermute | solution.py:89
  117.9 4.7 %collective-permute-done.3 = f32[3,256,256]{2,1,0:T(8,128)} collective-permute-done((f32[3,256,256]{2,1,0:T(8,128)}, f32[3,256,256]{2,1,0:T(8,128)}, u32[]{:S(2)}, u32[]{:S(2)}) %collective-permute-start.3) | collective-permute-done | bytes 786464 | tf_op jit(solution)/shard_map/ppermute | solution.py:23
  124.3 3.3 %collective-permute-start.4 = (f32[5,64,128]{2,1,0:T(8,128)S(1)}, f32[5,64,128]{2,1,0:T(8,128)S(1)}, u32[]{:S(2)}, u32[]{:S(2)}) collective-permute-start(f32[5,64,128]{2,1,0:T(8,128)S(1)} %constant_dynamic-slice_fusion.3), channel_id=1, source_target_pairs={{0,1},{1,2},{2,3},{3,0},{4,5},{5,6},{6,7},{7,4},{8,9},{9,10},{10,1... | collective-permute-start | bytes 491528 | tf_op jit(solution)/shard_map/ppermute | solution.py:89
  127.8 3.3 %collective-permute-start.17 = (f32[5,64,128]{2,1,0:T(8,128)S(1)}, f32[5,64,128]{2,1,0:T(8,128)S(1)}, u32[]{:S(2)}, u32[]{:S(2)}) collective-permute-start(f32[5,64,128]{2,1,0:T(8,128)S(1)} %dynamic-slice_add_fusion.5), channel_id=1, source_target_pairs={{0,1},{1,2},{2,3},{3,0},{4,5},{5,6},{6,7},{7,4},{8,9},{9,10},{10,1... | collective-permute-start | bytes 491528 | tf_op jit(solution)/shard_map/ppermute | solution.py:89
  132.2 3.6 %collective-permute-start.5 = (f32[5,64,128]{2,1,0:T(8,128)S(1)}, f32[5,64,128]{2,1,0:T(8,128)S(1)}, u32[]{:S(2)}, u32[]{:S(2)}) collective-permute-start(f32[5,64,128]{2,1,0:T(8,128)S(1)} %dynamic-slice_add_fusion.11), channel_id=1, source_target_pairs={{0,1},{1,2},{2,3},{3,0},{4,5},{5,6},{6,7},{7,4},{8,9},{9,10},{10,1... | collective-permute-start | bytes 491528 | tf_op jit(solution)/shard_map/ppermute | solution.py:89
  136.2 3.3 %collective-permute-start.18 = (f32[5,64,128]{2,1,0:T(8,128)S(1)}, f32[5,64,128]{2,1,0:T(8,128)S(1)}, u32[]{:S(2)}, u32[]{:S(2)}) collective-permute-start(f32[5,64,128]{2,1,0:T(8,128)S(1)} %dynamic-slice_add_fusion.4), channel_id=1, source_target_pairs={{0,1},{1,2},{2,3},{3,0},{4,5},{5,6},{6,7},{7,4},{8,9},{9,10},{10,1... | collective-permute-start | bytes 491528 | tf_op jit(solution)/shard_map/ppermute | solution.py:89
  139.7 3.3 %collective-permute-start.6 = (f32[5,64,128]{2,1,0:T(8,128)S(1)}, f32[5,64,128]{2,1,0:T(8,128)S(1)}, u32[]{:S(2)}, u32[]{:S(2)}) collective-permute-start(f32[5,64,128]{2,1,0:T(8,128)S(1)} %dynamic-slice_add_fusion.10), channel_id=1, source_target_pairs={{0,1},{1,2},{2,3},{3,0},{4,5},{5,6},{6,7},{7,4},{8,9},{9,10},{10,1... | collective-permute-start | bytes 491528 | tf_op jit(solution)/shard_map/ppermute | solution.py:89
  143.0 3.1 %collective-permute-done.9 = f32[5,64,128]{2,1,0:T(8,128)S(1)} collective-permute-done((f32[5,64,128]{2,1,0:T(8,128)S(1)}, f32[5,64,128]{2,1,0:T(8,128)S(1)}, u32[]{:S(2)}, u32[]{:S(2)}) %collective-permute-start.9) | collective-permute-done | bytes 163872 | tf_op jit(solution)/shard_map/ppermute | solution.py:90
  (122 shorter events, 40.6 us)
Async XLA Ops:
  8.9 15.8 %copy-start = (bf16[256,12,8,128]{3,0,2,1:T(8,128)(2,1)}, bf16[256,12,8,128]{3,0,2,1:T(8,128)(2,1)S(1)}, u32[]{:S(2)}) copy-start(bf16[256,12,8,128]{3,0,2,1:T(8,128)(2,1)S(1)} %fusion.1) | copy-start | bytes 18874372
  10.4 20.7 %collective-permute-start.11 = (bf16[256,12,128]{2,0,1:T(8,128)(2,1)}, bf16[256,12,128]{2,0,1:T(8,128)(2,1)S(1)}, u32[]{:S(2)}, u32[]{:S(2)}) collective-permute-start(bf16[256,12,128]{2,0,1:T(8,128)(2,1)} %get-tuple-element.6), channel_id=1, source_target_pairs={{1,0},{2,1},{3,2},{0,3},{5,4},{6,5},{7,6},{4,7},{9,8},{10,9},{11,1... | collective-permute-start | bytes 2359304 | tf_op jit(solution)/shard_map/ppermute | solution.py:124
  14.8 44.6 %collective-permute-start.1 = (bf16[256,4,8,128]{3,0,2,1:T(8,128)(2,1)}, bf16[256,4,8,128]{3,0,2,1:T(8,128)(2,1)}, u32[]{:S(2)}, u32[]{:S(2)}) collective-permute-start(bf16[256,4,8,128]{3,0,2,1:T(8,128)(2,1)} %get-tuple-element.3), channel_id=1, source_target_pairs={{4,0},{8,4},{12,8},{16,12},{20,16},{24,20},{28,24},{32,28},{36,32}... | collective-permute-start | bytes 6291464 | tf_op jit(solution)/shard_map/ppermute | solution.py:23
  22.3 12.8 %collective-permute-start.10 = (bf16[256,12,128]{2,0,1:T(8,128)(2,1)}, bf16[256,12,128]{2,0,1:T(8,128)(2,1)}, u32[]{:S(2)}, u32[]{:S(2)}) collective-permute-start(bf16[256,12,128]{2,0,1:T(8,128)(2,1)} %get-tuple-element.5), channel_id=1, source_target_pairs={{0,1},{1,2},{2,3},{3,0},{4,5},{5,6},{6,7},{7,4},{8,9},{9,10},{10,1... | collective-permute-start | bytes 2359304 | tf_op jit(solution)/shard_map/ppermute | solution.py:123
  24.7 48.0 %collective-permute-start = (bf16[256,4,8,128]{3,0,2,1:T(8,128)(2,1)}, bf16[256,4,8,128]{3,0,2,1:T(8,128)(2,1)S(1)}, u32[]{:S(2)}, u32[]{:S(2)}) collective-permute-start(bf16[256,4,8,128]{3,0,2,1:T(8,128)(2,1)} %get-tuple-element.4), channel_id=1, source_target_pairs={{252,0},{0,4},{4,8},{8,12},{12,16},{16,20},{20,24},{24,28},{28,32}... | collective-permute-start | bytes 6291464 | tf_op jit(solution)/shard_map/ppermute | solution.py:23
  36.2 15.4 %collective-permute-start.13 = (bf16[2,256,4,128]{3,1,2,0:T(8,128)(2,1)S(1)}, bf16[2,256,4,128]{3,1,2,0:T(8,128)(2,1)S(1)}, u32[]{:S(2)}, u32[]{:S(2)}) collective-permute-start(bf16[2,256,4,128]{3,1,2,0:T(8,128)(2,1)S(1)} %pad_maximum_fusion.9), channel_id=1, source_target_pairs={{4,0},{8,4},{12,8},{16,12},{20,16},{24,20},{28,24},{32,28},{36,32}... | collective-permute-start | bytes 1572872 | tf_op jit(solution)/shard_map/ppermute | solution.py:23
  43.8 15.5 %collective-permute-start.12 = (bf16[2,256,4,128]{3,1,2,0:T(8,128)(2,1)S(1)}, bf16[2,256,4,128]{3,1,2,0:T(8,128)(2,1)S(1)}, u32[]{:S(2)}, u32[]{:S(2)}) collective-permute-start(bf16[2,256,4,128]{3,1,2,0:T(8,128)(2,1)S(1)} %pad_maximum_fusion.8), channel_id=1, source_target_pairs={{252,0},{0,4},{4,8},{8,12},{12,16},{16,20},{20,24},{24,28},{28,32}... | collective-permute-start | bytes 1572872 | tf_op jit(solution)/shard_map/ppermute | solution.py:23
  60.9 9.6 %copy-start.2 = (bf16[256,3,8,128]{3,0,2,1:T(8,128)(2,1)}, bf16[256,3,8,128]{3,0,2,1:T(8,128)(2,1)S(1)}, u32[]{:S(2)}) copy-start(bf16[256,3,8,128]{3,0,2,1:T(8,128)(2,1)S(1)} %slice.198) | copy-start | bytes 4718596
  95.2 17.6 %collective-permute-start.15 = (f32[3,256,256]{2,1,0:T(8,128)}, f32[3,256,256]{2,1,0:T(8,128)}, u32[]{:S(2)}, u32[]{:S(2)}) collective-permute-start(f32[3,256,256]{2,1,0:T(8,128)} %get-tuple-element.8), channel_id=1, source_target_pairs={{252,0},{0,4},{4,8},{8,12},{12,16},{16,20},{20,24},{24,28},{28,32}... | collective-permute-start | bytes 2359304 | tf_op jit(solution)/shard_map/ppermute | solution.py:23
  95.2 17.6 %collective-permute-start.14 = (f32[3,256,256]{2,1,0:T(8,128)}, f32[3,256,256]{2,1,0:T(8,128)}, u32[]{:S(2)}, u32[]{:S(2)}) collective-permute-start(f32[3,256,256]{2,1,0:T(8,128)} %get-tuple-element.9), channel_id=1, source_target_pairs={{4,0},{8,4},{12,8},{16,12},{20,16},{24,20},{28,24},{32,28},{36,32}... | collective-permute-start | bytes 2359304 | tf_op jit(solution)/shard_map/ppermute | solution.py:23
  107.5 15.1 %collective-permute-start.3 = (f32[3,256,256]{2,1,0:T(8,128)}, f32[3,256,256]{2,1,0:T(8,128)}, u32[]{:S(2)}, u32[]{:S(2)}) collective-permute-start(f32[3,256,256]{2,1,0:T(8,128)} %get-tuple-element.11), channel_id=1, source_target_pairs={{252,0},{0,4},{4,8},{8,12},{12,16},{16,20},{20,24},{24,28},{28,32}... | collective-permute-start | bytes 2359304 | tf_op jit(solution)/shard_map/ppermute | solution.py:23
  107.5 15.1 %collective-permute-start.2 = (f32[3,256,256]{2,1,0:T(8,128)S(1)}, f32[3,256,256]{2,1,0:T(8,128)}, u32[]{:S(2)}, u32[]{:S(2)}) collective-permute-start(f32[3,256,256]{2,1,0:T(8,128)S(1)} %get-tuple-element.12), channel_id=1, source_target_pairs={{4,0},{8,4},{12,8},{16,12},{20,16},{24,20},{28,24},{32,28},{36,32}... | collective-permute-start | bytes 2359304 | tf_op jit(solution)/shard_map/ppermute | solution.py:23
  114.5 13.2 %collective-permute-start.19 = (f32[5,64,128]{2,1,0:T(8,128)S(1)}, f32[5,64,128]{2,1,0:T(8,128)S(1)}, u32[]{:S(2)}, u32[]{:S(2)}) collective-permute-start(f32[5,64,128]{2,1,0:T(8,128)S(1)} %constant_dynamic-slice_fusion), channel_id=1, source_target_pairs={{1,0},{2,1},{3,2},{0,3},{5,4},{6,5},{7,6},{4,7},{9,8},{10,9},{11,1... | collective-permute-start | bytes 491528 | tf_op jit(solution)/shard_map/ppermute | solution.py:90
  114.6 13.2 %collective-permute-start.16 = (f32[5,64,128]{2,1,0:T(8,128)S(1)}, f32[5,64,128]{2,1,0:T(8,128)S(1)}, u32[]{:S(2)}, u32[]{:S(2)}) collective-permute-start(f32[5,64,128]{2,1,0:T(8,128)S(1)} %constant_dynamic-slice_fusion.1), channel_id=1, source_target_pairs={{0,1},{1,2},{2,3},{3,0},{4,5},{5,6},{6,7},{7,4},{8,9},{9,10},{10,1... | collective-permute-start | bytes 491528 | tf_op jit(solution)/shard_map/ppermute | solution.py:89
  124.2 7.8 %collective-permute-start.7 = (f32[5,64,128]{2,1,0:T(8,128)S(1)}, f32[5,64,128]{2,1,0:T(8,128)S(1)}, u32[]{:S(2)}, u32[]{:S(2)}) collective-permute-start(f32[5,64,128]{2,1,0:T(8,128)S(1)} %constant_dynamic-slice_fusion.2), channel_id=1, source_target_pairs={{1,0},{2,1},{3,2},{0,3},{5,4},{6,5},{7,6},{4,7},{9,8},{10,9},{11,1... | collective-permute-start | bytes 491528 | tf_op jit(solution)/shard_map/ppermute | solution.py:90
  124.3 7.8 %collective-permute-start.4 = (f32[5,64,128]{2,1,0:T(8,128)S(1)}, f32[5,64,128]{2,1,0:T(8,128)S(1)}, u32[]{:S(2)}, u32[]{:S(2)}) collective-permute-start(f32[5,64,128]{2,1,0:T(8,128)S(1)} %constant_dynamic-slice_fusion.3), channel_id=1, source_target_pairs={{0,1},{1,2},{2,3},{3,0},{4,5},{5,6},{6,7},{7,4},{8,9},{9,10},{10,1... | collective-permute-start | bytes 491528 | tf_op jit(solution)/shard_map/ppermute | solution.py:89
  127.7 8.4 %collective-permute-start.20 = (f32[5,64,128]{2,1,0:T(8,128)S(1)}, f32[5,64,128]{2,1,0:T(8,128)S(1)}, u32[]{:S(2)}, u32[]{:S(2)}) collective-permute-start(f32[5,64,128]{2,1,0:T(8,128)S(1)} %dynamic-slice_add_fusion.2), channel_id=1, source_target_pairs={{1,0},{2,1},{3,2},{0,3},{5,4},{6,5},{7,6},{4,7},{9,8},{10,9},{11,1... | collective-permute-start | bytes 491528 | tf_op jit(solution)/shard_map/ppermute | solution.py:90
  127.8 8.4 %collective-permute-start.17 = (f32[5,64,128]{2,1,0:T(8,128)S(1)}, f32[5,64,128]{2,1,0:T(8,128)S(1)}, u32[]{:S(2)}, u32[]{:S(2)}) collective-permute-start(f32[5,64,128]{2,1,0:T(8,128)S(1)} %dynamic-slice_add_fusion.5), channel_id=1, source_target_pairs={{0,1},{1,2},{2,3},{3,0},{4,5},{5,6},{6,7},{7,4},{8,9},{9,10},{10,1... | collective-permute-start | bytes 491528 | tf_op jit(solution)/shard_map/ppermute | solution.py:89
  132.0 7.5 %collective-permute-start.8 = (f32[5,64,128]{2,1,0:T(8,128)S(1)}, f32[5,64,128]{2,1,0:T(8,128)S(1)}, u32[]{:S(2)}, u32[]{:S(2)}) collective-permute-start(f32[5,64,128]{2,1,0:T(8,128)S(1)} %dynamic-slice_add_fusion.8), channel_id=1, source_target_pairs={{1,0},{2,1},{3,2},{0,3},{5,4},{6,5},{7,6},{4,7},{9,8},{10,9},{11,1... | collective-permute-start | bytes 491528 | tf_op jit(solution)/shard_map/ppermute | solution.py:90
  132.2 7.5 %collective-permute-start.5 = (f32[5,64,128]{2,1,0:T(8,128)S(1)}, f32[5,64,128]{2,1,0:T(8,128)S(1)}, u32[]{:S(2)}, u32[]{:S(2)}) collective-permute-start(f32[5,64,128]{2,1,0:T(8,128)S(1)} %dynamic-slice_add_fusion.11), channel_id=1, source_target_pairs={{0,1},{1,2},{2,3},{3,0},{4,5},{5,6},{6,7},{7,4},{8,9},{9,10},{10,1... | collective-permute-start | bytes 491528 | tf_op jit(solution)/shard_map/ppermute | solution.py:89
  136.1 6.9 %collective-permute-start.21 = (f32[5,64,128]{2,1,0:T(8,128)S(1)}, f32[5,64,128]{2,1,0:T(8,128)S(1)}, u32[]{:S(2)}, u32[]{:S(2)}) collective-permute-start(f32[5,64,128]{2,1,0:T(8,128)S(1)} %dynamic-slice_add_fusion.1), channel_id=1, source_target_pairs={{1,0},{2,1},{3,2},{0,3},{5,4},{6,5},{7,6},{4,7},{9,8},{10,9},{11,1... | collective-permute-start | bytes 491528 | tf_op jit(solution)/shard_map/ppermute | solution.py:90
  136.2 6.8 %collective-permute-start.18 = (f32[5,64,128]{2,1,0:T(8,128)S(1)}, f32[5,64,128]{2,1,0:T(8,128)S(1)}, u32[]{:S(2)}, u32[]{:S(2)}) collective-permute-start(f32[5,64,128]{2,1,0:T(8,128)S(1)} %dynamic-slice_add_fusion.4), channel_id=1, source_target_pairs={{0,1},{1,2},{2,3},{3,0},{4,5},{5,6},{6,7},{7,4},{8,9},{9,10},{10,1... | collective-permute-start | bytes 491528 | tf_op jit(solution)/shard_map/ppermute | solution.py:89
  139.6 6.6 %collective-permute-start.9 = (f32[5,64,128]{2,1,0:T(8,128)S(1)}, f32[5,64,128]{2,1,0:T(8,128)S(1)}, u32[]{:S(2)}, u32[]{:S(2)}) collective-permute-start(f32[5,64,128]{2,1,0:T(8,128)S(1)} %dynamic-slice_add_fusion.7), channel_id=1, source_target_pairs={{1,0},{2,1},{3,2},{0,3},{5,4},{6,5},{7,6},{4,7},{9,8},{10,9},{11,1... | collective-permute-start | bytes 491528 | tf_op jit(solution)/shard_map/ppermute | solution.py:90
  139.7 6.5 %collective-permute-start.6 = (f32[5,64,128]{2,1,0:T(8,128)S(1)}, f32[5,64,128]{2,1,0:T(8,128)S(1)}, u32[]{:S(2)}, u32[]{:S(2)}) collective-permute-start(f32[5,64,128]{2,1,0:T(8,128)S(1)} %dynamic-slice_add_fusion.10), channel_id=1, source_target_pairs={{0,1},{1,2},{2,3},{3,0},{4,5},{5,6},{6,7},{7,4},{8,9},{9,10},{10,1... | collective-permute-start | bytes 491528 | tf_op jit(solution)/shard_map/ppermute | solution.py:89
  (10 other events, 35.5 us)

commit v2 on v0

--- a/solution.py
+++ b/solution.py
@@ -2,6 +2,9 @@
 import jax.numpy as jnp
 from jax import lax
 from jax.sharding import PartitionSpec as P
+from jax.experimental import pallas as pl
+from jax.experimental.pallas import tpu as pltpu
+import functools
 
 
 def extended_2(array, sides, width):
@@ -93,6 +96,71 @@
     return jnp.concatenate([ahead, behind], axis=-1)
 
 
+def ring_kernel(count, share, half, x_ref, o_ref, stage_f, stage_b, land_f, land_b, send_f, recv_f, send_b, recv_b):
+    me = lax.axis_index("mat")
+    dom = lax.axis_index("dom")
+    right = lax.rem(me + 1, count)
+    left = lax.rem(me + count - 1, count)
+    mesh_ids = pl.DeviceIdType.MESH
+    barrier = pltpu.get_barrier_semaphore()
+    for neighbour in (left, right):
+        pl.semaphore_signal(barrier, 1, device_id=(dom, neighbour), device_id_type=mesh_ids)
+    pl.semaphore_wait(barrier, 2)
+
+    def own(index, low):
+        start = pl.multiple_of(index * share, share)
+        return x_ref[:, pl.ds(start, share), pl.ds(low, half)]
+
+    stage_f[0] = own(lax.rem(me + count - 1, count), 0)
+    stage_b[0] = own(lax.rem(me + 1, count), half)
+    for step in range(count - 1):
+        ahead = pltpu.make_async_remote_copy(
+            src_ref=stage_f.at[step],
+            dst_ref=land_f.at[step],
+            send_sem=send_f.at[step],
+            recv_sem=recv_f.at[step],
+            device_id=(dom, right),
+            device_id_type=mesh_ids,
+        )
+        behind = pltpu.make_async_remote_copy(
+            src_ref=stage_b.at[step],
+            dst_ref=land_b.at[step],
+            send_sem=send_b.at[step],
+            recv_sem=recv_b.at[step],
+            device_id=(dom, left),
+            device_id_type=mesh_ids,
+        )
+        ahead.start()
+        behind.start()
+        ahead.wait()
+        behind.wait()
+        forward_sum = land_f[step] + own(lax.rem(me + 2 * count - 2 - step, count), 0)
+        backward_sum = land_b[step] + own(lax.rem(me + 2 + step, count), half)
+        if step < count - 2:
+            stage_f[step + 1] = forward_sum
+            stage_b[step + 1] = backward_sum
+        else:
+            o_ref[:, :, pl.ds(0, half)] = forward_sum
+            o_ref[:, :, pl.ds(half, half)] = backward_sum
+
+
+def ring_scatter_kernel(full):
+    count = lax.axis_size("mat")
+    planes, rows, cols = full.shape
+    share = rows // count
+    half = cols // 2
+    piece = pltpu.VMEM((count - 1, planes, share, half), jnp.float32)
+    return pl.pallas_call(
+        functools.partial(ring_kernel, count, share, half),
+        out_shape=jax.ShapeDtypeStruct((planes, share, cols), jnp.float32),
+        in_specs=[pl.BlockSpec(memory_space=pltpu.VMEM)],
+        out_specs=pl.BlockSpec(memory_space=pltpu.VMEM),
+        scratch_shapes=[piece, piece, piece, piece]
+        + [pltpu.SemaphoreType.DMA((count - 1,))] * 4,
+        compiler_params=pltpu.CompilerParams(collective_id=0, has_side_effects=True),
+    )(full)
+
+
 def on_device(orbitals, potential, centre_first, centre_second, centre_third, correlation_pairs):
     block_orbs, window_cells, second_cells, third_cells = orbitals.shape
     patch_cells = potential.shape[0]
@@ -173,7 +241,9 @@
         return assembled
 
     both = jnp.stack([row_blocks(gram_full), row_blocks(energy_full)])
-    gram_rows, energy_rows = ring_scatter(both, 2)
+    blocks = both.shape[:2]
+    summed = ring_scatter_kernel(both.reshape((-1,) + both.shape[2:]))
+    gram_rows, energy_rows = summed.reshape(blocks + summed.shape[1:])
     columns = lax.axis_index("mat") * col_count + lax.iota(jnp.int32, col_count)
     block_ids = lax.iota(jnp.int32, local_blocks)
     column_pick = ((columns // per_block)[:, None] == block_ids[None, :]).astype(jnp.float32)

time: 143 us -> 145 us (1.014)
  Pallas kernels: 0 us -> 25.7 us
  waiting for transfers between devices: 52.4 us -> 34.1 us
  starting transfers between devices: 34.7 us -> 28.6 us
  other arithmetic: 29.3 us -> 25.1 us
  local copies, waits for them, and re-layouts: 8.63 us -> 10.6 us
  matrix products: 16.3 us -> 18.1 us
    pallas_call x0 -> x1, Pallas kernels: none -> 25.7 us  [ring_scatter_kernel(): pl.pallas_call(functools.partial(ring_kernel, count, share, half), out_sh...]
    ppermute x6 -> x0, waiting for transfers between devices: 16 us -> none  [the longest x3 11.8 us: ring_scatter(): ahead = lax.ppermute(ahead, 'mat', forward)]
    ppermute x6 -> x0, starting transfers between devices: 9.81 us -> none  [the longest x3 9.31 us: ring_scatter(): ahead = lax.ppermute(ahead, 'mat', forward)]
    ppermute x1, waiting for transfers between devices: 7.94 us -> 1.55 us  [on_device(): row_above = lax.ppermute(masked[:, :, second_cells - 1], 'mat', up)]
    add x6 -> x0, other arithmetic: 4.88 us -> none  [the longest x3 3.05 us: ring_scatter(): ahead = ahead + chunk(halves[0], lax.rem(me + 2 * count - 2 - step, count))]
    ppermute x8, starting transfers between devices: 22.6 us -> 25.3 us  [passed_along(): return lax.ppermute(block, axis, route)]
    unnamed x16 -> x24, local copies, waits for them, and re-layouts: 1.94 us -> 4.62 us
    ppermute x1, waiting for transfers between devices: 5.14 us -> 7.74 us  [on_device(): row_below = lax.ppermute(masked[:, :, 0], 'mat', down)]
  transfers between devices with their start and end apart: 16 -> 10, of which waited for: 13 -> 5; matrix products, arithmetic and copies ran while one was open for 19% -> 12% of each run, Pallas kernels for 0% -> 0%
where the time goes in v2:
time: 145 us; the launch traced here: 143 us
  waiting for transfers between devices  34.1 us (24%)
  starting transfers between devices  28.6 us (20%)
  Pallas kernels  25.7 us (18%)
  other arithmetic  25.1 us (17%)
  matrix products  18.1 us (12%)
  local copies, waits for them, and re-layouts  10.6 us (7%)
    pallas_call x1, Pallas kernels, ring_scatter_kernel(): pl.pallas_call(functools.partial(ring_kernel, count, share, half), out_sh...  25.7 us
    ppermute x8, starting transfers between devices, passed_along(): return lax.ppermute(block, axis, route)  25.3 us
    ppermute x8, waiting for transfers between devices, passed_along(): return lax.ppermute(block, axis, route)  24.8 us
    dot_general x18, matrix products, pair_product(): lax.dot_general(left, right, (((1, 2, 3), (1, 2, 3)), ((), ())), preferre...  15.7 us
    convert_element_type x2, other arithmetic, on_device(): stencil(ext, potential).astype(jnp.bfloat16)  9.46 us
    ppermute x1, waiting for transfers between devices, on_device(): row_below = lax.ppermute(masked[:, :, 0], 'mat', down)  7.74 us
    select_n x1, other arithmetic, on_device(): masked = jnp.where(inside, orbitals, jnp.zeros_like(orbitals))  5.94 us
    another operation x3, other arithmetic, on_device(): both = jnp.stack([row_blocks(gram_full), row_blocks(energy_full)])  4.64 us
  transfers between devices with their start and end apart: 10, of which 5 were waited for; matrix products, arithmetic and copies ran while one was open for 12% of the time, Pallas kernels for 0%

profile of v2, /device:TPU:6, one launch (start us, length us, event | category | flops | bytes accessed | tf_op | source)
XLA Modules:
  0.0 143.3 jit_solution(10347848798034325830)
XLA Ops:
  2.9 5.9 %fusion.1 = bf16[256,12,8,128]{3,0,2,1:T(8,128)(2,1)S(1)} fusion(bf16[256,12,8,128]{3,2,1,0:T(8,128)(2,1)} %param.6, s32[256,128]{1,0:T(8,128)S(1)} %subtract_multiply_fusion, s32[256,12,8]{0,2,1:T(8,128)S(1)} %broadcast_add_fusion, pred[12]{0:T(512)(128)(4,1)S(1)} %compare_and_fusion), kind=kLoop, calls=%fused_computation.2 | loop fusion | flops 12582912 | bytes 12812300 | tf_op jit(solution)/shard_map/jit(_where)/select_n | solution.py:182
  11.1 7.5 %collective-permute-start.1 = (bf16[256,4,8,128]{3,0,2,1:T(8,128)(2,1)S(1)}, bf16[256,4,8,128]{3,0,2,1:T(8,128)(2,1)S(1)}, u32[]{:S(2)}, u32[]{:S(2)}) collective-permute-start(bf16[256,4,8,128]{3,0,2,1:T(8,128)(2,1)S(1)} %get-tuple-element.3), channel_id=1, source_target_pairs={{4,0},{8,4},{12,8},{16,12},{20,16},{24,20},{28,24},{32,28},{36,32}... | collective-permute-start | bytes 6291464 | tf_op jit(solution)/shard_map/ppermute | solution.py:26
  18.7 2.4 %collective-permute-start.4 = (bf16[256,12,128]{2,0,1:T(8,128)(2,1)S(1)}, bf16[256,12,128]{2,0,1:T(8,128)(2,1)S(1)}, u32[]{:S(2)}, u32[]{:S(2)}) collective-permute-start(bf16[256,12,128]{2,0,1:T(8,128)(2,1)S(1)} %get-tuple-element.5), channel_id=1, source_target_pairs={{0,1},{1,2},{2,3},{3,0},{4,5},{5,6},{6,7},{7,4},{8,9},{9,10},{10,1... | collective-permute-start | bytes 2359304 | tf_op jit(solution)/shard_map/ppermute | solution.py:191
  21.8 7.7 %collective-permute-done.5 = bf16[256,12,128]{2,0,1:T(8,128)(2,1)S(1)} collective-permute-done((bf16[256,12,128]{2,0,1:T(8,128)(2,1)S(1)}, bf16[256,12,128]{2,0,1:T(8,128)(2,1)S(1)}, u32[]{:S(2)}, u32[]{:S(2)}) %collective-permute-start.5) | collective-permute-done | bytes 786464 | tf_op jit(solution)/shard_map/ppermute | solution.py:192
  29.6 1.6 %collective-permute-done.4 = bf16[256,12,128]{2,0,1:T(8,128)(2,1)S(1)} collective-permute-done((bf16[256,12,128]{2,0,1:T(8,128)(2,1)S(1)}, bf16[256,12,128]{2,0,1:T(8,128)(2,1)S(1)}, u32[]{:S(2)}, u32[]{:S(2)}) %collective-permute-start.4) | collective-permute-done | bytes 786464 | tf_op jit(solution)/shard_map/ppermute | solution.py:191
  31.3 7.5 %collective-permute-start.7 = (bf16[2,256,4,128]{3,1,2,0:T(8,128)(2,1)S(1)}, bf16[2,256,4,128]{3,1,2,0:T(8,128)(2,1)S(1)}, u32[]{:S(2)}, u32[]{:S(2)}) collective-permute-start(bf16[2,256,4,128]{3,1,2,0:T(8,128)(2,1)S(1)} %pad_maximum_fusion.10), channel_id=1, source_target_pairs={{4,0},{8,4},{12,8},{16,12},{20,16},{24,20},{28,24},{32,28},{36,32}... | collective-permute-start | bytes 1572872 | tf_op jit(solution)/shard_map/ppermute | solution.py:26
  39.0 8.8 %collective-permute-done.7 = bf16[2,256,4,128]{3,1,2,0:T(8,128)(2,1)S(1)} collective-permute-done((bf16[2,256,4,128]{3,1,2,0:T(8,128)(2,1)S(1)}, bf16[2,256,4,128]{3,1,2,0:T(8,128)(2,1)S(1)}, u32[]{:S(2)}, u32[]{:S(2)}) %collective-permute-start.7) | collective-permute-done | bytes 524320 | tf_op jit(solution)/shard_map/ppermute | solution.py:26
  47.9 7.6 %collective-permute-done.6 = bf16[2,256,4,128]{3,1,2,0:T(8,128)(2,1)S(1)} collective-permute-done((bf16[2,256,4,128]{3,1,2,0:T(8,128)(2,1)S(1)}, bf16[2,256,4,128]{3,1,2,0:T(8,128)(2,1)S(1)}, u32[]{:S(2)}, u32[]{:S(2)}) %collective-permute-start.6) | collective-permute-done | bytes 524320 | tf_op jit(solution)/shard_map/ppermute | solution.py:26
  57.9 3.3 %fusion.19 = bf16[256,4,8,128]{3,0,2,1:T(8,128)(2,1)S(1)} fusion(f32[256,4,8,128]{3,0,2,1:T(8,128)S(1)} %slice_convert_fusion, bf16[256,4,8,128]{3,0,2,1:T(8,128)(2,1)S(1)} %collective-permute-done.1, bf16[256,6,8,128]{3,0,2,1:T(8,128)(2,1)S(1)} %concatenate.47, bf16[256,6,1,128]{3,0,2,1:T(8,128)(2,1)S(1)} %get-tuple-element.22, ...), kind=kLoop, calls=%fused_computation.26 | loop fusion | flops 17825792 | bytes 14434304 | tf_op jit(solution)/shard_map/convert_element_type | solution.py:223
  61.2 1.4 fusion.68
  62.6 1.4 %convolution_bitcast_fusion.4 = f32[256,1,256]{2,0,1:T(8,128)} fusion(bf16[256,4,8,128]{3,0,2,1:T(8,128)(2,1)S(1)} %fusion.19, bf16[256,12,8,128]{3,0,2,1:T(8,128)(2,1)S(1)} %fusion.1), kind=kOutput, calls=%fused_computation.80 | convolution fusion | flops 536870912 | bytes 4456448 | tf_op jit(solution)/shard_map/dot_general | solution.py:72
  65.0 1.9 %copy-done.1 = bf16[256,12,8,128]{3,0,2,1:T(8,128)(2,1)S(1)} copy-done((bf16[256,12,8,128]{3,0,2,1:T(8,128)(2,1)S(1)}, bf16[256,12,8,128]{3,0,2,1:T(8,128)(2,1)}, u32[]{:S(2)}) %copy-start.1) | copy-done | bytes 6291480
  68.0 6.2 %fusion.7 = (bf16[256,4,8,128]{3,0,2,1:T(8,128)(2,1)S(1)}, bf16[256,4,8,128]{3,0,2,1:T(8,128)(2,1)S(1)}) fusion(f32[256,4,8,128]{3,0,2,1:T(8,128)S(1)} %slice_convert_fusion.1, bf16[256,4,8,128]{3,0,2,1:T(8,128)(2,1)S(1)} %collective-permute-done, bf16[256,6,8,128]{3,0,2,1:T(8,128)(2,1)S(1)} %concatenate.41, bf16[256,6,1,128]{3,0,2,1:T(8,128)(2,1)S(1)} %copy-done.5, ...), kind=kLoop, calls=%fused_computation.14 | loop fusion | flops 35651584 | bytes 28852224 | tf_op jit(solution)/shard_map/convert_element_type | solution.py:223
  74.2 2.1 %fusion.77 = f32[256,1,256]{2,0,1:T(8,128)S(1)} fusion(bf16[256,4,8,128]{3,0,2,1:T(8,128)(2,1)S(1)} %get-tuple-element.23, bf16[256,3,8,128]{3,0,2,1:T(8,128)(2,1)} %copy-done.6), kind=kOutput, calls=%fused_computation.77 | convolution fusion | flops 536870912 | bytes 3932160 | tf_op jit(solution)/shard_map/dot_general | solution.py:72
  77.2 1.4 copy-done.3
  87.4 5.1 %collective-permute-start.8 = (f32[3,256,256]{2,1,0:T(8,128)S(1)}, f32[3,256,256]{2,1,0:T(8,128)}, u32[]{:S(2)}, u32[]{:S(2)}) collective-permute-start(f32[3,256,256]{2,1,0:T(8,128)S(1)} %get-tuple-element.12), channel_id=1, source_target_pairs={{4,0},{8,4},{12,8},{16,12},{20,16},{24,20},{28,24},{32,28},{36,32}... | collective-permute-start | bytes 2359304 | tf_op jit(solution)/shard_map/ppermute | solution.py:26
  95.8 1.3 slice_bitcast_fusion.7
  97.1 5.1 %collective-permute-start.2 = (f32[3,256,256]{2,1,0:T(8,128)}, f32[3,256,256]{2,1,0:T(8,128)}, u32[]{:S(2)}, u32[]{:S(2)}) collective-permute-start(f32[3,256,256]{2,1,0:T(8,128)} %get-tuple-element.9), channel_id=1, source_target_pairs={{4,0},{8,4},{12,8},{16,12},{20,16},{24,20},{28,24},{32,28},{36,32}... | collective-permute-start | bytes 2359304 | tf_op jit(solution)/shard_map/ppermute | solution.py:26
  102.4 1.3 add_bitcast_fusion
  103.7 8.4 %collective-permute-done.3 = f32[3,256,256]{2,1,0:T(8,128)} collective-permute-done((f32[3,256,256]{2,1,0:T(8,128)}, f32[3,256,256]{2,1,0:T(8,128)}, u32[]{:S(2)}, u32[]{:S(2)}) %collective-permute-start.3) | collective-permute-done | bytes 786464 | tf_op jit(solution)/shard_map/ppermute | solution.py:26
  112.1 1.5 %add_bitcast_fusion.1 = f32[1,5,256,256]{3,2,1,0:T(8,128)S(1)} fusion(f32[3,256,256]{2,1,0:T(8,128)} %collective-permute-done.3, f32[3,256,256]{2,1,0:T(8,128)} %collective-permute-done.2, f32[3,256,256]{2,1,0:T(8,128)S(1)} %get-tuple-element.7), kind=kLoop, calls=%fused_computation.63 | loop fusion | flops 655360 | bytes 3670016 | tf_op jit(solution)/shard_map/stack | solution.py:243
  113.7 1.8 %pad_maximum_fusion = f32[2,5,256,256]{3,2,1,0:T(8,128)} fusion(f32[1,5,256,256]{3,2,1,0:T(8,128)S(1)} %add_bitcast_fusion, f32[1,5,256,256]{3,2,1,0:T(8,128)S(1)} %add_bitcast_fusion.1), kind=kLoop, calls=%fused_computation.51 | loop fusion | flops 655360 | bytes 5242880 | tf_op jit(solution)/shard_map/stack | solution.py:243
  115.5 25.7 %shard_map.77 = f32[10,64,256]{2,1,0:T(8,128)} custom-call(f32[10,256,256]{2,1,0:T(8,128)} %bitcast.203), custom_call_target="tpu_custom_call" | custom-call | tf_op jit(solution)/shard_map/pallas_call | solution.py:153
  141.1 2.2 %slice_multiply_fusion = (f32[5,64,256]{2,1,0:T(8,128)}, f32[5,64,256]{2,1,0:T(8,128)}) fusion(f32[10,64,256]{2,1,0:T(8,128)} %shard_map.77, s32[256]{0:T(256)S(1)} %and_select_fusion, bf16[64,2,5]{0,2,1:T(8,128)(2,1)S(1)} %fusion.91), kind=kOutput, calls=%fused_computation.116 | convolution fusion | flops 492032 | bytes 1313024 | tf_op jit(solution)/shard_map/rkb,cb,ar->kca/dot_general | solution.py:253
  (82 shorter events, 23.0 us)
Async XLA Ops:
  8.9 53.7 %copy-start = (bf16[256,12,8,128]{3,0,2,1:T(8,128)(2,1)}, bf16[256,12,8,128]{3,0,2,1:T(8,128)(2,1)S(1)}, u32[]{:S(2)}) copy-start(bf16[256,12,8,128]{3,0,2,1:T(8,128)(2,1)S(1)} %fusion.1) | copy-start | bytes 18874372
  9.0 20.6 %collective-permute-start.5 = (bf16[256,12,128]{2,0,1:T(8,128)(2,1)S(1)}, bf16[256,12,128]{2,0,1:T(8,128)(2,1)S(1)}, u32[]{:S(2)}, u32[]{:S(2)}) collective-permute-start(bf16[256,12,128]{2,0,1:T(8,128)(2,1)S(1)} %get-tuple-element.6), channel_id=1, source_target_pairs={{1,0},{2,1},{3,2},{0,3},{5,4},{6,5},{7,6},{4,7},{9,8},{10,9},{11,1... | collective-permute-start | bytes 2359304 | tf_op jit(solution)/shard_map/ppermute | solution.py:192
  11.1 45.3 %collective-permute-start.1 = (bf16[256,4,8,128]{3,0,2,1:T(8,128)(2,1)S(1)}, bf16[256,4,8,128]{3,0,2,1:T(8,128)(2,1)S(1)}, u32[]{:S(2)}, u32[]{:S(2)}) collective-permute-start(bf16[256,4,8,128]{3,0,2,1:T(8,128)(2,1)S(1)} %get-tuple-element.3), channel_id=1, source_target_pairs={{4,0},{8,4},{12,8},{16,12},{20,16},{24,20},{28,24},{32,28},{36,32}... | collective-permute-start | bytes 6291464 | tf_op jit(solution)/shard_map/ppermute | solution.py:26
  18.7 12.5 %collective-permute-start.4 = (bf16[256,12,128]{2,0,1:T(8,128)(2,1)S(1)}, bf16[256,12,128]{2,0,1:T(8,128)(2,1)S(1)}, u32[]{:S(2)}, u32[]{:S(2)}) collective-permute-start(bf16[256,12,128]{2,0,1:T(8,128)(2,1)S(1)} %get-tuple-element.5), channel_id=1, source_target_pairs={{0,1},{1,2},{2,3},{3,0},{4,5},{5,6},{6,7},{7,4},{8,9},{9,10},{10,1... | collective-permute-start | bytes 2359304 | tf_op jit(solution)/shard_map/ppermute | solution.py:191
  21.1 43.0 %collective-permute-start = (bf16[256,4,8,128]{3,0,2,1:T(8,128)(2,1)S(1)}, bf16[256,4,8,128]{3,0,2,1:T(8,128)(2,1)S(1)}, u32[]{:S(2)}, u32[]{:S(2)}) collective-permute-start(bf16[256,4,8,128]{3,0,2,1:T(8,128)(2,1)S(1)} %get-tuple-element.4), channel_id=1, source_target_pairs={{252,0},{0,4},{4,8},{8,12},{12,16},{16,20},{20,24},{24,28},{28,32}... | collective-permute-start | bytes 6291464 | tf_op jit(solution)/shard_map/ppermute | solution.py:26
  31.3 16.6 %collective-permute-start.7 = (bf16[2,256,4,128]{3,1,2,0:T(8,128)(2,1)S(1)}, bf16[2,256,4,128]{3,1,2,0:T(8,128)(2,1)S(1)}, u32[]{:S(2)}, u32[]{:S(2)}) collective-permute-start(bf16[2,256,4,128]{3,1,2,0:T(8,128)(2,1)S(1)} %pad_maximum_fusion.10), channel_id=1, source_target_pairs={{4,0},{8,4},{12,8},{16,12},{20,16},{24,20},{28,24},{32,28},{36,32}... | collective-permute-start | bytes 1572872 | tf_op jit(solution)/shard_map/ppermute | solution.py:26
  38.9 16.6 %collective-permute-start.6 = (bf16[2,256,4,128]{3,1,2,0:T(8,128)(2,1)S(1)}, bf16[2,256,4,128]{3,1,2,0:T(8,128)(2,1)S(1)}, u32[]{:S(2)}, u32[]{:S(2)}) collective-permute-start(bf16[2,256,4,128]{3,1,2,0:T(8,128)(2,1)S(1)} %pad_maximum_fusion.9), channel_id=1, source_target_pairs={{252,0},{0,4},{4,8},{8,12},{12,16},{16,20},{20,24},{24,28},{28,32}... | collective-permute-start | bytes 1572872 | tf_op jit(solution)/shard_map/ppermute | solution.py:26
  56.6 4.6 %copy-start.6 = (bf16[256,3,8,128]{3,0,2,1:T(8,128)(2,1)}, bf16[256,3,8,128]{3,0,2,1:T(8,128)(2,1)S(1)}, u32[]{:S(2)}) copy-start(bf16[256,3,8,128]{3,0,2,1:T(8,128)(2,1)S(1)} %slice.184) | copy-start | bytes 4718596
  57.1 0.7 copy-start.10
  61.2 1.4 %copy-start.2 = (bf16[256,4,8,128]{3,0,2,1:T(8,128)(2,1)}, bf16[256,4,8,128]{3,0,2,1:T(8,128)(2,1)S(1)}, u32[]{:S(2)}) copy-start(bf16[256,4,8,128]{3,0,2,1:T(8,128)(2,1)S(1)} %fusion.19) | copy-start | bytes 6291460
  64.1 2.8 %copy-start.1 = (bf16[256,12,8,128]{3,0,2,1:T(8,128)(2,1)S(1)}, bf16[256,12,8,128]{3,0,2,1:T(8,128)(2,1)}, u32[]{:S(2)}) copy-start(bf16[256,12,8,128]{3,0,2,1:T(8,128)(2,1)} %copy-done) | copy-start | bytes 18874372
  64.5 3.4 %slice-start = ((bf16[256,12,8,128]{3,0,2,1:T(8,128)(2,1)}), bf16[256,6,8,128]{3,0,2,1:T(8,128)(2,1)S(1)}, s32[]{:S(2)}) async-start(bf16[256,12,8,128]{3,0,2,1:T(8,128)(2,1)} %copy-done), calls=%async_computation | async-start | bytes 6291456 | tf_op jit(solution)/shard_map/slice | solution.py:206
  64.5 3.4 %copy-start.4 = (bf16[256,6,1,128]{3,0,2,1:T(8,128)(2,1)S(1)}, bf16[256,6,1,128]{3,0,2,1:T(8,128)(2,1)}, u32[]{:S(2)}) copy-start(bf16[256,6,1,128]{3,0,2,1:T(8,128)(2,1)} %get-tuple-element.19) | copy-start | bytes 1179652
  64.5 3.5 %copy-start.5 = (bf16[256,6,1,128]{3,0,2,1:T(8,128)(2,1)S(1)}, bf16[256,6,1,128]{3,0,2,1:T(8,128)(2,1)}, u32[]{:S(2)}) copy-start(bf16[256,6,1,128]{3,0,2,1:T(8,128)(2,1)} %get-tuple-element.20) | copy-start | bytes 1179652
  77.0 1.6 %copy-start.3 = (bf16[256,4,8,128]{3,0,2,1:T(8,128)(2,1)S(1)}, bf16[256,4,8,128]{3,0,2,1:T(8,128)(2,1)}, u32[]{:S(2)}) copy-start(bf16[256,4,8,128]{3,0,2,1:T(8,128)(2,1)} %copy-done.2) | copy-start | bytes 6291460
  79.3 1.4 copy-start.7
  85.0 1.0 copy-start.8
  85.0 1.0 copy-start.9
  87.4 15.0 %collective-permute-start.9 = (f32[3,256,256]{2,1,0:T(8,128)}, f32[3,256,256]{2,1,0:T(8,128)S(1)}, u32[]{:S(2)}, u32[]{:S(2)}) collective-permute-start(f32[3,256,256]{2,1,0:T(8,128)} %get-tuple-element.11), channel_id=1, source_target_pairs={{252,0},{0,4},{4,8},{8,12},{12,16},{16,20},{20,24},{24,28},{28,32}... | collective-permute-start | bytes 2359304 | tf_op jit(solution)/shard_map/ppermute | solution.py:26
  87.4 15.0 %collective-permute-start.8 = (f32[3,256,256]{2,1,0:T(8,128)S(1)}, f32[3,256,256]{2,1,0:T(8,128)}, u32[]{:S(2)}, u32[]{:S(2)}) collective-permute-start(f32[3,256,256]{2,1,0:T(8,128)S(1)} %get-tuple-element.12), channel_id=1, source_target_pairs={{4,0},{8,4},{12,8},{16,12},{20,16},{24,20},{28,24},{32,28},{36,32}... | collective-permute-start | bytes 2359304 | tf_op jit(solution)/shard_map/ppermute | solution.py:26
  95.8 6.4 %copy-start.11 = (s32[2,5,2]{1,2,0:T(2,128)S(1)}, s32[2,5,2]{1,2,0:T(2,128)}, u32[]{:S(2)}) copy-start(s32[2,5,2]{1,2,0:T(2,128)} %param.11) | copy-start | bytes 244
  97.1 15.1 %collective-permute-start.3 = (f32[3,256,256]{2,1,0:T(8,128)}, f32[3,256,256]{2,1,0:T(8,128)}, u32[]{:S(2)}, u32[]{:S(2)}) collective-permute-start(f32[3,256,256]{2,1,0:T(8,128)} %get-tuple-element.8), channel_id=1, source_target_pairs={{252,0},{0,4},{4,8},{8,12},{12,16},{16,20},{20,24},{24,28},{28,32}... | collective-permute-start | bytes 2359304 | tf_op jit(solution)/shard_map/ppermute | solution.py:26
  97.1 15.1 %collective-permute-start.2 = (f32[3,256,256]{2,1,0:T(8,128)}, f32[3,256,256]{2,1,0:T(8,128)}, u32[]{:S(2)}, u32[]{:S(2)}) collective-permute-start(f32[3,256,256]{2,1,0:T(8,128)} %get-tuple-element.9), channel_id=1, source_target_pairs={{4,0},{8,4},{12,8},{16,12},{20,16},{24,20},{28,24},{32,28},{36,32}... | collective-permute-start | bytes 2359304 | tf_op jit(solution)/shard_map/ppermute | solution.py:26

commit v3 on v2

--- a/solution.py
+++ b/solution.py
@@ -219,12 +219,13 @@
         masked[:, patch_cells:upper_start],
         jnp.concatenate([zero_plane, from_right[:, :-1]], axis=1),
     ]
+    gram_full = jnp.stack(
+        [jnp.stack([pair_product(phi_slots[a], phi_slots[b]) for b in range(3)], 1) for a in range(3)]
+    )
+    gram_full, left_ext, right_ext = lax.optimization_barrier((gram_full, left_ext, right_ext))
     applied_slots = [
         stencil(ext, potential).astype(jnp.bfloat16) for ext in (left_ext, own_ext, right_ext)
     ]
-    gram_full = jnp.stack(
-        [jnp.stack([pair_product(phi_slots[a], phi_slots[b]) for b in range(3)], 1) for a in range(3)]
-    )
     energy_full = jnp.stack(
         [
             jnp.stack([pair_product(applied_slots[a], phi_slots[b]) for b in range(3)], 1)

time: 145 us -> 153 us (1.055)
  other arithmetic: 25.1 us -> 40.7 us
  local copies, waits for them, and re-layouts: 10.6 us -> 6.39 us
  waiting for transfers between devices: 34.1 us -> 30.5 us
  Pallas kernels: 25.7 us -> 27.8 us
  starting transfers between devices: 28.6 us -> 26.6 us
    convert_element_type x2, other arithmetic: 9.46 us -> 19.2 us  [on_device(): stencil(ext, potential).astype(jnp.bfloat16)]
    ppermute x1, waiting for transfers between devices: 7.74 us -> 1.26 us  [on_device(): row_below = lax.ppermute(masked[:, :, 0], 'mat', down)]
    convert_element_type x3, other arithmetic: 2.05 us -> 7.64 us  [stencil(): centre_cells = extended[:, 1:-1, 1:-1, :].astype(jnp.float32)]
    ppermute x1, waiting for transfers between devices: 1.55 us -> 6.25 us  [on_device(): row_above = lax.ppermute(masked[:, :, second_cells - 1], 'mat', up)]
    unnamed x24 -> x36, local copies, waits for them, and re-layouts: 4.62 us -> 1.86 us
    pallas_call x1, Pallas kernels: 25.7 us -> 27.8 us  [ring_scatter_kernel(): pl.pallas_call(functools.partial(ring_kernel, count, share, half), out_sh...]
    ppermute x8, waiting for transfers between devices: 24.8 us -> 23 us  [passed_along(): return lax.ppermute(block, axis, route)]
  transfers between devices with their start and end apart: 10 -> 10, of which waited for: 5 -> 7; matrix products, arithmetic and copies ran while one was open for 12% -> 11% of each run, Pallas kernels for 0% -> 0%
where the time goes in v3:
time: 153 us; the launch traced here: 152 us
  other arithmetic  40.7 us (27%)
  waiting for transfers between devices  30.5 us (20%)
  Pallas kernels  27.8 us (18%)
  starting transfers between devices  26.6 us (17%)
  matrix products  19 us (12%)
  local copies, waits for them, and re-layouts  6.39 us (4%)
    pallas_call x1, Pallas kernels, ring_scatter_kernel(): pl.pallas_call(functools.partial(ring_kernel, count, share, half), out_sh...  27.8 us
    ppermute x8, starting transfers between devices, passed_along(): return lax.ppermute(block, axis, route)  24.4 us
    ppermute x8, waiting for transfers between devices, passed_along(): return lax.ppermute(block, axis, route)  23 us
    convert_element_type x2, other arithmetic, on_device(): stencil(ext, potential).astype(jnp.bfloat16)  19.2 us
    dot_general x18, matrix products, pair_product(): lax.dot_general(left, right, (((1, 2, 3), (1, 2, 3)), ((), ())), preferre...  16.7 us
    convert_element_type x3, other arithmetic, stencil(): centre_cells = extended[:, 1:-1, 1:-1, :].astype(jnp.float32)  7.64 us
    ppermute x1, waiting for transfers between devices, on_device(): row_above = lax.ppermute(masked[:, :, second_cells - 1], 'mat', up)  6.25 us
    select_n x1, other arithmetic, on_device(): masked = jnp.where(inside, orbitals, jnp.zeros_like(orbitals))  6 us
  transfers between devices with their start and end apart: 10, of which 7 were waited for; matrix products, arithmetic and copies ran while one was open for 11% of the time, Pallas kernels for 0%

profile of v3, /device:TPU:6, one launch (start us, length us, event | category | flops | bytes accessed | tf_op | source)
XLA Modules:
  0.0 152.3 jit_solution(13794046605966549871)
XLA Ops:
  2.9 6.0 %fusion.1 = bf16[256,12,8,128]{3,0,1,2:T(8,128)(2,1)S(1)} fusion(bf16[256,12,8,128]{3,2,1,0:T(8,128)(2,1)} %param.6, s32[256,128]{1,0:T(8,128)S(1)} %subtract_multiply_fusion, s32[256,12,8]{0,1,2:T(8,128)S(1)} %broadcast_add_fusion, pred[12]{0:T(512)(128)(4,1)S(1)} %compare_and_fusion), kind=kLoop, calls=%fused_computation.2 | loop fusion | flops 12582912 | bytes 12812300 | tf_op jit(solution)/shard_map/jit(_where)/select_n | solution.py:182
  9.1 2.3 %collective-permute-start.2 = (bf16[256,12,128]{2,0,1:T(8,128)(2,1)S(1)}, bf16[256,12,128]{2,0,1:T(8,128)(2,1)S(1)}, u32[]{:S(2)}, u32[]{:S(2)}) collective-permute-start(bf16[256,12,128]{2,0,1:T(8,128)(2,1)S(1)} %get-tuple-element.12), channel_id=1, source_target_pairs={{0,1},{1,2},{2,3},{3,0},{4,5},{5,6},{6,7},{7,4},{8,9},{9,10},{10,1... | collective-permute-start | bytes 2359304 | tf_op jit(solution)/shard_map/ppermute | solution.py:191
  11.4 2.7 %slice_convert_fusion.2 = (f32[256,4,8,128]{3,0,1,2:T(8,128)S(1)}, bf16[256,4,8,128]{3,0,1,2:T(8,128)(2,1)}, bf16[256,4,8,128]{3,0,1,2:T(8,128)(2,1)S(1)}, bf16[256,4,8,128]{3,0,1,2:T(8,128)(2,1)S(1)}) fusion(bf16[256,12,8,128]{3,0,1,2:T(8,128)(2,1)S(1)} %fusion.1), kind=kLoop, calls=%fused_computation.176 | loop fusion | flops 1048576 | bytes 16777216 | tf_op jit(solution)/shard_map/convert_element_type | solution.py:57
  14.4 7.1 %collective-permute-start.1 = (bf16[256,4,8,128]{3,0,1,2:T(8,128)(2,1)}, bf16[256,4,8,128]{3,0,1,2:T(8,128)(2,1)S(1)}, u32[]{:S(2)}, u32[]{:S(2)}) collective-permute-start(bf16[256,4,8,128]{3,0,1,2:T(8,128)(2,1)} %get-tuple-element.9), channel_id=1, source_target_pairs={{4,0},{8,4},{12,8},{16,12},{20,16},{24,20},{28,24},{32,28},{36,32}... | collective-permute-start | bytes 6291464 | tf_op jit(solution)/shard_map/ppermute | solution.py:26
  22.2 6.2 %collective-permute-done.2 = bf16[256,12,128]{2,0,1:T(8,128)(2,1)S(1)} collective-permute-done((bf16[256,12,128]{2,0,1:T(8,128)(2,1)S(1)}, bf16[256,12,128]{2,0,1:T(8,128)(2,1)S(1)}, u32[]{:S(2)}, u32[]{:S(2)}) %collective-permute-start.2) | collective-permute-done | bytes 786464 | tf_op jit(solution)/shard_map/ppermute | solution.py:191
  30.0 6.7 %collective-permute-start.5 = (bf16[2,256,4,128]{3,1,2,0:T(8,128)(2,1)S(1)}, bf16[2,256,4,128]{3,1,2,0:T(8,128)(2,1)S(1)}, u32[]{:S(2)}, u32[]{:S(2)}) collective-permute-start(bf16[2,256,4,128]{3,1,2,0:T(8,128)(2,1)S(1)} %pad_maximum_fusion.6), channel_id=1, source_target_pairs={{4,0},{8,4},{12,8},{16,12},{20,16},{24,20},{28,24},{32,28},{36,32}... | collective-permute-start | bytes 1572872 | tf_op jit(solution)/shard_map/ppermute | solution.py:26
  36.8 3.7 %fusion.16 = bf16[256,4,8,128]{3,0,1,2:T(8,128)(2,1)S(1)} fusion(f32[256,4,8,128]{3,0,1,2:T(8,128)S(1)} %get-tuple-element.8, bf16[256,6,8,128]{3,0,1,2:T(8,128)(2,1)S(1)} %slice-done, bf16[256,6,1,128]{3,0,1,2:T(8,128)(2,1)S(1)} %slice_bitcast_fusion.8, bf16[256,6,1,128]{3,0,1,2:T(8,128)(2,1)S(1)} %slice_bitcast_fusion.9, ...), kind=kLoop, calls=%fused_computation.25 | loop fusion | flops 17825792 | bytes 14434304 | tf_op jit(solution)/shard_map/convert_element_type | solution.py:227
  40.5 1.4 fusion.55
  42.0 8.7 %collective-permute-done.4 = bf16[2,256,4,128]{3,1,2,0:T(8,128)(2,1)S(1)} collective-permute-done((bf16[2,256,4,128]{3,1,2,0:T(8,128)(2,1)S(1)}, bf16[2,256,4,128]{3,1,2,0:T(8,128)(2,1)S(1)}, u32[]{:S(2)}, u32[]{:S(2)}) %collective-permute-start.4) | collective-permute-done | bytes 524320 | tf_op jit(solution)/shard_map/ppermute | solution.py:26
  51.7 1.4 fusion.64
  61.2 1.4 slice_bitcast_fusion.4
  62.6 2.5 %slice_convert_fusion.1 = f32[256,4,8,128]{3,0,2,1:T(8,128)} fusion(bf16[256,6,10,128]{3,0,2,1:T(8,128)(2,1)S(1)} %fusion.24), kind=kLoop, calls=%fused_computation.66 | loop fusion | flops 1048576 | bytes 6291456 | tf_op jit(solution)/shard_map/convert_element_type | solution.py:57
  65.1 2.5 %slice_convert_fusion = f32[256,4,8,128]{3,0,2,1:T(8,128)} fusion(bf16[256,6,10,128]{3,0,2,1:T(8,128)(2,1)S(1)} %fusion.26), kind=kLoop, calls=%fused_computation.65 | loop fusion | flops 1048576 | bytes 6291456 | tf_op jit(solution)/shard_map/convert_element_type | solution.py:57
  67.6 15.6 %fusion.10 = (bf16[256,4,8,128]{3,0,2,1:T(8,128)(2,1)}, bf16[256,4,8,128]{3,0,2,1:T(8,128)(2,1)}) fusion(f32[256,4,8,128]{3,0,2,1:T(8,128)} %slice_convert_fusion.1, f32[4,8,128]{2,1,0:T(8,128)S(1)} %copy-done.15, bf16[256,6,10,128]{3,0,2,1:T(8,128)(2,1)S(1)} %fusion.24, f32[256,4,8,128]{3,0,2,1:T(8,128)} %slice_convert_fusion, ...), kind=kLoop, calls=%fused_computation.19 | loop fusion | flops 31457280 | bytes 29376512 | tf_op jit(solution)/shard_map/convert_element_type | solution.py:227
  83.2 3.1 %convolution_bitcast_fusion.3 = f32[256,1,256]{2,0,1:T(8,128)S(1)} fusion(bf16[256,4,8,128]{3,0,2,1:T(8,128)(2,1)} %get-tuple-element.30, bf16[256,4,8,128]{3,0,1,2:T(8,128)(2,1)} %copy-done.9), kind=kOutput, calls=%fused_computation.89 | convolution fusion | flops 536870912 | bytes 4456448 | tf_op jit(solution)/shard_map/dot_general | solution.py:72
  90.2 5.3 %collective-permute-start.6 = (f32[3,256,256]{2,1,0:T(8,128)}, f32[3,256,256]{2,1,0:T(8,128)S(1)}, u32[]{:S(2)}, u32[]{:S(2)}) collective-permute-start(f32[3,256,256]{2,1,0:T(8,128)} %get-tuple-element.15), channel_id=1, source_target_pairs={{4,0},{8,4},{12,8},{16,12},{20,16},{24,20},{28,24},{32,28},{36,32}... | collective-permute-start | bytes 2359304 | tf_op jit(solution)/shard_map/ppermute | solution.py:26
  98.0 1.3 slice_bitcast_fusion.2
  99.3 5.1 %collective-permute-start.8 = (f32[3,256,256]{2,1,0:T(8,128)}, f32[3,256,256]{2,1,0:T(8,128)}, u32[]{:S(2)}, u32[]{:S(2)}) collective-permute-start(f32[3,256,256]{2,1,0:T(8,128)} %get-tuple-element.18), channel_id=1, source_target_pairs={{4,0},{8,4},{12,8},{16,12},{20,16},{24,20},{28,24},{32,28},{36,32}... | collective-permute-start | bytes 2359304 | tf_op jit(solution)/shard_map/ppermute | solution.py:26
  105.3 5.1 %collective-permute-done.7 = f32[3,256,256]{2,1,0:T(8,128)S(1)} collective-permute-done((f32[3,256,256]{2,1,0:T(8,128)}, f32[3,256,256]{2,1,0:T(8,128)S(1)}, u32[]{:S(2)}, u32[]{:S(2)}) %collective-permute-start.7) | collective-permute-done | bytes 786464 | tf_op jit(solution)/shard_map/ppermute | solution.py:26
  110.7 8.3 %collective-permute-done.9 = f32[3,256,256]{2,1,0:T(8,128)} collective-permute-done((f32[3,256,256]{2,1,0:T(8,128)}, f32[3,256,256]{2,1,0:T(8,128)}, u32[]{:S(2)}, u32[]{:S(2)}) %collective-permute-start.9) | collective-permute-done | bytes 786464 | tf_op jit(solution)/shard_map/ppermute | solution.py:26
  119.0 1.5 %add_bitcast_fusion = f32[1,5,256,256]{3,2,1,0:T(8,128)S(1)} fusion(f32[3,256,256]{2,1,0:T(8,128)} %collective-permute-done.9, f32[3,256,256]{2,1,0:T(8,128)} %collective-permute-done.8, f32[3,256,256]{2,1,0:T(8,128)S(1)} %get-tuple-element.16), kind=kLoop, calls=%fused_computation.71 | loop fusion | flops 655360 | bytes 3670016 | tf_op jit(solution)/shard_map/stack | solution.py:244
  120.5 1.8 %pad_maximum_fusion = f32[2,5,256,256]{3,2,1,0:T(8,128)} fusion(f32[1,5,256,256]{3,2,1,0:T(8,128)S(1)} %add_bitcast_fusion, f32[1,5,256,256]{3,2,1,0:T(8,128)S(1)} %add_bitcast_fusion.1), kind=kLoop, calls=%fused_computation.60 | loop fusion | flops 655360 | bytes 5242880 | tf_op jit(solution)/shard_map/stack | solution.py:244
  122.3 27.8 %shard_map.77 = f32[10,64,256]{2,1,0:T(8,128)} custom-call(f32[10,256,256]{2,1,0:T(8,128)} %bitcast.185), custom_call_target="tpu_custom_call" | custom-call | tf_op jit(solution)/shard_map/pallas_call | solution.py:153
  150.1 2.2 %slice_multiply_fusion = (f32[5,64,256]{2,1,0:T(8,128)}, f32[5,64,256]{2,1,0:T(8,128)}) fusion(f32[10,64,256]{2,1,0:T(8,128)} %shard_map.77, s32[256]{0:T(256)S(1)} %and_select_fusion, bf16[64,2,5]{0,2,1:T(8,128)(2,1)S(1)} %fusion.111), kind=kOutput, calls=%fused_computation.126 | convolution fusion | flops 492032 | bytes 1313024 | tf_op jit(solution)/shard_map/rkb,cb,ar->kca/dot_general | solution.py:254
  (97 shorter events, 21.3 us)
Async XLA Ops:
  8.9 12.5 %copy-start = (bf16[256,12,8,128]{3,0,1,2:T(8,128)(2,1)}, bf16[256,12,8,128]{3,0,1,2:T(8,128)(2,1)S(1)}, u32[]{:S(2)}) copy-start(bf16[256,12,8,128]{3,0,1,2:T(8,128)(2,1)S(1)} %fusion.1) | copy-start | bytes 18874372
  9.1 19.4 %collective-permute-start.2 = (bf16[256,12,128]{2,0,1:T(8,128)(2,1)S(1)}, bf16[256,12,128]{2,0,1:T(8,128)(2,1)S(1)}, u32[]{:S(2)}, u32[]{:S(2)}) collective-permute-start(bf16[256,12,128]{2,0,1:T(8,128)(2,1)S(1)} %get-tuple-element.12), channel_id=1, source_target_pairs={{0,1},{1,2},{2,3},{3,0},{4,5},{5,6},{6,7},{7,4},{8,9},{9,10},{10,1... | collective-permute-start | bytes 2359304 | tf_op jit(solution)/shard_map/ppermute | solution.py:191
  11.4 18.4 %collective-permute-start.3 = (bf16[256,12,128]{2,0,1:T(8,128)(2,1)S(1)}, bf16[256,12,128]{2,0,1:T(8,128)(2,1)S(1)}, u32[]{:S(2)}, u32[]{:S(2)}) collective-permute-start(bf16[256,12,128]{2,0,1:T(8,128)(2,1)S(1)} %get-tuple-element.13), channel_id=1, source_target_pairs={{1,0},{2,1},{3,2},{0,3},{5,4},{6,5},{7,6},{4,7},{9,8},{10,9},{11,1... | collective-permute-start | bytes 2359304 | tf_op jit(solution)/shard_map/ppermute | solution.py:192
  14.0 43.2 %copy-start.9 = (bf16[256,4,8,128]{3,0,1,2:T(8,128)(2,1)}, bf16[256,4,8,128]{3,0,1,2:T(8,128)(2,1)S(1)}, u32[]{:S(2)}) copy-start(bf16[256,4,8,128]{3,0,1,2:T(8,128)(2,1)S(1)} %get-tuple-element.10) | copy-start | bytes 6291460
  14.3 36.6 %collective-permute-start = (bf16[256,4,8,128]{3,0,2,1:T(8,128)(2,1)S(1)}, bf16[256,4,8,128]{3,0,2,1:T(8,128)(2,1)S(1)}, u32[]{:S(2)}, u32[]{:S(2)}) collective-permute-start(bf16[256,4,8,128]{3,0,2,1:T(8,128)(2,1)S(1)} %copy.9), channel_id=1, source_target_pairs={{252,0},{0,4},{4,8},{8,12},{12,16},{16,20},{20,24},{24,28},{28,32}... | collective-permute-start | bytes 6291464 | tf_op jit(solution)/shard_map/ppermute | solution.py:26
  14.3 7.1 %copy-start.15 = (f32[4,8,128]{2,1,0:T(8,128)S(1)}, f32[4,8,128]{2,1,0:T(8,128)}, u32[]{:S(2)}) copy-start(f32[4,8,128]{2,1,0:T(8,128)} %param.7) | copy-start | bytes 49156
  14.4 39.5 %collective-permute-start.1 = (bf16[256,4,8,128]{3,0,1,2:T(8,128)(2,1)}, bf16[256,4,8,128]{3,0,1,2:T(8,128)(2,1)S(1)}, u32[]{:S(2)}, u32[]{:S(2)}) collective-permute-start(bf16[256,4,8,128]{3,0,1,2:T(8,128)(2,1)} %get-tuple-element.9), channel_id=1, source_target_pairs={{4,0},{8,4},{12,8},{16,12},{20,16},{24,20},{28,24},{32,28},{36,32}... | collective-permute-start | bytes 6291464 | tf_op jit(solution)/shard_map/ppermute | solution.py:26
  21.4 15.4 %copy-start.1 = (bf16[256,12,8,128]{3,0,1,2:T(8,128)(2,1)S(1)}, bf16[256,12,8,128]{3,0,1,2:T(8,128)(2,1)}, u32[]{:S(2)}) copy-start(bf16[256,12,8,128]{3,0,1,2:T(8,128)(2,1)} %copy-done) | copy-start | bytes 18874372
  29.8 7.0 %slice-start = ((bf16[256,12,8,128]{3,0,1,2:T(8,128)(2,1)}), bf16[256,6,8,128]{3,0,1,2:T(8,128)(2,1)S(1)}, s32[]{:S(2)}) async-start(bf16[256,12,8,128]{3,0,1,2:T(8,128)(2,1)} %copy-done), calls=%async_computation | async-start | bytes 6291456 | tf_op jit(solution)/shard_map/slice | solution.py:206
  29.9 20.8 %collective-permute-start.4 = (bf16[2,256,4,128]{3,1,2,0:T(8,128)(2,1)S(1)}, bf16[2,256,4,128]{3,1,2,0:T(8,128)(2,1)S(1)}, u32[]{:S(2)}, u32[]{:S(2)}) collective-permute-start(bf16[2,256,4,128]{3,1,2,0:T(8,128)(2,1)S(1)} %pad_maximum_fusion.5), channel_id=1, source_target_pairs={{252,0},{0,4},{4,8},{8,12},{12,16},{16,20},{20,24},{24,28},{28,32}... | collective-permute-start | bytes 1572872 | tf_op jit(solution)/shard_map/ppermute | solution.py:26
  30.0 20.8 %collective-permute-start.5 = (bf16[2,256,4,128]{3,1,2,0:T(8,128)(2,1)S(1)}, bf16[2,256,4,128]{3,1,2,0:T(8,128)(2,1)S(1)}, u32[]{:S(2)}, u32[]{:S(2)}) collective-permute-start(bf16[2,256,4,128]{3,1,2,0:T(8,128)(2,1)S(1)} %pad_maximum_fusion.6), channel_id=1, source_target_pairs={{4,0},{8,4},{12,8},{16,12},{20,16},{24,20},{28,24},{32,28},{36,32}... | collective-permute-start | bytes 1572872 | tf_op jit(solution)/shard_map/ppermute | solution.py:26
  40.5 11.2 %copy-start.7 = (bf16[256,4,8,128]{3,0,1,2:T(8,128)(2,1)}, bf16[256,4,8,128]{3,0,1,2:T(8,128)(2,1)S(1)}, u32[]{:S(2)}) copy-start(bf16[256,4,8,128]{3,0,1,2:T(8,128)(2,1)S(1)} %fusion.16) | copy-start | bytes 6291460
  51.0 4.6 %copy-start.11 = (bf16[256,3,8,128]{3,0,2,1:T(8,128)(2,1)}, bf16[256,3,8,128]{3,0,2,1:T(8,128)(2,1)S(1)}, u32[]{:S(2)}) copy-start(bf16[256,3,8,128]{3,0,2,1:T(8,128)(2,1)S(1)} %slice.185) | copy-start | bytes 4718596
  53.9 5.7 %copy-start.2 = (bf16[256,4,8,128]{3,0,1,2:T(8,128)(2,1)}, bf16[256,4,8,128]{3,0,1,2:T(8,128)(2,1)S(1)}, u32[]{:S(2)}) copy-start(bf16[256,4,8,128]{3,0,1,2:T(8,128)(2,1)S(1)} %collective-permute-done.1) | copy-start | bytes 6291460
  89.4 6.1 %copy-start.3 = (bf16[256,4,8,128]{3,0,1,2:T(8,128)(2,1)S(1)}, bf16[256,4,8,128]{3,0,1,2:T(8,128)(2,1)}, u32[]{:S(2)}) copy-start(bf16[256,4,8,128]{3,0,1,2:T(8,128)(2,1)} %copy-done.2) | copy-start | bytes 6291460
  89.4 6.1 %copy-start.8 = (bf16[256,4,8,128]{3,0,1,2:T(8,128)(2,1)S(1)}, bf16[256,4,8,128]{3,0,1,2:T(8,128)(2,1)}, u32[]{:S(2)}) copy-start(bf16[256,4,8,128]{3,0,1,2:T(8,128)(2,1)} %copy-done.7) | copy-start | bytes 6291460
  90.2 6.0 %copy-start.13 = (f32[256,1,256]{2,0,1:T(8,128)S(1)}, f32[256,1,256]{2,0,1:T(8,128)}, u32[]{:S(2)}) copy-start(f32[256,1,256]{2,0,1:T(8,128)} %fusion.55) | copy-start | bytes 786436
  90.2 6.0 %copy-start.14 = (f32[256,1,256]{2,0,1:T(8,128)S(1)}, f32[256,1,256]{2,0,1:T(8,128)}, u32[]{:S(2)}) copy-start(f32[256,1,256]{2,0,1:T(8,128)} %fusion.64) | copy-start | bytes 786436
  90.2 15.1 %collective-permute-start.6 = (f32[3,256,256]{2,1,0:T(8,128)}, f32[3,256,256]{2,1,0:T(8,128)S(1)}, u32[]{:S(2)}, u32[]{:S(2)}) collective-permute-start(f32[3,256,256]{2,1,0:T(8,128)} %get-tuple-element.15), channel_id=1, source_target_pairs={{4,0},{8,4},{12,8},{16,12},{20,16},{24,20},{28,24},{32,28},{36,32}... | collective-permute-start | bytes 2359304 | tf_op jit(solution)/shard_map/ppermute | solution.py:26
  95.5 14.9 %collective-permute-start.7 = (f32[3,256,256]{2,1,0:T(8,128)}, f32[3,256,256]{2,1,0:T(8,128)S(1)}, u32[]{:S(2)}, u32[]{:S(2)}) collective-permute-start(f32[3,256,256]{2,1,0:T(8,128)} %slice_bitcast_fusion.7), channel_id=1, source_target_pairs={{252,0},{0,4},{4,8},{8,12},{12,16},{16,20},{20,24},{24,28},{28,32}... | collective-permute-start | bytes 2359304 | tf_op jit(solution)/shard_map/ppermute | solution.py:26
  98.0 6.5 %copy-start.16 = (s32[2,5,2]{1,2,0:T(2,128)S(1)}, s32[2,5,2]{1,2,0:T(2,128)}, u32[]{:S(2)}) copy-start(s32[2,5,2]{1,2,0:T(2,128)} %param.11) | copy-start | bytes 244
  98.0 12.5 %copy-start.4 = (f32[3,256,256]{2,1,0:T(8,128)S(1)}, f32[3,256,256]{2,1,0:T(8,128)}, u32[]{:S(2)}) copy-start(f32[3,256,256]{2,1,0:T(8,128)} %get-tuple-element.14) | copy-start | bytes 2359300
  99.3 19.7 %collective-permute-start.9 = (f32[3,256,256]{2,1,0:T(8,128)}, f32[3,256,256]{2,1,0:T(8,128)}, u32[]{:S(2)}, u32[]{:S(2)}) collective-permute-start(f32[3,256,256]{2,1,0:T(8,128)} %get-tuple-element.17), channel_id=1, source_target_pairs={{252,0},{0,4},{4,8},{8,12},{12,16},{16,20},{20,24},{24,28},{28,32}... | collective-permute-start | bytes 2359304 | tf_op jit(solution)/shard_map/ppermute | solution.py:26
  99.3 19.7 %collective-permute-start.8 = (f32[3,256,256]{2,1,0:T(8,128)}, f32[3,256,256]{2,1,0:T(8,128)}, u32[]{:S(2)}, u32[]{:S(2)}) collective-permute-start(f32[3,256,256]{2,1,0:T(8,128)} %get-tuple-element.18), channel_id=1, source_target_pairs={{4,0},{8,4},{12,8},{16,12},{20,16},{24,20},{28,24},{32,28},{36,32}... | collective-permute-start | bytes 2359304 | tf_op jit(solution)/shard_map/ppermute | solution.py:26
  (4 other events, 10.2 us)

commit v4 on v2

--- a/solution.py
+++ b/solution.py
@@ -96,20 +96,51 @@
     return jnp.concatenate([ahead, behind], axis=-1)
 
 
-def ring_kernel(count, share, half, x_ref, o_ref, stage_f, stage_b, land_f, land_b, send_f, recv_f, send_b, recv_b):
+def exchange_kernel(
+    count, domains, share, half, x_ref, o_ref, total, from_left, from_right, stage_f, stage_b,
+    land_f, land_b, dom_send, dom_recv, send_f, recv_f, send_b, recv_b,
+):
     me = lax.axis_index("mat")
     dom = lax.axis_index("dom")
     right = lax.rem(me + 1, count)
     left = lax.rem(me + count - 1, count)
+    up = lax.rem(dom + 1, domains)
+    down = lax.rem(dom + domains - 1, domains)
     mesh_ids = pl.DeviceIdType.MESH
     barrier = pltpu.get_barrier_semaphore()
-    for neighbour in (left, right):
-        pl.semaphore_signal(barrier, 1, device_id=(dom, neighbour), device_id_type=mesh_ids)
-    pl.semaphore_wait(barrier, 2)
+    for device in ((dom, left), (dom, right), (down, me), (up, me)):
+        pl.semaphore_signal(barrier, 1, device_id=device, device_id_type=mesh_ids)
+    pl.semaphore_wait(barrier, 4)
+
+    to_down = pltpu.make_async_remote_copy(
+        src_ref=x_ref.at[0],
+        dst_ref=from_right,
+        send_sem=dom_send.at[0],
+        recv_sem=dom_recv.at[0],
+        device_id=(down, me),
+        device_id_type=mesh_ids,
+    )
+    to_up = pltpu.make_async_remote_copy(
+        src_ref=x_ref.at[2],
+        dst_ref=from_left,
+        send_sem=dom_send.at[1],
+        recv_sem=dom_recv.at[1],
+        device_id=(up, me),
+        device_id_type=mesh_ids,
+    )
+    to_down.start()
+    to_up.start()
+    to_down.wait()
+    to_up.wait()
+    total[:, 0] = from_left[:, 0]
+    total[:, 1] = from_left[:, 1] + x_ref[1, :, 0]
+    total[:, 2] = from_left[:, 2] + x_ref[1, :, 1] + from_right[:, 0]
+    total[:, 3] = x_ref[1, :, 2] + from_right[:, 1]
+    total[:, 4] = from_right[:, 2]
 
     def own(index, low):
         start = pl.multiple_of(index * share, share)
-        return x_ref[:, pl.ds(start, share), pl.ds(low, half)]
+        return total[:, :, pl.ds(start, share), pl.ds(low, half)]
 
     stage_f[0] = own(lax.rem(me + count - 1, count), 0)
     stage_b[0] = own(lax.rem(me + 1, count), half)
@@ -140,24 +171,37 @@
             stage_f[step + 1] = forward_sum
             stage_b[step + 1] = backward_sum
         else:
-            o_ref[:, :, pl.ds(0, half)] = forward_sum
-            o_ref[:, :, pl.ds(half, half)] = backward_sum
-
-
-def ring_scatter_kernel(full):
+            o_ref[:, :, :, pl.ds(0, half)] = forward_sum
+            o_ref[:, :, :, pl.ds(half, half)] = backward_sum
+
+
+def exchange_and_sum(full):
     count = lax.axis_size("mat")
-    planes, rows, cols = full.shape
+    domains = lax.axis_size("dom")
+    slots, outputs, columns, rows, cols = full.shape
     share = rows // count
     half = cols // 2
-    piece = pltpu.VMEM((count - 1, planes, share, half), jnp.float32)
+    piece = pltpu.VMEM((count - 1, outputs, 2 * columns - 1, share, half), jnp.float32)
+    arrived = pltpu.VMEM((outputs, columns, rows, cols), jnp.float32)
     return pl.pallas_call(
-        functools.partial(ring_kernel, count, share, half),
-        out_shape=jax.ShapeDtypeStruct((planes, share, cols), jnp.float32),
+        functools.partial(exchange_kernel, count, domains, share, half),
+        out_shape=jax.ShapeDtypeStruct((outputs, 2 * columns - 1, share, cols), jnp.float32),
         in_specs=[pl.BlockSpec(memory_space=pltpu.VMEM)],
         out_specs=pl.BlockSpec(memory_space=pltpu.VMEM),
-        scratch_shapes=[piece, piece, piece, piece]
+        scratch_shapes=[
+            pltpu.VMEM((outputs, 2 * columns - 1, rows, cols), jnp.float32),
+            arrived,
+            arrived,
+            piece,
+            piece,
+            piece,
+            piece,
+        ]
+        + [pltpu.SemaphoreType.DMA((2,))] * 2
         + [pltpu.SemaphoreType.DMA((count - 1,))] * 4,
-        compiler_params=pltpu.CompilerParams(collective_id=0, has_side_effects=True),
+        compiler_params=pltpu.CompilerParams(
+            collective_id=0, has_side_effects=True, vmem_limit_bytes=48 * 1024 * 1024
+        ),
     )(full)
 
 
@@ -222,28 +266,19 @@
     applied_slots = [
         stencil(ext, potential).astype(jnp.bfloat16) for ext in (left_ext, own_ext, right_ext)
     ]
-    gram_full = jnp.stack(
-        [jnp.stack([pair_product(phi_slots[a], phi_slots[b]) for b in range(3)], 1) for a in range(3)]
-    )
-    energy_full = jnp.stack(
+    full = jnp.stack(
         [
-            jnp.stack([pair_product(applied_slots[a], phi_slots[b]) for b in range(3)], 1)
-            for a in range(3)
+            jnp.stack(
+                [
+                    jnp.stack([pair_product(phi_slots[a], phi_slots[b]) for a in range(3)]),
+                    jnp.stack([pair_product(applied_slots[a], phi_slots[b]) for a in range(3)]),
+                ]
+            )
+            for b in range(3)
         ]
     )
     col_count = block_orbs // mat_count
-
-    def row_blocks(full):
-        assembled = jnp.pad(full[:, :, 1], ((1, 1), (0, 0), (0, 0)))
-        for slot_index, offset in ((0, -1), (2, 1)):
-            arrived = passed_along(full[:, :, slot_index], "dom", offset)
-            assembled = assembled + jnp.pad(arrived, ((2 - slot_index, slot_index), (0, 0), (0, 0)))
-        return assembled
-
-    both = jnp.stack([row_blocks(gram_full), row_blocks(energy_full)])
-    blocks = both.shape[:2]
-    summed = ring_scatter_kernel(both.reshape((-1,) + both.shape[2:]))
-    gram_rows, energy_rows = summed.reshape(blocks + summed.shape[1:])
+    gram_rows, energy_rows = exchange_and_sum(full)
     columns = lax.axis_index("mat") * col_count + lax.iota(jnp.int32, col_count)
     block_ids = lax.iota(jnp.int32, local_blocks)
     column_pick = ((columns // per_block)[:, None] == block_ids[None, :]).astype(jnp.float32)

time: 145 us -> 144 us (level)
  Pallas kernels: 25.7 us -> 50.1 us
  waiting for transfers between devices: 34.1 us -> 16.3 us
  starting transfers between devices: 28.6 us -> 17.6 us
  local copies, waits for them, and re-layouts: 10.6 us -> 14.7 us
    pallas_call x1, Pallas kernels: 25.7 us -> 50.1 us  [exchange_and_sum(): pl.pallas_call(functools.partial(exchange_kernel, count, domains, share,...]
    ppermute x8 -> x4, waiting for transfers between devices: 24.8 us -> 13.6 us  [passed_along(): return lax.ppermute(block, axis, route)]
    ppermute x8 -> x4, starting transfers between devices: 25.3 us -> 14.4 us  [passed_along(): return lax.ppermute(block, axis, route)]
    ppermute x1, waiting for transfers between devices: 7.74 us -> 2.69 us  [on_device(): row_below = lax.ppermute(masked[:, :, 0], 'mat', down)]
    another operation x9, other arithmetic: 5.3 us -> 1.04 us  [the longest x3 0.72 us: on_device(): jnp.stack([jnp.stack([jnp.stack([pair_product(phi_slots[a], phi_slots[b])...]
    slice x0 -> x1, other arithmetic: none -> 3.82 us  [on_device(): to_right = masked[:, upper_start - 1:window_cells - 1]]
    squeeze x2 -> x0, local copies, waits for them, and re-layouts: 2.35 us -> none  [row_blocks(): assembled = jnp.pad(full[:, :, 1], ((1, 1), (0, 0), (0, 0)))]
    concatenate x1, local copies, waits for them, and re-layouts: 0.53 us -> 2.11 us  [on_device(): jnp.concatenate([zero_plane, zero_plane, from_right], axis=1)]
  transfers between devices with their start and end apart: 10 -> 6, of which waited for: 5 -> 2; matrix products, arithmetic and copies ran while one was open for 12% -> 12% of each run, Pallas kernels for 0% -> 0%
where the time goes in v4:
time: 144 us; the launch traced here: 143 us
  Pallas kernels  50.1 us (35%)
  other arithmetic  26.3 us (18%)
  starting transfers between devices  17.6 us (12%)
  matrix products  17 us (12%)
  waiting for transfers between devices  16.3 us (11%)
  local copies, waits for them, and re-layouts  14.7 us (10%)
    pallas_call x1, Pallas kernels, exchange_and_sum(): pl.pallas_call(functools.partial(exchange_kernel, count, domains, share,...  50.1 us
    dot_general x18, matrix products, pair_product(): lax.dot_general(left, right, (((1, 2, 3), (1, 2, 3)), ((), ())), preferre...  15.7 us
    ppermute x4, starting transfers between devices, passed_along(): return lax.ppermute(block, axis, route)  14.4 us
    ppermute x4, waiting for transfers between devices, passed_along(): return lax.ppermute(block, axis, route)  13.6 us
    convert_element_type x2, other arithmetic, on_device(): stencil(ext, potential).astype(jnp.bfloat16)  10.9 us
    select_n x1, other arithmetic, on_device(): masked = jnp.where(inside, orbitals, jnp.zeros_like(orbitals))  5.94 us
    unnamed x14, local copies, waits for them, and re-layouts  5.83 us
    slice x1, other arithmetic, on_device(): to_right = masked[:, upper_start - 1:window_cells - 1]  3.82 us
  transfers between devices with their start and end apart: 6, of which 2 were waited for; matrix products, arithmetic and copies ran while one was open for 12% of the time, Pallas kernels for 0%

profile of v4, /device:TPU:6, one launch (start us, length us, event | category | flops | bytes accessed | tf_op | source)
XLA Modules:
  0.0 143.1 jit_solution(13326283262145423337)
XLA Ops:
  2.9 5.9 %fusion.1 = bf16[256,12,8,128]{3,0,2,1:T(8,128)(2,1)S(1)} fusion(bf16[256,12,8,128]{3,2,1,0:T(8,128)(2,1)} %param.6, s32[256,128]{1,0:T(8,128)S(1)} %subtract_multiply_fusion, s32[256,12,8]{0,2,1:T(8,128)S(1)} %broadcast_add_fusion, pred[12]{0:T(512)(128)(4,1)S(1)} %compare_and_fusion), kind=kLoop, calls=%fused_computation.2 | loop fusion | flops 12582912 | bytes 12812300 | tf_op jit(solution)/shard_map/jit(_where)/select_n | solution.py:226
  8.9 1.5 %slice_bitcast_fusion.1 = (bf16[256,12,128]{2,0,1:T(8,128)(2,1)}, bf16[256,12,128]{2,0,1:T(8,128)(2,1)}) fusion(bf16[256,12,8,128]{3,0,2,1:T(8,128)(2,1)S(1)} %fusion.1), kind=kLoop, calls=%fused_computation.87 | loop fusion | bytes 3145728 | tf_op jit(solution)/shard_map/squeeze | solution.py:235
  10.4 0.8 collective-permute-start.3
  11.2 2.4 %collective-permute-start.2 = (bf16[256,12,128]{2,0,1:T(8,128)(2,1)}, bf16[256,12,128]{2,0,1:T(8,128)(2,1)}, u32[]{:S(2)}, u32[]{:S(2)}) collective-permute-start(bf16[256,12,128]{2,0,1:T(8,128)(2,1)} %get-tuple-element.5), channel_id=1, source_target_pairs={{0,1},{1,2},{2,3},{3,0},{4,5},{5,6},{6,7},{7,4},{8,9},{9,10},{10,1... | collective-permute-start | bytes 2359304 | tf_op jit(solution)/shard_map/ppermute | solution.py:235
  13.6 3.8 %fusion.118 = (bf16[256,4,8,128]{3,0,2,1:T(8,128)(2,1)}, f32[256,4,8,128]{3,0,2,1:T(8,128)}, bf16[256,4,8,128]{3,0,2,1:T(8,128)(2,1)}) fusion(bf16[256,12,8,128]{3,0,2,1:T(8,128)(2,1)S(1)} %fusion.1), kind=kLoop, calls=%fused_computation.163 | loop fusion | flops 1048576 | bytes 14680064 | tf_op jit(solution)/shard_map/slice | solution.py:228
  17.4 7.2 %collective-permute-start.1 = (bf16[256,4,8,128]{3,0,2,1:T(8,128)(2,1)}, bf16[256,4,8,128]{3,0,2,1:T(8,128)(2,1)}, u32[]{:S(2)}, u32[]{:S(2)}) collective-permute-start(bf16[256,4,8,128]{3,0,2,1:T(8,128)(2,1)} %get-tuple-element.4), channel_id=1, source_target_pairs={{4,0},{8,4},{12,8},{16,12},{20,16},{24,20},{28,24},{32,28},{36,32}... | collective-permute-start | bytes 6291464 | tf_op jit(solution)/shard_map/ppermute | solution.py:26
  24.8 2.8 %copy-done.1 = bf16[256,12,8,128]{3,0,2,1:T(8,128)(2,1)S(1)} copy-done((bf16[256,12,8,128]{3,0,2,1:T(8,128)(2,1)S(1)}, bf16[256,12,8,128]{3,0,2,1:T(8,128)(2,1)}, u32[]{:S(2)}) %copy-start.1) | copy-done | bytes 6291480
  28.4 2.7 %collective-permute-done.3 = bf16[256,12,128]{2,0,1:T(8,128)(2,1)S(1)} collective-permute-done((bf16[256,12,128]{2,0,1:T(8,128)(2,1)}, bf16[256,12,128]{2,0,1:T(8,128)(2,1)S(1)}, u32[]{:S(2)}, u32[]{:S(2)}) %collective-permute-start.3) | collective-permute-done | bytes 786464 | tf_op jit(solution)/shard_map/ppermute | solution.py:236
  31.1 1.1 slice_bitcast_fusion.7
  32.4 7.1 %collective-permute-start.5 = (bf16[2,256,4,128]{3,1,2,0:T(8,128)(2,1)S(1)}, bf16[2,256,4,128]{3,1,2,0:T(8,128)(2,1)S(1)}, u32[]{:S(2)}, u32[]{:S(2)}) collective-permute-start(bf16[2,256,4,128]{3,1,2,0:T(8,128)(2,1)S(1)} %pad_maximum_fusion.8), channel_id=1, source_target_pairs={{4,0},{8,4},{12,8},{16,12},{20,16},{24,20},{28,24},{32,28},{36,32}... | collective-permute-start | bytes 1572872 | tf_op jit(solution)/shard_map/ppermute | solution.py:26
  39.5 1.0 slice_bitcast_fusion.2
  40.6 13.6 %collective-permute-done.4 = bf16[2,256,4,128]{3,1,2,0:T(8,128)(2,1)S(1)} collective-permute-done((bf16[2,256,4,128]{3,1,2,0:T(8,128)(2,1)S(1)}, bf16[2,256,4,128]{3,1,2,0:T(8,128)(2,1)S(1)}, u32[]{:S(2)}, u32[]{:S(2)}) %collective-permute-start.4) | collective-permute-done | bytes 524320 | tf_op jit(solution)/shard_map/ppermute | solution.py:26
  55.4 1.0 slice-done
  57.1 1.3 copy-done.2
  58.4 0.9 slice-done.2
  59.3 6.1 %fusion.7 = (bf16[256,4,8,128]{3,0,2,1:T(8,128)(2,1)S(1)}, bf16[256,4,8,128]{3,0,2,1:T(8,128)(2,1)S(1)}) fusion(f32[256,4,8,128]{3,0,2,1:T(8,128)S(1)} %slice_convert_fusion.1, bf16[256,4,8,128]{3,0,2,1:T(8,128)(2,1)S(1)} %collective-permute-done, bf16[256,6,8,128]{3,0,2,1:T(8,128)(2,1)S(1)} %concatenate.41, ...), kind=kLoop, calls=%fused_computation.15 | loop fusion | flops 35651584 | bytes 28852224 | tf_op jit(solution)/shard_map/convert_element_type | solution.py:267
  68.4 1.8 %slice_convert_fusion = f32[256,4,8,128]{3,0,2,1:T(8,128)S(1)} fusion(bf16[256,4,8,128]{3,0,2,1:T(8,128)(2,1)} %collective-permute-done.1), kind=kLoop, calls=%fused_computation.58 | loop fusion | flops 1048576 | bytes 6291456 | tf_op jit(solution)/shard_map/convert_element_type | solution.py:57
  70.3 2.1 %concatenate.47 = bf16[256,6,8,128]{3,0,2,1:T(8,128)(2,1)S(1)} pad(bf16[256,4,8,128]{3,0,2,1:T(8,128)(2,1)} %collective-permute-done.1, bf16[]{:T(256)} %constant.61.clone.1), padding=0_0x2_0x0_0x0_0 | pad | bytes 5242882 | tf_op jit(solution)/shard_map/concatenate | solution.py:258
  72.4 4.8 %fusion.19 = bf16[256,4,8,128]{3,0,2,1:T(8,128)(2,1)S(1)} fusion(f32[256,4,8,128]{3,0,2,1:T(8,128)S(1)} %slice_convert_fusion, bf16[256,4,8,128]{3,0,2,1:T(8,128)(2,1)} %collective-permute-done.1, bf16[256,6,8,128]{3,0,2,1:T(8,128)(2,1)S(1)} %concatenate.47, bf16[256,6,1,128]{3,0,2,1:T(8,128)(2,1)S(1)} %get-tuple-element.16, ...), kind=kLoop, calls=%fused_computation.27 | loop fusion | flops 17825792 | bytes 14434304 | tf_op jit(solution)/shard_map/convert_element_type | solution.py:267
  80.1 1.6 %slice.157 = bf16[256,3,8,128]{3,0,2,1:T(8,128)(2,1)S(1)} slice(bf16[256,4,8,128]{3,0,2,1:T(8,128)(2,1)} %collective-permute-done.1), slice={[0:256], [0:3], [0:8], [0:128]} | slice | bytes 3145728 | tf_op jit(solution)/shard_map/slice | solution.py:264
  86.2 2.2 %fusion.50 = f32[1,256,256]{2,1,0:T(8,128)S(1)} fusion(bf16[256,3,8,128]{3,0,2,1:T(8,128)(2,1)S(1)} %slice.155, bf16[256,4,8,128]{3,0,2,1:T(8,128)(2,1)} %collective-permute-done.1), kind=kOutput, calls=%fused_computation.67 | convolution fusion | flops 402653184 | bytes 3407872 | tf_op jit(solution)/shard_map/dot_general | solution.py:72
  88.4 2.2 %convolution_bitcast_fusion.2 = f32[1,256,256]{2,1,0:T(8,128)S(1)} fusion(bf16[256,12,8,128]{3,0,2,1:T(8,128)(2,1)S(1)} %bitcast.193, bf16[256,4,8,128]{3,0,2,1:T(8,128)(2,1)} %collective-permute-done.1), kind=kOutput, calls=%fused_computation.77 | convolution fusion | flops 402653184 | bytes 3932160 | tf_op jit(solution)/shard_map/dot_general | solution.py:72
  92.0 50.1 %shard_map.77 = f32[2,5,64,256]{3,2,1,0:T(8,128)S(1)} custom-call(f32[3,2,3,256,256]{4,3,2,1,0:T(8,128)S(1)} %pad_maximum_fusion.x_ref), custom_call_target="tpu_custom_call" | custom-call | tf_op jit(solution)/shard_map/pallas_call | solution.py:186
  142.0 1.1 bitcast_multiply_fusion
  (63 shorter events, 17.0 us)
Async XLA Ops:
  8.9 8.6 %copy-start = (bf16[256,12,8,128]{3,0,2,1:T(8,128)(2,1)}, bf16[256,12,8,128]{3,0,2,1:T(8,128)(2,1)S(1)}, u32[]{:S(2)}) copy-start(bf16[256,12,8,128]{3,0,2,1:T(8,128)(2,1)S(1)} %fusion.1) | copy-start | bytes 18874372
  10.4 20.7 %collective-permute-start.3 = (bf16[256,12,128]{2,0,1:T(8,128)(2,1)}, bf16[256,12,128]{2,0,1:T(8,128)(2,1)S(1)}, u32[]{:S(2)}, u32[]{:S(2)}) collective-permute-start(bf16[256,12,128]{2,0,1:T(8,128)(2,1)} %get-tuple-element.6), channel_id=1, source_target_pairs={{1,0},{2,1},{3,2},{0,3},{5,4},{6,5},{7,6},{4,7},{9,8},{10,9},{11,1... | collective-permute-start | bytes 2359304 | tf_op jit(solution)/shard_map/ppermute | solution.py:236
  11.2 13.4 %copy-start.4 = (s32[2,5,2]{1,2,0:T(2,128)S(1)}, s32[2,5,2]{1,2,0:T(2,128)}, u32[]{:S(2)}) copy-start(s32[2,5,2]{1,2,0:T(2,128)} %param.11) | copy-start | bytes 244
  11.2 19.9 %collective-permute-start.2 = (bf16[256,12,128]{2,0,1:T(8,128)(2,1)}, bf16[256,12,128]{2,0,1:T(8,128)(2,1)}, u32[]{:S(2)}, u32[]{:S(2)}) collective-permute-start(bf16[256,12,128]{2,0,1:T(8,128)(2,1)} %get-tuple-element.5), channel_id=1, source_target_pairs={{0,1},{1,2},{2,3},{3,0},{4,5},{5,6},{6,7},{7,4},{8,9},{9,10},{10,1... | collective-permute-start | bytes 2359304 | tf_op jit(solution)/shard_map/ppermute | solution.py:235
  17.4 36.9 %collective-permute-start = (bf16[256,4,8,128]{3,0,2,1:T(8,128)(2,1)}, bf16[256,4,8,128]{3,0,2,1:T(8,128)(2,1)S(1)}, u32[]{:S(2)}, u32[]{:S(2)}) collective-permute-start(bf16[256,4,8,128]{3,0,2,1:T(8,128)(2,1)} %get-tuple-element.2), channel_id=1, source_target_pairs={{252,0},{0,4},{4,8},{8,12},{12,16},{16,20},{20,24},{24,28},{28,32}... | collective-permute-start | bytes 6291464 | tf_op jit(solution)/shard_map/ppermute | solution.py:26
  17.4 51.0 %collective-permute-start.1 = (bf16[256,4,8,128]{3,0,2,1:T(8,128)(2,1)}, bf16[256,4,8,128]{3,0,2,1:T(8,128)(2,1)}, u32[]{:S(2)}, u32[]{:S(2)}) collective-permute-start(bf16[256,4,8,128]{3,0,2,1:T(8,128)(2,1)} %get-tuple-element.4), channel_id=1, source_target_pairs={{4,0},{8,4},{12,8},{16,12},{20,16},{24,20},{28,24},{32,28},{36,32}... | collective-permute-start | bytes 6291464 | tf_op jit(solution)/shard_map/ppermute | solution.py:26
  24.8 2.8 %copy-start.1 = (bf16[256,12,8,128]{3,0,2,1:T(8,128)(2,1)S(1)}, bf16[256,12,8,128]{3,0,2,1:T(8,128)(2,1)}, u32[]{:S(2)}) copy-start(bf16[256,12,8,128]{3,0,2,1:T(8,128)(2,1)} %copy-done) | copy-start | bytes 18874372
  32.2 21.9 %collective-permute-start.4 = (bf16[2,256,4,128]{3,1,2,0:T(8,128)(2,1)S(1)}, bf16[2,256,4,128]{3,1,2,0:T(8,128)(2,1)S(1)}, u32[]{:S(2)}, u32[]{:S(2)}) collective-permute-start(bf16[2,256,4,128]{3,1,2,0:T(8,128)(2,1)S(1)} %pad_maximum_fusion.7), channel_id=1, source_target_pairs={{252,0},{0,4},{4,8},{8,12},{12,16},{16,20},{20,24},{24,28},{28,32}... | collective-permute-start | bytes 1572872 | tf_op jit(solution)/shard_map/ppermute | solution.py:26
  32.4 21.8 %collective-permute-start.5 = (bf16[2,256,4,128]{3,1,2,0:T(8,128)(2,1)S(1)}, bf16[2,256,4,128]{3,1,2,0:T(8,128)(2,1)S(1)}, u32[]{:S(2)}, u32[]{:S(2)}) collective-permute-start(bf16[2,256,4,128]{3,1,2,0:T(8,128)(2,1)S(1)} %pad_maximum_fusion.8), channel_id=1, source_target_pairs={{4,0},{8,4},{12,8},{16,12},{20,16},{24,20},{28,24},{32,28},{36,32}... | collective-permute-start | bytes 1572872 | tf_op jit(solution)/shard_map/ppermute | solution.py:26
  54.1 2.2 %slice-start = ((s8[6291456]{0:T(1024)(128)(4,1)}), s8[4194304]{0:T(1024)(128)(4,1)S(1)}, s32[]{:S(2)}) async-start(s8[6291456]{0:T(1024)(128)(4,1)} %bitcast.192), calls=%async_computation | async-start | bytes 8388608
  54.3 2.7 %slice-start.1 = ((s8[6291456]{0:T(1024)(128)(4,1)}), s8[2097152]{0:T(1024)(128)(4,1)S(1)}, s32[]{:S(2)}) async-start(s8[6291456]{0:T(1024)(128)(4,1)} %bitcast.192), calls=%async_computation.1 | async-start | bytes 4194304
  54.8 3.6 %copy-start.2 = (f32[256,4,8,128]{3,0,2,1:T(8,128)S(1)}, f32[256,4,8,128]{3,0,2,1:T(8,128)}, u32[]{:S(2)}) copy-start(f32[256,4,8,128]{3,0,2,1:T(8,128)} %get-tuple-element.3) | copy-start | bytes 12582916
  54.9 4.4 %slice-start.2 = ((bf16[256,12,8,128]{3,0,2,1:T(8,128)(2,1)}), bf16[256,6,8,128]{3,0,2,1:T(8,128)(2,1)S(1)}, s32[]{:S(2)}) async-start(bf16[256,12,8,128]{3,0,2,1:T(8,128)(2,1)} %copy-done), calls=%async_computation.2 | async-start | bytes 6291456 | tf_op jit(solution)/shard_map/slice | solution.py:250
  54.9 4.4 %copy-start.3 = (f32[4,8,128]{2,1,0:T(8,128)S(1)}, f32[4,8,128]{2,1,0:T(8,128)}, u32[]{:S(2)}) copy-start(f32[4,8,128]{2,1,0:T(8,128)} %param.7) | copy-start | bytes 49156

commit v5 on v4

--- a/solution.py
+++ b/solution.py
@@ -112,67 +112,77 @@
         pl.semaphore_signal(barrier, 1, device_id=device, device_id_type=mesh_ids)
     pl.semaphore_wait(barrier, 4)
 
-    to_down = pltpu.make_async_remote_copy(
-        src_ref=x_ref.at[0],
-        dst_ref=from_right,
-        send_sem=dom_send.at[0],
-        recv_sem=dom_recv.at[0],
-        device_id=(down, me),
-        device_id_type=mesh_ids,
-    )
-    to_up = pltpu.make_async_remote_copy(
-        src_ref=x_ref.at[2],
-        dst_ref=from_left,
-        send_sem=dom_send.at[1],
-        recv_sem=dom_recv.at[1],
-        device_id=(up, me),
-        device_id_type=mesh_ids,
-    )
-    to_down.start()
-    to_up.start()
-    to_down.wait()
-    to_up.wait()
-    total[:, 0] = from_left[:, 0]
-    total[:, 1] = from_left[:, 1] + x_ref[1, :, 0]
-    total[:, 2] = from_left[:, 2] + x_ref[1, :, 1] + from_right[:, 0]
-    total[:, 3] = x_ref[1, :, 2] + from_right[:, 1]
-    total[:, 4] = from_right[:, 2]
-
-    def own(index, low):
-        start = pl.multiple_of(index * share, share)
-        return total[:, :, pl.ds(start, share), pl.ds(low, half)]
-
-    stage_f[0] = own(lax.rem(me + count - 1, count), 0)
-    stage_b[0] = own(lax.rem(me + 1, count), half)
-    for step in range(count - 1):
-        ahead = pltpu.make_async_remote_copy(
-            src_ref=stage_f.at[step],
-            dst_ref=land_f.at[step],
-            send_sem=send_f.at[step],
-            recv_sem=recv_f.at[step],
-            device_id=(dom, right),
+    exchanges = []
+    for part in range(2):
+        low = part * half
+        to_down = pltpu.make_async_remote_copy(
+            src_ref=x_ref.at[0, :, :, :, pl.ds(low, half)],
+            dst_ref=from_right.at[part],
+            send_sem=dom_send.at[2 * part],
+            recv_sem=dom_recv.at[2 * part],
+            device_id=(down, me),
             device_id_type=mesh_ids,
         )
-        behind = pltpu.make_async_remote_copy(
-            src_ref=stage_b.at[step],
-            dst_ref=land_b.at[step],
-            send_sem=send_b.at[step],
-            recv_sem=recv_b.at[step],
-            device_id=(dom, left),
+        to_up = pltpu.make_async_remote_copy(
+            src_ref=x_ref.at[2, :, :, :, pl.ds(low, half)],
+            dst_ref=from_left.at[part],
+            send_sem=dom_send.at[2 * part + 1],
+            recv_sem=dom_recv.at[2 * part + 1],
+            device_id=(up, me),
             device_id_type=mesh_ids,
         )
-        ahead.start()
-        behind.start()
-        ahead.wait()
-        behind.wait()
-        forward_sum = land_f[step] + own(lax.rem(me + 2 * count - 2 - step, count), 0)
-        backward_sum = land_b[step] + own(lax.rem(me + 2 + step, count), half)
-        if step < count - 2:
-            stage_f[step + 1] = forward_sum
-            stage_b[step + 1] = backward_sum
-        else:
-            o_ref[:, :, :, pl.ds(0, half)] = forward_sum
-            o_ref[:, :, :, pl.ds(half, half)] = backward_sum
+        to_down.start()
+        to_up.start()
+        exchanges.append((to_down, to_up))
+
+    for part in range(2):
+        low = part * half
+        for copy in exchanges[part]:
+            copy.wait()
+        lefts, rights = from_left.at[part], from_right.at[part]
+        here = total.at[part]
+        here[:, 0] = lefts[:, 0]
+        here[:, 1] = lefts[:, 1] + x_ref[1, :, 0, :, pl.ds(low, half)]
+        here[:, 2] = lefts[:, 2] + x_ref[1, :, 1, :, pl.ds(low, half)] + rights[:, 0]
+        here[:, 3] = x_ref[1, :, 2, :, pl.ds(low, half)] + rights[:, 1]
+        here[:, 4] = rights[:, 2]
+
+        def own(output, index):
+            start = pl.multiple_of(index * share, share)
+            return here[output, :, pl.ds(start, share), :]
+
+        stage_f[part, 0] = own(0, lax.rem(me + count - 1, count))
+        stage_b[part, 0] = own(1, lax.rem(me + 1, count))
+        for step in range(count - 1):
+            slot = part * (count - 1) + step
+            ahead = pltpu.make_async_remote_copy(
+                src_ref=stage_f.at[part, step],
+                dst_ref=land_f.at[part, step],
+                send_sem=send_f.at[slot],
+                recv_sem=recv_f.at[slot],
+                device_id=(dom, right),
+                device_id_type=mesh_ids,
+            )
+            behind = pltpu.make_async_remote_copy(
+                src_ref=stage_b.at[part, step],
+                dst_ref=land_b.at[part, step],
+                send_sem=send_b.at[slot],
+                recv_sem=recv_b.at[slot],
+                device_id=(dom, left),
+                device_id_type=mesh_ids,
+            )
+            ahead.start()
+            behind.start()
+            ahead.wait()
+            behind.wait()
+            forward_sum = land_f[part, step] + own(0, lax.rem(me + 2 * count - 2 - step, count))
+            backward_sum = land_b[part, step] + own(1, lax.rem(me + 2 + step, count))
+            if step < count - 2:
+                stage_f[part, step + 1] = forward_sum
+                stage_b[part, step + 1] = backward_sum
+            else:
+                o_ref[0, :, :, pl.ds(low, half)] = forward_sum
+                o_ref[1, :, :, pl.ds(low, half)] = backward_sum
 
 
 def exchange_and_sum(full):
@@ -181,15 +191,16 @@
     slots, outputs, columns, rows, cols = full.shape
     share = rows // count
     half = cols // 2
-    piece = pltpu.VMEM((count - 1, outputs, 2 * columns - 1, share, half), jnp.float32)
-    arrived = pltpu.VMEM((outputs, columns, rows, cols), jnp.float32)
+    offsets = 2 * columns - 1
+    piece = pltpu.VMEM((2, count - 1, offsets, share, half), jnp.float32)
+    arrived = pltpu.VMEM((2, outputs, columns, rows, half), jnp.float32)
     return pl.pallas_call(
         functools.partial(exchange_kernel, count, domains, share, half),
-        out_shape=jax.ShapeDtypeStruct((outputs, 2 * columns - 1, share, cols), jnp.float32),
+        out_shape=jax.ShapeDtypeStruct((outputs, offsets, share, cols), jnp.float32),
         in_specs=[pl.BlockSpec(memory_space=pltpu.VMEM)],
         out_specs=pl.BlockSpec(memory_space=pltpu.VMEM),
         scratch_shapes=[
-            pltpu.VMEM((outputs, 2 * columns - 1, rows, cols), jnp.float32),
+            pltpu.VMEM((2, outputs, offsets, rows, half), jnp.float32),
             arrived,
             arrived,
             piece,
@@ -197,8 +208,8 @@
             piece,
             piece,
         ]
-        + [pltpu.SemaphoreType.DMA((2,))] * 2
-        + [pltpu.SemaphoreType.DMA((count - 1,))] * 4,
+        + [pltpu.SemaphoreType.DMA((4,))] * 2
+        + [pltpu.SemaphoreType.DMA((2 * (count - 1),))] * 4,
         compiler_params=pltpu.CompilerParams(
             collective_id=0, has_side_effects=True, vmem_limit_bytes=48 * 1024 * 1024
         ),

time: 144 us -> 142 us (0.986)
  Pallas kernels: 50.1 us -> 47.7 us
    pallas_call x1, Pallas kernels: 50.1 us -> 47.7 us  [exchange_and_sum(): pl.pallas_call(functools.partial(exchange_kernel, count, domains, share,...]
where the time goes in v5:
time: 142 us; the launch traced here: 141 us
  Pallas kernels  47.7 us (34%)
  other arithmetic  26.3 us (19%)
  starting transfers between devices  17.6 us (12%)
  matrix products  17 us (12%)
  waiting for transfers between devices  16.3 us (11%)
  local copies, waits for them, and re-layouts  14.7 us (10%)
    pallas_call x1, Pallas kernels, exchange_and_sum(): pl.pallas_call(functools.partial(exchange_kernel, count, domains, share,...  47.7 us
    dot_general x18, matrix products, pair_product(): lax.dot_general(left, right, (((1, 2, 3), (1, 2, 3)), ((), ())), preferre...  15.7 us
    ppermute x4, starting transfers between devices, passed_along(): return lax.ppermute(block, axis, route)  14.4 us
    ppermute x4, waiting for transfers between devices, passed_along(): return lax.ppermute(block, axis, route)  13.6 us
    convert_element_type x2, other arithmetic, on_device(): stencil(ext, potential).astype(jnp.bfloat16)  10.9 us
    select_n x1, other arithmetic, on_device(): masked = jnp.where(inside, orbitals, jnp.zeros_like(orbitals))  5.94 us
    unnamed x14, local copies, waits for them, and re-layouts  5.83 us
    slice x1, other arithmetic, on_device(): to_right = masked[:, upper_start - 1:window_cells - 1]  3.82 us
  transfers between devices with their start and end apart: 6, of which 2 were waited for; matrix products, arithmetic and copies ran while one was open for 12% of the time, Pallas kernels for 0%

profile of v5, /device:TPU:6, one launch (start us, length us, event | category | flops | bytes accessed | tf_op | source)
XLA Modules:
  0.0 140.7 jit_solution(163286861841794385)
XLA Ops:
  2.9 5.9 %fusion.1 = bf16[256,12,8,128]{3,0,2,1:T(8,128)(2,1)S(1)} fusion(bf16[256,12,8,128]{3,2,1,0:T(8,128)(2,1)} %param.6, s32[256,128]{1,0:T(8,128)S(1)} %subtract_multiply_fusion, s32[256,12,8]{0,2,1:T(8,128)S(1)} %broadcast_add_fusion, pred[12]{0:T(512)(128)(4,1)S(1)} %compare_and_fusion), kind=kLoop, calls=%fused_computation.2 | loop fusion | flops 12582912 | bytes 12812300 | tf_op jit(solution)/shard_map/jit(_where)/select_n | solution.py:237
  8.9 1.5 %slice_bitcast_fusion.1 = (bf16[256,12,128]{2,0,1:T(8,128)(2,1)}, bf16[256,12,128]{2,0,1:T(8,128)(2,1)}) fusion(bf16[256,12,8,128]{3,0,2,1:T(8,128)(2,1)S(1)} %fusion.1), kind=kLoop, calls=%fused_computation.87 | loop fusion | bytes 3145728 | tf_op jit(solution)/shard_map/squeeze | solution.py:246
  10.4 0.8 collective-permute-start.3
  11.2 2.4 %collective-permute-start.2 = (bf16[256,12,128]{2,0,1:T(8,128)(2,1)}, bf16[256,12,128]{2,0,1:T(8,128)(2,1)}, u32[]{:S(2)}, u32[]{:S(2)}) collective-permute-start(bf16[256,12,128]{2,0,1:T(8,128)(2,1)} %get-tuple-element.5), channel_id=1, source_target_pairs={{0,1},{1,2},{2,3},{3,0},{4,5},{5,6},{6,7},{7,4},{8,9},{9,10},{10,1... | collective-permute-start | bytes 2359304 | tf_op jit(solution)/shard_map/ppermute | solution.py:246
  13.6 3.8 %fusion.118 = (bf16[256,4,8,128]{3,0,2,1:T(8,128)(2,1)}, f32[256,4,8,128]{3,0,2,1:T(8,128)}, bf16[256,4,8,128]{3,0,2,1:T(8,128)(2,1)}) fusion(bf16[256,12,8,128]{3,0,2,1:T(8,128)(2,1)S(1)} %fusion.1), kind=kLoop, calls=%fused_computation.163 | loop fusion | flops 1048576 | bytes 14680064 | tf_op jit(solution)/shard_map/slice | solution.py:239
  17.4 7.2 %collective-permute-start.1 = (bf16[256,4,8,128]{3,0,2,1:T(8,128)(2,1)}, bf16[256,4,8,128]{3,0,2,1:T(8,128)(2,1)}, u32[]{:S(2)}, u32[]{:S(2)}) collective-permute-start(bf16[256,4,8,128]{3,0,2,1:T(8,128)(2,1)} %get-tuple-element.4), channel_id=1, source_target_pairs={{4,0},{8,4},{12,8},{16,12},{20,16},{24,20},{28,24},{32,28},{36,32}... | collective-permute-start | bytes 6291464 | tf_op jit(solution)/shard_map/ppermute | solution.py:26
  24.8 2.8 %copy-done.1 = bf16[256,12,8,128]{3,0,2,1:T(8,128)(2,1)S(1)} copy-done((bf16[256,12,8,128]{3,0,2,1:T(8,128)(2,1)S(1)}, bf16[256,12,8,128]{3,0,2,1:T(8,128)(2,1)}, u32[]{:S(2)}) %copy-start.1) | copy-done | bytes 6291480
  28.4 2.7 %collective-permute-done.3 = bf16[256,12,128]{2,0,1:T(8,128)(2,1)S(1)} collective-permute-done((bf16[256,12,128]{2,0,1:T(8,128)(2,1)}, bf16[256,12,128]{2,0,1:T(8,128)(2,1)S(1)}, u32[]{:S(2)}, u32[]{:S(2)}) %collective-permute-start.3) | collective-permute-done | bytes 786464 | tf_op jit(solution)/shard_map/ppermute | solution.py:247
  31.1 1.1 slice_bitcast_fusion.7
  32.4 7.1 %collective-permute-start.5 = (bf16[2,256,4,128]{3,1,2,0:T(8,128)(2,1)S(1)}, bf16[2,256,4,128]{3,1,2,0:T(8,128)(2,1)S(1)}, u32[]{:S(2)}, u32[]{:S(2)}) collective-permute-start(bf16[2,256,4,128]{3,1,2,0:T(8,128)(2,1)S(1)} %pad_maximum_fusion.8), channel_id=1, source_target_pairs={{4,0},{8,4},{12,8},{16,12},{20,16},{24,20},{28,24},{32,28},{36,32}... | collective-permute-start | bytes 1572872 | tf_op jit(solution)/shard_map/ppermute | solution.py:26
  39.5 1.0 slice_bitcast_fusion.2
  40.6 13.6 %collective-permute-done.4 = bf16[2,256,4,128]{3,1,2,0:T(8,128)(2,1)S(1)} collective-permute-done((bf16[2,256,4,128]{3,1,2,0:T(8,128)(2,1)S(1)}, bf16[2,256,4,128]{3,1,2,0:T(8,128)(2,1)S(1)}, u32[]{:S(2)}, u32[]{:S(2)}) %collective-permute-start.4) | collective-permute-done | bytes 524320 | tf_op jit(solution)/shard_map/ppermute | solution.py:26
  55.4 1.0 slice-done
  57.1 1.3 copy-done.2
  58.4 0.9 slice-done.2
  59.3 6.1 %fusion.7 = (bf16[256,4,8,128]{3,0,2,1:T(8,128)(2,1)S(1)}, bf16[256,4,8,128]{3,0,2,1:T(8,128)(2,1)S(1)}) fusion(f32[256,4,8,128]{3,0,2,1:T(8,128)S(1)} %slice_convert_fusion.1, bf16[256,4,8,128]{3,0,2,1:T(8,128)(2,1)S(1)} %collective-permute-done, bf16[256,6,8,128]{3,0,2,1:T(8,128)(2,1)S(1)} %concatenate.41, ...), kind=kLoop, calls=%fused_computation.15 | loop fusion | flops 35651584 | bytes 28852224 | tf_op jit(solution)/shard_map/convert_element_type | solution.py:278
  68.4 1.8 %slice_convert_fusion = f32[256,4,8,128]{3,0,2,1:T(8,128)S(1)} fusion(bf16[256,4,8,128]{3,0,2,1:T(8,128)(2,1)} %collective-permute-done.1), kind=kLoop, calls=%fused_computation.58 | loop fusion | flops 1048576 | bytes 6291456 | tf_op jit(solution)/shard_map/convert_element_type | solution.py:57
  70.3 2.1 %concatenate.47 = bf16[256,6,8,128]{3,0,2,1:T(8,128)(2,1)S(1)} pad(bf16[256,4,8,128]{3,0,2,1:T(8,128)(2,1)} %collective-permute-done.1, bf16[]{:T(256)} %constant.61.clone.1), padding=0_0x2_0x0_0x0_0 | pad | bytes 5242882 | tf_op jit(solution)/shard_map/concatenate | solution.py:269
  72.4 4.8 %fusion.19 = bf16[256,4,8,128]{3,0,2,1:T(8,128)(2,1)S(1)} fusion(f32[256,4,8,128]{3,0,2,1:T(8,128)S(1)} %slice_convert_fusion, bf16[256,4,8,128]{3,0,2,1:T(8,128)(2,1)} %collective-permute-done.1, bf16[256,6,8,128]{3,0,2,1:T(8,128)(2,1)S(1)} %concatenate.47, bf16[256,6,1,128]{3,0,2,1:T(8,128)(2,1)S(1)} %get-tuple-element.16, ...), kind=kLoop, calls=%fused_computation.27 | loop fusion | flops 17825792 | bytes 14434304 | tf_op jit(solution)/shard_map/convert_element_type | solution.py:278
  80.1 1.6 %slice.157 = bf16[256,3,8,128]{3,0,2,1:T(8,128)(2,1)S(1)} slice(bf16[256,4,8,128]{3,0,2,1:T(8,128)(2,1)} %collective-permute-done.1), slice={[0:256], [0:3], [0:8], [0:128]} | slice | bytes 3145728 | tf_op jit(solution)/shard_map/slice | solution.py:275
  86.2 2.2 %fusion.50 = f32[1,256,256]{2,1,0:T(8,128)S(1)} fusion(bf16[256,3,8,128]{3,0,2,1:T(8,128)(2,1)S(1)} %slice.155, bf16[256,4,8,128]{3,0,2,1:T(8,128)(2,1)} %collective-permute-done.1), kind=kOutput, calls=%fused_computation.67 | convolution fusion | flops 402653184 | bytes 3407872 | tf_op jit(solution)/shard_map/dot_general | solution.py:72
  88.4 2.2 %convolution_bitcast_fusion.2 = f32[1,256,256]{2,1,0:T(8,128)S(1)} fusion(bf16[256,12,8,128]{3,0,2,1:T(8,128)(2,1)S(1)} %bitcast.193, bf16[256,4,8,128]{3,0,2,1:T(8,128)(2,1)} %collective-permute-done.1), kind=kOutput, calls=%fused_computation.77 | convolution fusion | flops 402653184 | bytes 3932160 | tf_op jit(solution)/shard_map/dot_general | solution.py:72
  92.0 47.7 %shard_map.77 = f32[2,5,64,256]{3,2,1,0:T(8,128)S(1)} custom-call(f32[3,2,3,256,256]{4,3,2,1,0:T(8,128)S(1)} %pad_maximum_fusion.x_ref), custom_call_target="tpu_custom_call" | custom-call | tf_op jit(solution)/shard_map/pallas_call | solution.py:197
  139.6 1.1 bitcast_multiply_fusion
  (63 shorter events, 17.0 us)
Async XLA Ops:
  8.9 8.6 %copy-start = (bf16[256,12,8,128]{3,0,2,1:T(8,128)(2,1)}, bf16[256,12,8,128]{3,0,2,1:T(8,128)(2,1)S(1)}, u32[]{:S(2)}) copy-start(bf16[256,12,8,128]{3,0,2,1:T(8,128)(2,1)S(1)} %fusion.1) | copy-start | bytes 18874372
  10.4 20.7 %collective-permute-start.3 = (bf16[256,12,128]{2,0,1:T(8,128)(2,1)}, bf16[256,12,128]{2,0,1:T(8,128)(2,1)S(1)}, u32[]{:S(2)}, u32[]{:S(2)}) collective-permute-start(bf16[256,12,128]{2,0,1:T(8,128)(2,1)} %get-tuple-element.6), channel_id=1, source_target_pairs={{1,0},{2,1},{3,2},{0,3},{5,4},{6,5},{7,6},{4,7},{9,8},{10,9},{11,1... | collective-permute-start | bytes 2359304 | tf_op jit(solution)/shard_map/ppermute | solution.py:247
  11.2 13.4 %copy-start.4 = (s32[2,5,2]{1,2,0:T(2,128)S(1)}, s32[2,5,2]{1,2,0:T(2,128)}, u32[]{:S(2)}) copy-start(s32[2,5,2]{1,2,0:T(2,128)} %param.11) | copy-start | bytes 244
  11.2 19.9 %collective-permute-start.2 = (bf16[256,12,128]{2,0,1:T(8,128)(2,1)}, bf16[256,12,128]{2,0,1:T(8,128)(2,1)}, u32[]{:S(2)}, u32[]{:S(2)}) collective-permute-start(bf16[256,12,128]{2,0,1:T(8,128)(2,1)} %get-tuple-element.5), channel_id=1, source_target_pairs={{0,1},{1,2},{2,3},{3,0},{4,5},{5,6},{6,7},{7,4},{8,9},{9,10},{10,1... | collective-permute-start | bytes 2359304 | tf_op jit(solution)/shard_map/ppermute | solution.py:246
  17.4 36.9 %collective-permute-start = (bf16[256,4,8,128]{3,0,2,1:T(8,128)(2,1)}, bf16[256,4,8,128]{3,0,2,1:T(8,128)(2,1)S(1)}, u32[]{:S(2)}, u32[]{:S(2)}) collective-permute-start(bf16[256,4,8,128]{3,0,2,1:T(8,128)(2,1)} %get-tuple-element.2), channel_id=1, source_target_pairs={{252,0},{0,4},{4,8},{8,12},{12,16},{16,20},{20,24},{24,28},{28,32}... | collective-permute-start | bytes 6291464 | tf_op jit(solution)/shard_map/ppermute | solution.py:26
  17.4 51.0 %collective-permute-start.1 = (bf16[256,4,8,128]{3,0,2,1:T(8,128)(2,1)}, bf16[256,4,8,128]{3,0,2,1:T(8,128)(2,1)}, u32[]{:S(2)}, u32[]{:S(2)}) collective-permute-start(bf16[256,4,8,128]{3,0,2,1:T(8,128)(2,1)} %get-tuple-element.4), channel_id=1, source_target_pairs={{4,0},{8,4},{12,8},{16,12},{20,16},{24,20},{28,24},{32,28},{36,32}... | collective-permute-start | bytes 6291464 | tf_op jit(solution)/shard_map/ppermute | solution.py:26
  24.8 2.8 %copy-start.1 = (bf16[256,12,8,128]{3,0,2,1:T(8,128)(2,1)S(1)}, bf16[256,12,8,128]{3,0,2,1:T(8,128)(2,1)}, u32[]{:S(2)}) copy-start(bf16[256,12,8,128]{3,0,2,1:T(8,128)(2,1)} %copy-done) | copy-start | bytes 18874372
  32.2 21.9 %collective-permute-start.4 = (bf16[2,256,4,128]{3,1,2,0:T(8,128)(2,1)S(1)}, bf16[2,256,4,128]{3,1,2,0:T(8,128)(2,1)S(1)}, u32[]{:S(2)}, u32[]{:S(2)}) collective-permute-start(bf16[2,256,4,128]{3,1,2,0:T(8,128)(2,1)S(1)} %pad_maximum_fusion.7), channel_id=1, source_target_pairs={{252,0},{0,4},{4,8},{8,12},{12,16},{16,20},{20,24},{24,28},{28,32}... | collective-permute-start | bytes 1572872 | tf_op jit(solution)/shard_map/ppermute | solution.py:26
  32.4 21.8 %collective-permute-start.5 = (bf16[2,256,4,128]{3,1,2,0:T(8,128)(2,1)S(1)}, bf16[2,256,4,128]{3,1,2,0:T(8,128)(2,1)S(1)}, u32[]{:S(2)}, u32[]{:S(2)}) collective-permute-start(bf16[2,256,4,128]{3,1,2,0:T(8,128)(2,1)S(1)} %pad_maximum_fusion.8), channel_id=1, source_target_pairs={{4,0},{8,4},{12,8},{16,12},{20,16},{24,20},{28,24},{32,28},{36,32}... | collective-permute-start | bytes 1572872 | tf_op jit(solution)/shard_map/ppermute | solution.py:26
  54.1 2.2 %slice-start = ((s8[6291456]{0:T(1024)(128)(4,1)}), s8[4194304]{0:T(1024)(128)(4,1)S(1)}, s32[]{:S(2)}) async-start(s8[6291456]{0:T(1024)(128)(4,1)} %bitcast.192), calls=%async_computation | async-start | bytes 8388608
  54.3 2.7 %slice-start.1 = ((s8[6291456]{0:T(1024)(128)(4,1)}), s8[2097152]{0:T(1024)(128)(4,1)S(1)}, s32[]{:S(2)}) async-start(s8[6291456]{0:T(1024)(128)(4,1)} %bitcast.192), calls=%async_computation.1 | async-start | bytes 4194304
  54.8 3.6 %copy-start.2 = (f32[256,4,8,128]{3,0,2,1:T(8,128)S(1)}, f32[256,4,8,128]{3,0,2,1:T(8,128)}, u32[]{:S(2)}) copy-start(f32[256,4,8,128]{3,0,2,1:T(8,128)} %get-tuple-element.3) | copy-start | bytes 12582916
  54.9 4.4 %slice-start.2 = ((bf16[256,12,8,128]{3,0,2,1:T(8,128)(2,1)}), bf16[256,6,8,128]{3,0,2,1:T(8,128)(2,1)S(1)}, s32[]{:S(2)}) async-start(bf16[256,12,8,128]{3,0,2,1:T(8,128)(2,1)} %copy-done), calls=%async_computation.2 | async-start | bytes 6291456 | tf_op jit(solution)/shard_map/slice | solution.py:261
  54.9 4.4 %copy-start.3 = (f32[4,8,128]{2,1,0:T(8,128)S(1)}, f32[4,8,128]{2,1,0:T(8,128)}, u32[]{:S(2)}) copy-start(f32[4,8,128]{2,1,0:T(8,128)} %param.7) | copy-start | bytes 49156

commit v6 on v5

--- a/solution.py
+++ b/solution.py
@@ -216,6 +216,53 @@
     )(full)
 
 
+def swap_kernel(domains, up_piece, down_piece, from_left, from_right, landed, send_sems, recv_sems):
+    me = lax.axis_index("mat")
+    dom = lax.axis_index("dom")
+    up = lax.rem(dom + 1, domains)
+    down = lax.rem(dom + domains - 1, domains)
+    mesh_ids = pl.DeviceIdType.MESH
+    barrier = pltpu.get_barrier_semaphore()
+    for device in ((down, me), (up, me)):
+        pl.semaphore_signal(barrier, 1, device_id=device, device_id_type=mesh_ids)
+    pl.semaphore_wait(barrier, 2)
+    copies = []
+    for index, (source, target) in enumerate(((up_piece, up), (down_piece, down))):
+        copy = pltpu.make_async_remote_copy(
+            src_ref=source,
+            dst_ref=landed.at[index],
+            send_sem=send_sems.at[index],
+            recv_sem=recv_sems.at[index],
+            device_id=(target, me),
+            device_id_type=mesh_ids,
+        )
+        copy.start()
+        copies.append(copy)
+    for copy in copies:
+        copy.wait()
+    from_left[...] = landed[0]
+    from_right[...] = landed[1]
+
+
+def swap_pieces(up_piece, down_piece):
+    domains = lax.axis_size("dom")
+    piece = jax.ShapeDtypeStruct(up_piece.shape, up_piece.dtype)
+    return pl.pallas_call(
+        functools.partial(swap_kernel, domains),
+        out_shape=(piece, piece),
+        in_specs=[pl.BlockSpec(memory_space=pltpu.VMEM)] * 2,
+        out_specs=(pl.BlockSpec(memory_space=pltpu.VMEM),) * 2,
+        scratch_shapes=[
+            pltpu.VMEM((2,) + up_piece.shape, up_piece.dtype),
+            pltpu.SemaphoreType.DMA((2,)),
+            pltpu.SemaphoreType.DMA((2,)),
+        ],
+        compiler_params=pltpu.CompilerParams(
+            collective_id=1, has_side_effects=True, vmem_limit_bytes=48 * 1024 * 1024
+        ),
+    )(up_piece, down_piece)
+
+
 def on_device(orbitals, potential, centre_first, centre_second, centre_third, correlation_pairs):
     block_orbs, window_cells, second_cells, third_cells = orbitals.shape
     patch_cells = potential.shape[0]
@@ -238,8 +285,7 @@
     upper_start = 2 * patch_cells
     to_right = masked[:, upper_start - 1 : window_cells - 1]
     to_left = masked[:, 1 : patch_cells + 1]
-    from_left = passed_along(to_right, "dom", 1)
-    from_right = passed_along(to_left, "dom", -1)
+    from_left, from_right = swap_pieces(to_right, to_left)
     mat_size = lax.axis_size("mat")
     up = [(i, (i + 1) % mat_size) for i in range(mat_size)]
     down = [(j, i) for i, j in up]

time: 142 us -> 188 us (1.32)
  Pallas kernels: 47.7 us -> 82.5 us
  waiting for transfers between devices: 16.3 us -> 1.67 us
  other arithmetic: 26.3 us -> 40.2 us
  matrix products: 17 us -> 29.5 us
  local copies, waits for them, and re-layouts: 14.7 us -> 24.8 us
  starting transfers between devices: 17.6 us -> 7.56 us
    pallas_call x0 -> x1, Pallas kernels: none -> 35.2 us  [swap_pieces(): pl.pallas_call(functools.partial(swap_kernel, domains), out_shape=(piece,...]
    dot_general x18, matrix products: 15.7 us -> 28.3 us  [pair_product(): lax.dot_general(left, right, (((1, 2, 3), (1, 2, 3)), ((), ())), preferre...]
    ppermute x4 -> x2, waiting for transfers between devices: 13.6 us -> 1.66 us  [passed_along(): return lax.ppermute(block, axis, route)]
    convert_element_type x2, other arithmetic: 10.9 us -> 22.3 us  [on_device(): stencil(ext, potential).astype(jnp.bfloat16)]
    ppermute x4 -> x2, starting transfers between devices: 14.4 us -> 5.35 us  [passed_along(): return lax.ppermute(block, axis, route)]
    slice x0 -> x3, local copies, waits for them, and re-layouts: none -> 4.24 us  [the longest x2 3.17 us: on_device(): row_above = lax.ppermute(masked[:, :, second_cells - 1], 'mat', up)]
    another operation x1 -> x4, local copies, waits for them, and re-layouts: 1.02 us -> 4.84 us  [with_rows(): rows[0][:, :, None]]
    another operation x3 -> x6, local copies, waits for them, and re-layouts: 0.17 us -> 3.9 us  [with_rows(): rows[1][:, :, None]]
  transfers between devices with their start and end apart: 6 -> 4, of which waited for: 2 -> 1; matrix products, arithmetic and copies ran while one was open for 12% -> 34% of each run, Pallas kernels for 0% -> 19%
where the time goes in v6:
time: 188 us
  Pallas kernels  82.5 us (44%)
  other arithmetic  40.2 us (21%)
  matrix products  29.5 us (16%)
  local copies, waits for them, and re-layouts  24.8 us (13%)
  starting transfers between devices  7.56 us (4%)
    pallas_call x1, Pallas kernels, exchange_and_sum(): pl.pallas_call(functools.partial(exchange_kernel, count, domains, share,...  47.3 us
    pallas_call x1, Pallas kernels, swap_pieces(): pl.pallas_call(functools.partial(swap_kernel, domains), out_shape=(piece,...  35.2 us
    dot_general x18, matrix products, pair_product(): lax.dot_general(left, right, (((1, 2, 3), (1, 2, 3)), ((), ())), preferre...  28.3 us
    convert_element_type x2, other arithmetic, on_device(): stencil(ext, potential).astype(jnp.bfloat16)  22.3 us
    select_n x1, other arithmetic, on_device(): masked = jnp.where(inside, orbitals, jnp.zeros_like(orbitals))  5.69 us
    unnamed x60, local copies, waits for them, and re-layouts  5.58 us
    ppermute x2, starting transfers between devices, passed_along(): return lax.ppermute(block, axis, route)  5.35 us
    another operation x4, local copies, waits for them, and re-layouts, with_rows(): rows[0][:, :, None]  4.84 us
  transfers between devices with their start and end apart: 4, of which 1 were waited for; matrix products, arithmetic and copies ran while one was open for 34% of the time, Pallas kernels for 19%

profile of v6, /device:TPU:6, one launch (start us, length us, event | category | flops | bytes accessed | tf_op | source)
XLA Modules:
  0.0 187.5 jit_solution(1112359234825913109)
XLA Ops:
  3.7 5.7 %fusion.1 = bf16[256,12,8,128]{3,2,1,0:T(8,128)(2,1)S(1)} fusion(bf16[256,12,8,128]{3,2,1,0:T(8,128)(2,1)} %param.6, s32[256,128]{1,0:T(8,128)S(1)} %subtract_multiply_fusion, s32[256,12,8]{2,1,0:T(8,128)S(1)} %broadcast_add_fusion, pred[12]{0:T(512)(128)(4,1)S(1)} %compare_and_fusion), kind=kLoop, calls=%fused_computation.2 | loop fusion | flops 12582912 | bytes 12812300 | tf_op jit(solution)/shard_map/jit(_where)/select_n | solution.py:284
  9.4 2.1 %fusion.155 = (bf16[256,12,1,128]{3,2,1,0:T(2,128)(2,1)S(1)}, bf16[256,12,1,128]{3,2,1,0:T(2,128)(2,1)S(1)}) fusion(bf16[256,12,8,128]{3,2,1,0:T(8,128)(2,1)S(1)} %fusion.1), kind=kLoop, calls=%fused_computation.179 | loop fusion | bytes 3145728 | tf_op jit(solution)/shard_map/slice | solution.py:292
  12.6 2.2 %collective-permute-start = (bf16[256,12,128]{2,0,1:T(8,128)(2,1)}, bf16[256,12,128]{2,0,1:T(8,128)(2,1)S(1)}, u32[]{:S(2)}, u32[]{:S(2)}) collective-permute-start(bf16[256,12,128]{2,0,1:T(8,128)(2,1)} %bitcast.167), channel_id=1, source_target_pairs={{0,1},{1,2},{2,3},{3,0},{4,5},{5,6},{6,7},{7,4},{8,9},{9,10},{10,1... | collective-permute-start | bytes 2359304 | tf_op jit(solution)/shard_map/ppermute | solution.py:292
  15.8 3.9 %fusion.154 = (bf16[256,4,8,128]{3,2,1,0:T(8,128)(2,1)S(1)}, f32[256,4,8,128]{3,2,1,0:T(8,128)}, bf16[256,4,8,128]{3,2,1,0:T(8,128)(2,1)}, bf16[256,4,8,128]{3,2,1,0:T(8,128)(2,1)}) fusion(bf16[256,12,8,128]{3,2,1,0:T(8,128)(2,1)S(1)} %fusion.1), kind=kLoop, calls=%fused_computation.178 | loop fusion | flops 1048576 | bytes 16777216 | tf_op jit(solution)/shard_map/slice | solution.py:320
  19.8 35.2 %shard_map.77 = (bf16[256,4,8,128]{3,2,1,0:T(8,128)(2,1)S(1)}, bf16[256,4,8,128]{3,2,1,0:T(8,128)(2,1)S(1)}) custom-call(bf16[256,4,8,128]{3,2,1,0:T(8,128)(2,1)} %get-tuple-element.9.up_piece, bf16[256,4,8,128]{3,2,1,0:T(8,128)(2,1)} %get-tuple-element.8.down_piece), custom_call_target="tpu_custom_call" | custom-call | tf_op jit(solution)/shard_map/pallas_call | solution.py:250
  55.0 2.7 %slice_convert_fusion.1 = f32[256,4,8,128]{3,2,1,0:T(8,128)} fusion(bf16[256,4,8,128]{3,2,1,0:T(8,128)(2,1)S(1)} %get-tuple-element.4), kind=kLoop, calls=%fused_computation.59 | loop fusion | flops 1048576 | bytes 6291456 | tf_op jit(solution)/shard_map/convert_element_type | solution.py:57
  58.0 2.1 %concatenate.41 = bf16[256,6,8,128]{3,2,1,0:T(8,128)(2,1)} pad(bf16[256,4,8,128]{3,2,1,0:T(8,128)(2,1)S(1)} %get-tuple-element.4, bf16[]{:T(256)} %constant.61.clone.1), padding=0_0x0_2x0_0x0_0 | pad | bytes 5242882 | tf_op jit(solution)/shard_map/concatenate | solution.py:311
  60.2 2.2 %concatenate.47 = bf16[256,6,8,128]{3,2,1,0:T(8,128)(2,1)} pad(bf16[256,4,8,128]{3,2,1,0:T(8,128)(2,1)S(1)} %get-tuple-element.5, bf16[]{:T(256)} %constant.61.clone.1), padding=0_0x2_0x0_0x0_0 | pad | bytes 5242882 | tf_op jit(solution)/shard_map/concatenate | solution.py:315
  64.3 1.4 fusion.71
  65.8 1.5 fusion.68
  67.3 1.5 convolution_bitcast_fusion.1
  68.8 1.9 %convolution_bitcast_fusion.3 = f32[1,256,256]{2,1,0:T(8,128)} fusion(bf16[256,4,8,128]{3,2,1,0:T(8,128)(2,1)S(1)} %get-tuple-element.6), kind=kOutput, calls=%fused_computation.93 | convolution fusion | flops 536870912 | bytes 2359296 | tf_op jit(solution)/shard_map/dot_general | solution.py:72
  72.5 1.5 fusion.102
  74.2 3.3 %fusion.105 = f32[1,256,256]{2,1,0:T(8,128)} fusion(bf16[256,3,8,128]{3,0,2,1:T(8,128)(2,1)} %copy-done.11), kind=kOutput, calls=%fused_computation.89 | convolution fusion | flops 402653184 | bytes 1835008 | tf_op jit(solution)/shard_map/dot_general | solution.py:72
  79.0 3.4 %convolution_bitcast_fusion.2 = f32[1,256,256]{2,1,0:T(8,128)} fusion(bf16[256,4,8,128]{3,2,1,0:T(8,128)(2,1)} %copy-done.9, bf16[256,3,8,128]{3,2,1,0:T(8,128)(2,1)S(1)} %copy-done.6), kind=kOutput, calls=%fused_computation.92 | convolution fusion | flops 402653184 | bytes 3932160 | tf_op jit(solution)/shard_map/dot_general | solution.py:72
  87.1 1.5 copy.399
  89.5 5.0 %collective-permute-start.3 = (bf16[2,256,4,128]{3,1,2,0:T(8,128)(2,1)}, bf16[2,256,4,128]{3,1,2,0:T(8,128)(2,1)S(1)}, u32[]{:S(2)}, u32[]{:S(2)}) collective-permute-start(bf16[2,256,4,128]{3,1,2,0:T(8,128)(2,1)} %pad_maximum_fusion.8), channel_id=1, source_target_pairs={{4,0},{8,4},{12,8},{16,12},{20,16},{24,20},{28,24},{32,28},{36,32}... | collective-permute-start | bytes 1572872 | tf_op jit(solution)/shard_map/ppermute | solution.py:26
  94.5 1.7 collective-permute-done.2
  96.2 1.5 copy.394
  97.8 1.6 copy.395
  99.4 17.9 %fusion.7 = (bf16[256,4,8,128]{3,2,1,0:T(8,128)(2,1)}, bf16[256,4,8,128]{3,2,1,0:T(8,128)(2,1)}) fusion(f32[256,4,8,128]{3,2,1,0:T(8,128)} %slice_convert_fusion.1, bf16[256,4,8,128]{3,2,1,0:T(8,128)(2,1)S(1)} %get-tuple-element.4, bf16[256,6,8,128]{3,2,1,0:T(8,128)(2,1)S(1)} %copy-done.3, bf16[256,6,1,128]{3,2,1,0:T(2,128)(2,1)} %copy.395, ...), kind=kLoop, calls=%fused_computation.15 | loop fusion | flops 44040192 | bytes 29245440 | tf_op jit(solution)/shard_map/convert_element_type | solution.py:324
  117.3 3.0 %fusion.74 = f32[1,256,256]{2,1,0:T(8,128)S(1)} fusion(bf16[256,3,8,128]{3,0,2,1:T(8,128)(2,1)} %copy-done.13, bf16[256,4,8,128]{3,2,1,0:T(8,128)(2,1)} %get-tuple-element.22), kind=kOutput, calls=%fused_computation.82 | convolution fusion | flops 536870912 | bytes 3932160 | tf_op jit(solution)/shard_map/dot_general | solution.py:72
  126.6 4.4 %fusion.19 = bf16[256,4,8,128]{3,2,1,0:T(8,128)(2,1)S(1)} fusion(f32[256,4,8,128]{3,2,1,0:T(8,128)S(1)} %slice_convert_fusion, bf16[256,4,8,128]{3,2,1,0:T(8,128)(2,1)S(1)} %copy-done.1, bf16[256,6,8,128]{3,2,1,0:T(8,128)(2,1)S(1)} %copy-done.4, bf16[256,6,1,128]{3,2,1,0:T(2,128)(2,1)S(1)} %copy.403, bf16[256,6,1,128]{3,2,1,0:T(2,128)(2,1)S(1)} %copy.402, ...), kind=kLoop, calls=%fused_computation.27 | loop fusion | flops 22020096 | bytes 15220736 | tf_op jit(solution)/shard_map/convert_element_type | solution.py:324
  139.1 47.3 %shard_map.78 = f32[2,5,64,256]{3,2,1,0:T(8,128)S(1)} custom-call(f32[3,2,3,256,256]{4,3,2,1,0:T(8,128)S(1)} %pad_maximum_fusion.x_ref), custom_call_target="tpu_custom_call" | custom-call | tf_op jit(solution)/shard_map/pallas_call | solution.py:197
  (112 shorter events, 31.6 us)
Async XLA Ops:
  9.4 10.4 %copy-start.2 = (bf16[256,12,8,128]{3,2,1,0:T(8,128)(2,1)}, bf16[256,12,8,128]{3,2,1,0:T(8,128)(2,1)S(1)}, u32[]{:S(2)}) copy-start(bf16[256,12,8,128]{3,2,1,0:T(8,128)(2,1)S(1)} %fusion.1) | copy-start | bytes 18874372
  12.6 69.9 %collective-permute-start = (bf16[256,12,128]{2,0,1:T(8,128)(2,1)}, bf16[256,12,128]{2,0,1:T(8,128)(2,1)S(1)}, u32[]{:S(2)}, u32[]{:S(2)}) collective-permute-start(bf16[256,12,128]{2,0,1:T(8,128)(2,1)} %bitcast.167), channel_id=1, source_target_pairs={{0,1},{1,2},{2,3},{3,0},{4,5},{5,6},{6,7},{7,4},{8,9},{9,10},{10,1... | collective-permute-start | bytes 2359304 | tf_op jit(solution)/shard_map/ppermute | solution.py:292
  15.8 66.6 %collective-permute-start.1 = (bf16[256,12,128]{2,0,1:T(8,128)(2,1)}, bf16[256,12,128]{2,0,1:T(8,128)(2,1)}, u32[]{:S(2)}, u32[]{:S(2)}) collective-permute-start(bf16[256,12,128]{2,0,1:T(8,128)(2,1)} %bitcast.166), channel_id=1, source_target_pairs={{1,0},{2,1},{3,2},{0,3},{5,4},{6,5},{7,6},{4,7},{9,8},{10,9},{11,1... | collective-permute-start | bytes 2359304 | tf_op jit(solution)/shard_map/ppermute | solution.py:293
  19.8 52.7 %copy-start.9 = (bf16[256,4,8,128]{3,2,1,0:T(8,128)(2,1)}, bf16[256,4,8,128]{3,2,1,0:T(8,128)(2,1)S(1)}, u32[]{:S(2)}) copy-start(bf16[256,4,8,128]{3,2,1,0:T(8,128)(2,1)S(1)} %get-tuple-element.6) | copy-start | bytes 6291460
  55.0 7.3 %copy-start = (bf16[256,4,8,128]{3,2,1,0:T(8,128)(2,1)}, bf16[256,4,8,128]{3,2,1,0:T(8,128)(2,1)S(1)}, u32[]{:S(2)}) copy-start(bf16[256,4,8,128]{3,2,1,0:T(8,128)(2,1)S(1)} %get-tuple-element.5) | copy-start | bytes 6291460
  58.0 13.1 %copy-start.5 = (bf16[256,3,8,128]{3,2,1,0:T(8,128)(2,1)}, bf16[256,3,8,128]{3,2,1,0:T(8,128)(2,1)S(1)}, u32[]{:S(2)}) copy-start(bf16[256,3,8,128]{3,2,1,0:T(8,128)(2,1)S(1)} %slice.120) | copy-start | bytes 4718596
  62.9 2.9 %copy-start.13 = (bf16[256,3,8,128]{3,0,2,1:T(8,128)(2,1)}, bf16[256,3,8,128]{3,0,2,1:T(8,128)(2,1)S(1)}, u32[]{:S(2)}) copy-start(bf16[256,3,8,128]{3,0,2,1:T(8,128)(2,1)S(1)} %copy.449) | copy-start | bytes 4718596
  71.1 2.9 %copy-start.11 = (bf16[256,3,8,128]{3,0,2,1:T(8,128)(2,1)}, bf16[256,3,8,128]{3,0,2,1:T(8,128)(2,1)S(1)}, u32[]{:S(2)}) copy-start(bf16[256,3,8,128]{3,0,2,1:T(8,128)(2,1)S(1)} %copy.450) | copy-start | bytes 4718596
  72.5 1.5 copy-start.26
  74.0 3.6 %copy-start.1 = (bf16[256,4,8,128]{3,2,1,0:T(8,128)(2,1)S(1)}, bf16[256,4,8,128]{3,2,1,0:T(8,128)(2,1)}, u32[]{:S(2)}) copy-start(bf16[256,4,8,128]{3,2,1,0:T(8,128)(2,1)} %copy-done) | copy-start | bytes 6291460
  77.6 21.7 %slice-start = ((s8[6291456]{0:T(1024)(128)(4,1)}), s8[4194304]{0:T(1024)(128)(4,1)S(1)}, s32[]{:S(2)}) async-start(s8[6291456]{0:T(1024)(128)(4,1)} %bitcast.168), calls=%async_computation | async-start | bytes 8388608
  82.4 16.9 %slice-start.1 = ((s8[6291456]{0:T(1024)(128)(4,1)}), s8[2097152]{0:T(1024)(128)(4,1)S(1)}, s32[]{:S(2)}) async-start(s8[6291456]{0:T(1024)(128)(4,1)} %bitcast.168), calls=%async_computation.1 | async-start | bytes 4194304
  82.4 1.8 copy-start.15
  83.9 12.2 %collective-permute-start.2 = (bf16[2,256,4,128]{3,1,2,0:T(8,128)(2,1)S(1)}, bf16[2,256,4,128]{3,1,2,0:T(8,128)(2,1)S(1)}, u32[]{:S(2)}, u32[]{:S(2)}) collective-permute-start(bf16[2,256,4,128]{3,1,2,0:T(8,128)(2,1)S(1)} %pad_maximum_fusion.7), channel_id=1, source_target_pairs={{252,0},{0,4},{4,8},{8,12},{12,16},{16,20},{20,24},{24,28},{28,32}... | collective-permute-start | bytes 1572872 | tf_op jit(solution)/shard_map/ppermute | solution.py:26
  85.9 13.4 %copy-start.3 = (bf16[256,6,8,128]{3,2,1,0:T(8,128)(2,1)S(1)}, bf16[256,6,8,128]{3,2,1,0:T(8,128)(2,1)}, u32[]{:S(2)}) copy-start(bf16[256,6,8,128]{3,2,1,0:T(8,128)(2,1)} %concatenate.41) | copy-start | bytes 9437188
  89.5 9.9 %slice-start.2 = ((bf16[256,12,8,128]{3,2,1,0:T(8,128)(2,1)}), bf16[256,6,8,128]{3,2,1,0:T(8,128)(2,1)S(1)}, s32[]{:S(2)}) async-start(bf16[256,12,8,128]{3,2,1,0:T(8,128)(2,1)} %copy-done.2), calls=%async_computation.2 | async-start | bytes 6291456 | tf_op jit(solution)/shard_map/slice | solution.py:307
  89.5 9.9 %copy-start.25 = (f32[4,8,128]{2,1,0:T(8,128)S(1)}, f32[4,8,128]{2,1,0:T(8,128)}, u32[]{:S(2)}) copy-start(f32[4,8,128]{2,1,0:T(8,128)} %param.7) | copy-start | bytes 49156
  89.5 35.2 %collective-permute-start.3 = (bf16[2,256,4,128]{3,1,2,0:T(8,128)(2,1)}, bf16[2,256,4,128]{3,1,2,0:T(8,128)(2,1)S(1)}, u32[]{:S(2)}, u32[]{:S(2)}) collective-permute-start(bf16[2,256,4,128]{3,1,2,0:T(8,128)(2,1)} %pad_maximum_fusion.8), channel_id=1, source_target_pairs={{4,0},{8,4},{12,8},{16,12},{20,16},{24,20},{28,24},{32,28},{36,32}... | collective-permute-start | bytes 1572872 | tf_op jit(solution)/shard_map/ppermute | solution.py:26
  117.3 3.0 %copy-start.8 = (bf16[256,4,8,128]{3,2,1,0:T(8,128)(2,1)S(1)}, bf16[256,4,8,128]{3,2,1,0:T(8,128)(2,1)}, u32[]{:S(2)}) copy-start(bf16[256,4,8,128]{3,2,1,0:T(8,128)(2,1)} %get-tuple-element.22) | copy-start | bytes 6291460
  117.3 3.3 %copy-start.10 = (bf16[256,4,8,128]{3,2,1,0:T(8,128)(2,1)S(1)}, bf16[256,4,8,128]{3,2,1,0:T(8,128)(2,1)}, u32[]{:S(2)}) copy-start(bf16[256,4,8,128]{3,2,1,0:T(8,128)(2,1)} %copy-done.9) | copy-start | bytes 6291460
  120.6 1.6 copy-start.7
  120.6 2.0 %copy-start.14 = (bf16[256,3,8,128]{3,0,2,1:T(8,128)(2,1)S(1)}, bf16[256,3,8,128]{3,0,2,1:T(8,128)(2,1)}, u32[]{:S(2)}) copy-start(bf16[256,3,8,128]{3,0,2,1:T(8,128)(2,1)} %copy-done.13) | copy-start | bytes 4718596
  124.7 1.9 %copy-start.4 = (bf16[256,6,8,128]{3,2,1,0:T(8,128)(2,1)S(1)}, bf16[256,6,8,128]{3,2,1,0:T(8,128)(2,1)}, u32[]{:S(2)}) copy-start(bf16[256,6,8,128]{3,2,1,0:T(8,128)(2,1)} %concatenate.47) | copy-start | bytes 9437188
  131.8 1.4 copy-start.12
  (10 other events, 10.6 us)

commit v7 on v5

--- a/solution.py
+++ b/solution.py
@@ -245,12 +245,11 @@
     down = [(j, i) for i, j in up]
     row_above = lax.ppermute(masked[:, :, second_cells - 1], "mat", up)
     row_below = lax.ppermute(masked[:, :, 0], "mat", down)
-    rows_right = jnp.stack(
-        [row_above[:, upper_start - 1 : window_cells - 1], row_below[:, upper_start - 1 : window_cells - 1]]
-    )
-    rows_left = jnp.stack([row_above[:, 1 : patch_cells + 1], row_below[:, 1 : patch_cells + 1]])
-    rows_from_left = passed_along(rows_right, "dom", 1)
-    rows_from_right = passed_along(rows_left, "dom", -1)
+    arrived = jnp.stack([from_left, from_right])
+    arrived_above = lax.ppermute(arrived[:, :, :, second_cells - 1], "mat", up)
+    arrived_below = lax.ppermute(arrived[:, :, :, 0], "mat", down)
+    rows_from_left = jnp.stack([arrived_above[0], arrived_below[0]])
+    rows_from_right = jnp.stack([arrived_above[1], arrived_below[1]])
 
     def with_rows(planes, rows):
         return jnp.concatenate([rows[0][:, :, None], planes, rows[1][:, :, None]], axis=2)

time: 142 us -> 141 us (level)
  starting transfers between devices: 17.6 us -> 11.9 us
  other arithmetic: 26.3 us -> 30.6 us
  matrix products: 17 us -> 19.2 us
    ppermute x1, waiting for transfers between devices: 0.01 us -> 8.26 us  [on_device(): row_above = lax.ppermute(masked[:, :, second_cells - 1], 'mat', up)]
    ppermute x4 -> x2, waiting for transfers between devices: 13.6 us -> 6.39 us  [passed_along(): return lax.ppermute(block, axis, route)]
    ppermute x4 -> x2, starting transfers between devices: 14.4 us -> 7.75 us  [passed_along(): return lax.ppermute(block, axis, route)]
    convert_element_type x2 -> x3, other arithmetic: 2.24 us -> 8.43 us  [stencil(): centre_cells = extended[:, 1:-1, 1:-1, :].astype(jnp.float32)]
    slice x1 -> x0, other arithmetic: 3.82 us -> none  [on_device(): to_right = masked[:, upper_start - 1:window_cells - 1]]
    ppermute x1, waiting for transfers between devices: 2.69 us -> 0.39 us  [on_device(): row_below = lax.ppermute(masked[:, :, 0], 'mat', down)]
    dot_general x18, matrix products: 15.7 us -> 17.9 us  [pair_product(): lax.dot_general(left, right, (((1, 2, 3), (1, 2, 3)), ((), ())), preferre...]
    ppermute x0 -> x2, starting transfers between devices: none -> 2.1 us  [the longest x1 1.54 us: on_device(): arrived_below = lax.ppermute(arrived[:, :, :, 0], 'mat', down)]
  transfers between devices with their start and end apart: 6 -> 6, of which waited for: 2 -> 3; matrix products, arithmetic and copies ran while one was open for 12% -> 13% of each run, Pallas kernels for 0% -> 0%
where the time goes in v7:
time: 141 us
  Pallas kernels  47.4 us (34%)
  other arithmetic  30.6 us (22%)
  matrix products  19.2 us (14%)
  local copies, waits for them, and re-layouts  15.4 us (11%)
  waiting for transfers between devices  15 us (11%)
  starting transfers between devices  11.9 us (8%)
    pallas_call x1, Pallas kernels, exchange_and_sum(): pl.pallas_call(functools.partial(exchange_kernel, count, domains, share,...  47.4 us
    dot_general x18, matrix products, pair_product(): lax.dot_general(left, right, (((1, 2, 3), (1, 2, 3)), ((), ())), preferre...  17.9 us
    convert_element_type x2, other arithmetic, on_device(): stencil(ext, potential).astype(jnp.bfloat16)  11.6 us
    convert_element_type x3, other arithmetic, stencil(): centre_cells = extended[:, 1:-1, 1:-1, :].astype(jnp.float32)  8.43 us
    ppermute x1, waiting for transfers between devices, on_device(): row_above = lax.ppermute(masked[:, :, second_cells - 1], 'mat', up)  8.26 us
    ppermute x2, starting transfers between devices, passed_along(): return lax.ppermute(block, axis, route)  7.75 us
    ppermute x2, waiting for transfers between devices, passed_along(): return lax.ppermute(block, axis, route)  6.39 us
    unnamed x28, local copies, waits for them, and re-layouts  6.14 us
  transfers between devices with their start and end apart: 6, of which 3 were waited for; matrix products, arithmetic and copies ran while one was open for 13% of the time, Pallas kernels for 0%

profile of v7, /device:TPU:6, one launch (start us, length us, event | category | flops | bytes accessed | tf_op | source)
XLA Modules:
  0.0 140.6 jit_solution(7123961991308096205)
XLA Ops:
  2.9 5.9 %fusion.1 = bf16[256,12,8,128]{3,0,2,1:T(8,128)(2,1)S(1)} fusion(bf16[256,12,8,128]{3,2,1,0:T(8,128)(2,1)} %param.6, s32[256,128]{1,0:T(8,128)S(1)} %subtract_multiply_fusion, s32[256,12,8]{0,2,1:T(8,128)S(1)} %broadcast_add_fusion, pred[12]{0:T(512)(128)(4,1)S(1)} %compare_and_fusion), kind=kLoop, calls=%fused_computation.2 | loop fusion | flops 12582912 | bytes 12812300 | tf_op jit(solution)/shard_map/jit(_where)/select_n | solution.py:237
  8.9 4.0 %slice_convert_fusion.2 = (f32[256,4,8,128]{3,0,2,1:T(8,128)}, bf16[256,4,8,128]{3,0,2,1:T(8,128)(2,1)}, bf16[256,4,8,128]{3,0,2,1:T(8,128)(2,1)}) fusion(bf16[256,12,8,128]{3,0,2,1:T(8,128)(2,1)S(1)} %fusion.1), kind=kLoop, calls=%fused_computation.103 | loop fusion | flops 1048576 | bytes 14680064 | tf_op jit(solution)/shard_map/convert_element_type | solution.py:57
  12.9 7.7 %collective-permute-start.1 = (bf16[256,4,8,128]{3,0,2,1:T(8,128)(2,1)}, bf16[256,4,8,128]{3,0,2,1:T(8,128)(2,1)}, u32[]{:S(2)}, u32[]{:S(2)}) collective-permute-start(bf16[256,4,8,128]{3,0,2,1:T(8,128)(2,1)} %get-tuple-element.5), channel_id=1, source_target_pairs={{4,0},{8,4},{12,8},{16,12},{20,16},{24,20},{28,24},{32,28},{36,32}... | collective-permute-start | bytes 6291464 | tf_op jit(solution)/shard_map/ppermute | solution.py:26
  20.6 1.0 slice_bitcast_fusion.1
  22.1 1.5 %collective-permute-start.4 = (bf16[256,12,128]{2,0,1:T(8,128)(2,1)S(1)}, bf16[256,12,128]{2,0,1:T(8,128)(2,1)}, u32[]{:S(2)}, u32[]{:S(2)}) collective-permute-start(bf16[256,12,128]{2,0,1:T(8,128)(2,1)S(1)} %get-tuple-element.2), channel_id=1, source_target_pairs={{1,0},{2,1},{3,2},{0,3},{5,4},{6,5},{7,6},{4,7},{9,8},{10,9},{11,1... | collective-permute-start | bytes 2359304 | tf_op jit(solution)/shard_map/ppermute | solution.py:247
  23.9 2.8 %copy-done.1 = bf16[256,12,8,128]{3,0,2,1:T(8,128)(2,1)S(1)} copy-done((bf16[256,12,8,128]{3,0,2,1:T(8,128)(2,1)S(1)}, bf16[256,12,8,128]{3,0,2,1:T(8,128)(2,1)}, u32[]{:S(2)}) %copy-start.1) | copy-done | bytes 6291480
  27.4 8.3 %collective-permute-done.5 = bf16[256,12,128]{2,0,1:T(8,128)(2,1)} collective-permute-done((bf16[256,12,128]{2,0,1:T(8,128)(2,1)}, bf16[256,12,128]{2,0,1:T(8,128)(2,1)}, u32[]{:S(2)}, u32[]{:S(2)}) %collective-permute-start.5) | collective-permute-done | bytes 786464 | tf_op jit(solution)/shard_map/ppermute | solution.py:246
  35.7 1.0 slice_bitcast_fusion.4
  37.1 1.0 slice_bitcast_fusion.5
  38.1 6.4 %collective-permute-done = bf16[256,4,8,128]{3,0,2,1:T(8,128)(2,1)S(1)} collective-permute-done((bf16[256,4,8,128]{3,0,2,1:T(8,128)(2,1)}, bf16[256,4,8,128]{3,0,2,1:T(8,128)(2,1)S(1)}, u32[]{:S(2)}, u32[]{:S(2)}) %collective-permute-start) | collective-permute-done | bytes 2097184 | tf_op jit(solution)/shard_map/ppermute | solution.py:26
  46.1 1.6 %slice.165 = bf16[256,3,8,128]{3,0,2,1:T(8,128)(2,1)S(1)} slice(bf16[256,4,8,128]{3,0,2,1:T(8,128)(2,1)} %collective-permute-done.1), slice={[0:256], [0:3], [0:8], [0:128]} | slice | bytes 3145728 | tf_op jit(solution)/shard_map/slice | solution.py:274
  49.0 1.1 maximum_bitcast_fusion.9
  50.7 1.5 %collective-permute-start.3 = (bf16[2,256,4,128]{3,1,2,0:T(8,128)(2,1)S(1)}, bf16[2,256,4,128]{3,1,2,0:T(8,128)(2,1)S(1)}, u32[]{:S(2)}, u32[]{:S(2)}) collective-permute-start(bf16[2,256,4,128]{3,1,2,0:T(8,128)(2,1)S(1)} %get-tuple-element.8), channel_id=1, source_target_pairs={{1,0},{2,1},{3,2},{0,3},{5,4},{6,5},{7,6},{4,7},{9,8},{10,9},{11,1... | collective-permute-start | bytes 1572872 | tf_op jit(solution)/shard_map/ppermute | solution.py:250
  52.7 2.2 %fusion.54 = f32[1,256,256]{2,1,0:T(8,128)S(1)} fusion(bf16[256,3,8,128]{3,0,2,1:T(8,128)(2,1)S(1)} %slice.163, bf16[256,4,8,128]{3,0,2,1:T(8,128)(2,1)} %collective-permute-done.1), kind=kOutput, calls=%fused_computation.73 | convolution fusion | flops 402653184 | bytes 3407872 | tf_op jit(solution)/shard_map/dot_general | solution.py:72
  54.8 2.2 %convolution_bitcast_fusion.2 = f32[1,256,256]{2,1,0:T(8,128)S(1)} fusion(bf16[256,12,8,128]{3,0,2,1:T(8,128)(2,1)S(1)} %copy-done.1, bf16[256,4,8,128]{3,0,2,1:T(8,128)(2,1)} %collective-permute-done.1), kind=kOutput, calls=%fused_computation.83 | convolution fusion | flops 402653184 | bytes 3932160 | tf_op jit(solution)/shard_map/dot_general | solution.py:72
  59.1 2.3 %concatenate.47 = bf16[256,6,8,128]{3,0,2,1:T(8,128)(2,1)S(1)} pad(bf16[256,4,8,128]{3,0,2,1:T(8,128)(2,1)} %collective-permute-done.1, bf16[]{:T(256)} %constant.61.clone.1), padding=0_0x2_0x0_0x0_0 | pad | bytes 5242882 | tf_op jit(solution)/shard_map/concatenate | solution.py:268
  61.4 4.0 %slice_convert_fusion = f32[256,4,8,128]{3,0,2,1:T(8,128)} fusion(bf16[256,4,8,128]{3,0,2,1:T(8,128)(2,1)} %collective-permute-done.1), kind=kLoop, calls=%fused_computation.58 | loop fusion | flops 1048576 | bytes 6291456 | tf_op jit(solution)/shard_map/convert_element_type | solution.py:57
  65.8 1.6 %slice-done.2 = bf16[256,6,8,128]{3,0,2,1:T(8,128)(2,1)S(1)} async-done(((bf16[256,12,8,128]{3,0,2,1:T(8,128)(2,1)}), bf16[256,6,8,128]{3,0,2,1:T(8,128)(2,1)S(1)}, s32[]{:S(2)}) %slice-start.2) | async-done | bytes 3145752 | tf_op jit(solution)/shard_map/slice | solution.py:260
  67.4 7.1 %fusion.7 = (bf16[256,4,8,128]{3,0,2,1:T(8,128)(2,1)}, bf16[256,4,8,128]{3,0,2,1:T(8,128)(2,1)}) fusion(f32[256,4,8,128]{3,0,2,1:T(8,128)S(1)} %slice_convert_fusion.1, bf16[256,4,8,128]{3,0,2,1:T(8,128)(2,1)S(1)} %collective-permute-done, bf16[256,6,8,128]{3,0,2,1:T(8,128)(2,1)S(1)} %concatenate.41, bf16[256,6,1,128]{3,0,2,1:T(8,128)(2,1)S(1)} %get-tuple-element.12, ...), kind=kLoop, calls=%fused_computation.15 | loop fusion | flops 35651584 | bytes 28852224 | tf_op jit(solution)/shard_map/convert_element_type | solution.py:277
  74.5 2.9 %fusion.57 = f32[1,256,256]{2,1,0:T(8,128)S(1)} fusion(bf16[256,4,8,128]{3,0,2,1:T(8,128)(2,1)} %get-tuple-element.19, bf16[256,3,8,128]{3,0,2,1:T(8,128)(2,1)} %copy-done.8), kind=kOutput, calls=%fused_computation.74 | convolution fusion | flops 536870912 | bytes 3932160 | tf_op jit(solution)/shard_map/dot_general | solution.py:72
  81.1 1.4 copy-done.3
  82.4 4.5 %fusion.19 = bf16[256,4,8,128]{3,0,2,1:T(8,128)(2,1)S(1)} fusion(f32[256,4,8,128]{3,0,2,1:T(8,128)S(1)} %copy-done.3, bf16[256,4,8,128]{3,0,2,1:T(8,128)(2,1)} %collective-permute-done.1, bf16[256,6,8,128]{3,0,2,1:T(8,128)(2,1)S(1)} %concatenate.47, bf16[256,6,1,128]{3,0,2,1:T(8,128)(2,1)S(1)} %get-tuple-element.14, ...), kind=kLoop, calls=%fused_computation.27 | loop fusion | flops 17825792 | bytes 14434304 | tf_op jit(solution)/shard_map/convert_element_type | solution.py:277
  92.1 47.4 %shard_map.77 = f32[2,5,64,256]{3,2,1,0:T(8,128)S(1)} custom-call(f32[3,2,3,256,256]{4,3,2,1,0:T(8,128)S(1)} %pad_maximum_fusion.x_ref), custom_call_target="tpu_custom_call" | custom-call | tf_op jit(solution)/shard_map/pallas_call | solution.py:197
  139.5 1.1 bitcast_multiply_fusion
  (78 shorter events, 18.9 us)
Async XLA Ops:
  8.9 11.8 %copy-start = (bf16[256,12,8,128]{3,0,2,1:T(8,128)(2,1)}, bf16[256,12,8,128]{3,0,2,1:T(8,128)(2,1)S(1)}, u32[]{:S(2)}) copy-start(bf16[256,12,8,128]{3,0,2,1:T(8,128)(2,1)S(1)} %fusion.1) | copy-start | bytes 18874372
  12.9 10.8 %copy-start.11 = (s32[2,5,2]{1,2,0:T(2,128)S(1)}, s32[2,5,2]{1,2,0:T(2,128)}, u32[]{:S(2)}) copy-start(s32[2,5,2]{1,2,0:T(2,128)} %param.11) | copy-start | bytes 244
  12.9 31.7 %collective-permute-start = (bf16[256,4,8,128]{3,0,2,1:T(8,128)(2,1)}, bf16[256,4,8,128]{3,0,2,1:T(8,128)(2,1)S(1)}, u32[]{:S(2)}, u32[]{:S(2)}) collective-permute-start(bf16[256,4,8,128]{3,0,2,1:T(8,128)(2,1)} %get-tuple-element.6), channel_id=1, source_target_pairs={{252,0},{0,4},{4,8},{8,12},{12,16},{16,20},{20,24},{24,28},{28,32}... | collective-permute-start | bytes 6291464 | tf_op jit(solution)/shard_map/ppermute | solution.py:26
  12.9 33.2 %collective-permute-start.1 = (bf16[256,4,8,128]{3,0,2,1:T(8,128)(2,1)}, bf16[256,4,8,128]{3,0,2,1:T(8,128)(2,1)}, u32[]{:S(2)}, u32[]{:S(2)}) collective-permute-start(bf16[256,4,8,128]{3,0,2,1:T(8,128)(2,1)} %get-tuple-element.5), channel_id=1, source_target_pairs={{4,0},{8,4},{12,8},{16,12},{20,16},{24,20},{28,24},{32,28},{36,32}... | collective-permute-start | bytes 6291464 | tf_op jit(solution)/shard_map/ppermute | solution.py:26
  21.7 14.0 %collective-permute-start.5 = (bf16[256,12,128]{2,0,1:T(8,128)(2,1)}, bf16[256,12,128]{2,0,1:T(8,128)(2,1)}, u32[]{:S(2)}, u32[]{:S(2)}) collective-permute-start(bf16[256,12,128]{2,0,1:T(8,128)(2,1)} %get-tuple-element.3), channel_id=1, source_target_pairs={{0,1},{1,2},{2,3},{3,0},{4,5},{5,6},{6,7},{7,4},{8,9},{9,10},{10,1... | collective-permute-start | bytes 2359304 | tf_op jit(solution)/shard_map/ppermute | solution.py:246
  22.1 15.0 %collective-permute-start.4 = (bf16[256,12,128]{2,0,1:T(8,128)(2,1)S(1)}, bf16[256,12,128]{2,0,1:T(8,128)(2,1)}, u32[]{:S(2)}, u32[]{:S(2)}) collective-permute-start(bf16[256,12,128]{2,0,1:T(8,128)(2,1)S(1)} %get-tuple-element.2), channel_id=1, source_target_pairs={{1,0},{2,1},{3,2},{0,3},{5,4},{6,5},{7,6},{4,7},{9,8},{10,9},{11,1... | collective-permute-start | bytes 2359304 | tf_op jit(solution)/shard_map/ppermute | solution.py:247
  23.9 2.8 %copy-start.1 = (bf16[256,12,8,128]{3,0,2,1:T(8,128)(2,1)S(1)}, bf16[256,12,8,128]{3,0,2,1:T(8,128)(2,1)}, u32[]{:S(2)}) copy-start(bf16[256,12,8,128]{3,0,2,1:T(8,128)(2,1)} %copy-done) | copy-start | bytes 18874372
  44.6 8.0 %copy-start.8 = (bf16[256,3,8,128]{3,0,2,1:T(8,128)(2,1)}, bf16[256,3,8,128]{3,0,2,1:T(8,128)(2,1)S(1)}, u32[]{:S(2)}) copy-start(bf16[256,3,8,128]{3,0,2,1:T(8,128)(2,1)S(1)} %slice.163) | copy-start | bytes 4718596
  47.6 10.1 %copy-start.6 = (bf16[256,3,8,128]{3,0,2,1:T(8,128)(2,1)}, bf16[256,3,8,128]{3,0,2,1:T(8,128)(2,1)S(1)}, u32[]{:S(2)}) copy-start(bf16[256,3,8,128]{3,0,2,1:T(8,128)(2,1)S(1)} %slice.165) | copy-start | bytes 4718596
  50.1 15.3 %collective-permute-start.2 = (bf16[2,256,4,128]{3,1,2,0:T(8,128)(2,1)S(1)}, bf16[2,256,4,128]{3,1,2,0:T(8,128)(2,1)S(1)}, u32[]{:S(2)}, u32[]{:S(2)}) collective-permute-start(bf16[2,256,4,128]{3,1,2,0:T(8,128)(2,1)S(1)} %get-tuple-element.7), channel_id=1, source_target_pairs={{0,1},{1,2},{2,3},{3,0},{4,5},{5,6},{6,7},{7,4},{8,9},{9,10},{10,1... | collective-permute-start | bytes 1572872 | tf_op jit(solution)/shard_map/ppermute | solution.py:249
  50.7 14.8 %collective-permute-start.3 = (bf16[2,256,4,128]{3,1,2,0:T(8,128)(2,1)S(1)}, bf16[2,256,4,128]{3,1,2,0:T(8,128)(2,1)S(1)}, u32[]{:S(2)}, u32[]{:S(2)}) collective-permute-start(bf16[2,256,4,128]{3,1,2,0:T(8,128)(2,1)S(1)} %get-tuple-element.8), channel_id=1, source_target_pairs={{1,0},{2,1},{3,2},{0,3},{5,4},{6,5},{7,6},{4,7},{9,8},{10,9},{11,1... | collective-permute-start | bytes 1572872 | tf_op jit(solution)/shard_map/ppermute | solution.py:250
  59.1 6.7 %slice-start = ((s8[6291456]{0:T(1024)(128)(4,1)}), s8[4194304]{0:T(1024)(128)(4,1)S(1)}, s32[]{:S(2)}) async-start(s8[6291456]{0:T(1024)(128)(4,1)} %bitcast.190), calls=%async_computation | async-start | bytes 8388608
  61.4 4.4 %slice-start.1 = ((s8[6291456]{0:T(1024)(128)(4,1)}), s8[2097152]{0:T(1024)(128)(4,1)S(1)}, s32[]{:S(2)}) async-start(s8[6291456]{0:T(1024)(128)(4,1)} %bitcast.190), calls=%async_computation.1 | async-start | bytes 4194304
  61.4 4.4 %copy-start.2 = (f32[256,4,8,128]{3,0,2,1:T(8,128)S(1)}, f32[256,4,8,128]{3,0,2,1:T(8,128)}, u32[]{:S(2)}) copy-start(f32[256,4,8,128]{3,0,2,1:T(8,128)} %get-tuple-element.4) | copy-start | bytes 12582916
  65.5 1.9 %slice-start.2 = ((bf16[256,12,8,128]{3,0,2,1:T(8,128)(2,1)}), bf16[256,6,8,128]{3,0,2,1:T(8,128)(2,1)S(1)}, s32[]{:S(2)}) async-start(bf16[256,12,8,128]{3,0,2,1:T(8,128)(2,1)} %copy-done), calls=%async_computation.2 | async-start | bytes 6291456 | tf_op jit(solution)/shard_map/slice | solution.py:260
  65.5 1.9 %copy-start.10 = (f32[4,8,128]{2,1,0:T(8,128)S(1)}, f32[4,8,128]{2,1,0:T(8,128)}, u32[]{:S(2)}) copy-start(f32[4,8,128]{2,1,0:T(8,128)} %param.7) | copy-start | bytes 49156
  74.5 2.9 %copy-start.5 = (bf16[256,4,8,128]{3,0,2,1:T(8,128)(2,1)S(1)}, bf16[256,4,8,128]{3,0,2,1:T(8,128)(2,1)}, u32[]{:S(2)}) copy-start(bf16[256,4,8,128]{3,0,2,1:T(8,128)(2,1)} %get-tuple-element.19) | copy-start | bytes 6291460
  77.5 1.6 %copy-start.4 = (bf16[256,4,8,128]{3,0,2,1:T(8,128)(2,1)S(1)}, bf16[256,4,8,128]{3,0,2,1:T(8,128)(2,1)}, u32[]{:S(2)}) copy-start(bf16[256,4,8,128]{3,0,2,1:T(8,128)(2,1)} %get-tuple-element.20) | copy-start | bytes 6291460
  77.5 2.0 %copy-start.9 = (bf16[256,3,8,128]{3,0,2,1:T(8,128)(2,1)S(1)}, bf16[256,3,8,128]{3,0,2,1:T(8,128)(2,1)}, u32[]{:S(2)}) copy-start(bf16[256,3,8,128]{3,0,2,1:T(8,128)(2,1)} %copy-done.8) | copy-start | bytes 4718596
  80.2 2.2 %copy-start.3 = (f32[256,4,8,128]{3,0,2,1:T(8,128)S(1)}, f32[256,4,8,128]{3,0,2,1:T(8,128)}, u32[]{:S(2)}) copy-start(f32[256,4,8,128]{3,0,2,1:T(8,128)} %slice_convert_fusion) | copy-start | bytes 12582916
  87.7 1.4 %copy-start.7 = (bf16[256,3,8,128]{3,0,2,1:T(8,128)(2,1)S(1)}, bf16[256,3,8,128]{3,0,2,1:T(8,128)(2,1)}, u32[]{:S(2)}) copy-start(bf16[256,3,8,128]{3,0,2,1:T(8,128)(2,1)} %copy-done.6) | copy-start | bytes 4718596

commit v8 on v7

--- a/solution.py
+++ b/solution.py
@@ -243,8 +243,9 @@
     mat_size = lax.axis_size("mat")
     up = [(i, (i + 1) % mat_size) for i in range(mat_size)]
     down = [(j, i) for i, j in up]
-    row_above = lax.ppermute(masked[:, :, second_cells - 1], "mat", up)
-    row_below = lax.ppermute(masked[:, :, 0], "mat", down)
+    own_planes = masked[:, patch_cells - 1 : upper_start + 1]
+    row_above = lax.ppermute(own_planes[:, :, second_cells - 1], "mat", up)
+    row_below = lax.ppermute(own_planes[:, :, 0], "mat", down)
     arrived = jnp.stack([from_left, from_right])
     arrived_above = lax.ppermute(arrived[:, :, :, second_cells - 1], "mat", up)
     arrived_below = lax.ppermute(arrived[:, :, :, 0], "mat", down)
@@ -258,7 +259,7 @@
     zero_rows = jnp.zeros((2, block_orbs, 1, third_cells), masked.dtype)
     own_ext = with_rows(
         masked[:, patch_cells - 1 : upper_start + 1],
-        jnp.stack([row_above[:, patch_cells - 1 : upper_start + 1], row_below[:, patch_cells - 1 : upper_start + 1]]),
+        jnp.stack([row_above, row_below]),
     )
     left_ext = with_rows(
         jnp.concatenate([from_left, zero_plane, zero_plane], axis=1),

time: 141 us -> 144 us (1.021)
  local copies, waits for them, and re-layouts: 15.4 us -> 13 us
  matrix products: 19.2 us -> 21.4 us
  waiting for transfers between devices: 15 us -> 16.5 us
    ppermute x2, waiting for transfers between devices: 6.39 us -> 16.5 us  [passed_along(): return lax.ppermute(block, axis, route)]
    ppermute x2, waiting for transfers between devices: 8.65 us -> 0.01 us  [the longest x1 0.01 us: on_device(): row_below = lax.ppermute(own_planes[:, :, 0], 'mat', down)]
    dot_general x18, matrix products: 17.9 us -> 20.1 us  [pair_product(): lax.dot_general(left, right, (((1, 2, 3), (1, 2, 3)), ((), ())), preferre...]
  transfers between devices with their start and end apart: 6 -> 6, of which waited for: 3 -> 1; matrix products, arithmetic and copies ran while one was open for 13% -> 16% of each run, Pallas kernels for 0% -> 0%
where the time goes in v8:
time: 144 us; the launch traced here: 143 us
  Pallas kernels  47.4 us (33%)
  other arithmetic  30.6 us (21%)
  matrix products  21.4 us (15%)
  waiting for transfers between devices  16.5 us (11%)
  starting transfers between devices  13.1 us (9%)
  local copies, waits for them, and re-layouts  13 us (9%)
    pallas_call x1, Pallas kernels, exchange_and_sum(): pl.pallas_call(functools.partial(exchange_kernel, count, domains, share,...  47.4 us
    dot_general x18, matrix products, pair_product(): lax.dot_general(left, right, (((1, 2, 3), (1, 2, 3)), ((), ())), preferre...  20.1 us
    ppermute x2, waiting for transfers between devices, passed_along(): return lax.ppermute(block, axis, route)  16.5 us
    convert_element_type x2, other arithmetic, on_device(): stencil(ext, potential).astype(jnp.bfloat16)  11.6 us
    convert_element_type x3, other arithmetic, stencil(): centre_cells = extended[:, 1:-1, 1:-1, :].astype(jnp.float32)  8.43 us
    ppermute x2, starting transfers between devices, passed_along(): return lax.ppermute(block, axis, route)  7.75 us
    select_n x1, other arithmetic, on_device(): masked = jnp.where(inside, orbitals, jnp.zeros_like(orbitals))  5.94 us
    unnamed x28, local copies, waits for them, and re-layouts  5.9 us
  transfers between devices with their start and end apart: 6, of which 1 were waited for; matrix products, arithmetic and copies ran while one was open for 16% of the time, Pallas kernels for 0%

profile of v8, /device:TPU:6, one launch (start us, length us, event | category | flops | bytes accessed | tf_op | source)
XLA Modules:
  0.0 143.1 jit_solution(6368729806024296764)
XLA Ops:
  2.9 5.9 %fusion.1 = bf16[256,12,8,128]{3,0,2,1:T(8,128)(2,1)S(1)} fusion(bf16[256,12,8,128]{3,2,1,0:T(8,128)(2,1)} %param.6, s32[256,128]{1,0:T(8,128)S(1)} %subtract_multiply_fusion, s32[256,12,8]{0,2,1:T(8,128)S(1)} %broadcast_add_fusion, pred[12]{0:T(512)(128)(4,1)S(1)} %compare_and_fusion), kind=kLoop, calls=%fused_computation.2 | loop fusion | flops 12582912 | bytes 12812300 | tf_op jit(solution)/shard_map/jit(_where)/select_n | solution.py:237
  8.9 4.0 %slice_convert_fusion.2 = (f32[256,4,8,128]{3,0,2,1:T(8,128)}, bf16[256,4,8,128]{3,0,2,1:T(8,128)(2,1)}, bf16[256,4,8,128]{3,0,2,1:T(8,128)(2,1)}) fusion(bf16[256,12,8,128]{3,0,2,1:T(8,128)(2,1)S(1)} %fusion.1), kind=kLoop, calls=%fused_computation.101 | loop fusion | flops 1048576 | bytes 14680064 | tf_op jit(solution)/shard_map/convert_element_type | solution.py:57
  12.9 7.7 %collective-permute-start.1 = (bf16[256,4,8,128]{3,0,2,1:T(8,128)(2,1)}, bf16[256,4,8,128]{3,0,2,1:T(8,128)(2,1)}, u32[]{:S(2)}, u32[]{:S(2)}) collective-permute-start(bf16[256,4,8,128]{3,0,2,1:T(8,128)(2,1)} %get-tuple-element.5), channel_id=1, source_target_pairs={{4,0},{8,4},{12,8},{16,12},{20,16},{24,20},{28,24},{32,28},{36,32}... | collective-permute-start | bytes 6291464 | tf_op jit(solution)/shard_map/ppermute | solution.py:26
  20.6 0.9 slice_bitcast_fusion.3
  21.5 0.8 collective-permute-start.4
  22.4 2.4 %collective-permute-start.5 = (bf16[256,6,128]{2,0,1:T(8,128)(2,1)}, bf16[256,6,128]{2,0,1:T(8,128)(2,1)S(1)}, u32[]{:S(2)}, u32[]{:S(2)}) collective-permute-start(bf16[256,6,128]{2,0,1:T(8,128)(2,1)} %get-tuple-element.3), channel_id=1, source_target_pairs={{0,1},{1,2},{2,3},{3,0},{4,5},{5,6},{6,7},{7,4},{8,9},{9,10},{10,1... | collective-permute-start | bytes 1179656 | tf_op jit(solution)/shard_map/ppermute | solution.py:247
  25.0 3.0 %convolution_bitcast_fusion.1 = f32[1,256,256]{2,1,0:T(8,128)S(1)} fusion(bf16[256,12,8,128]{3,0,2,1:T(8,128)(2,1)} %copy-done), kind=kOutput, calls=%fused_computation.70 | convolution fusion | flops 536870912 | bytes 8650752 | tf_op jit(solution)/shard_map/dot_general | solution.py:72
  28.0 16.5 %collective-permute-done = bf16[256,4,8,128]{3,0,2,1:T(8,128)(2,1)S(1)} collective-permute-done((bf16[256,4,8,128]{3,0,2,1:T(8,128)(2,1)}, bf16[256,4,8,128]{3,0,2,1:T(8,128)(2,1)S(1)}, u32[]{:S(2)}, u32[]{:S(2)}) %collective-permute-start) | collective-permute-done | bytes 2097184 | tf_op jit(solution)/shard_map/ppermute | solution.py:26
  45.3 2.6 %copy-done.1 = bf16[256,12,8,128]{3,0,2,1:T(8,128)(2,1)S(1)} copy-done((bf16[256,12,8,128]{3,0,2,1:T(8,128)(2,1)S(1)}, bf16[256,12,8,128]{3,0,2,1:T(8,128)(2,1)}, u32[]{:S(2)}) %copy-start.1) | copy-done | bytes 6291480
  48.6 1.6 %slice.160 = bf16[256,3,8,128]{3,0,2,1:T(8,128)(2,1)S(1)} slice(bf16[256,4,8,128]{3,0,2,1:T(8,128)(2,1)} %collective-permute-done.1), slice={[0:256], [0:3], [0:8], [0:128]} | slice | bytes 3145728 | tf_op jit(solution)/shard_map/slice | solution.py:275
  51.6 1.1 maximum_bitcast_fusion.9
  53.3 1.5 %collective-permute-start.3 = (bf16[2,256,4,128]{3,1,2,0:T(8,128)(2,1)S(1)}, bf16[2,256,4,128]{3,1,2,0:T(8,128)(2,1)S(1)}, u32[]{:S(2)}, u32[]{:S(2)}) collective-permute-start(bf16[2,256,4,128]{3,1,2,0:T(8,128)(2,1)S(1)} %get-tuple-element.8), channel_id=1, source_target_pairs={{1,0},{2,1},{3,2},{0,3},{5,4},{6,5},{7,6},{4,7},{9,8},{10,9},{11,1... | collective-permute-start | bytes 1572872 | tf_op jit(solution)/shard_map/ppermute | solution.py:251
  55.2 2.2 %fusion.54 = f32[1,256,256]{2,1,0:T(8,128)S(1)} fusion(bf16[256,3,8,128]{3,0,2,1:T(8,128)(2,1)S(1)} %slice.158, bf16[256,4,8,128]{3,0,2,1:T(8,128)(2,1)} %collective-permute-done.1), kind=kOutput, calls=%fused_computation.73 | convolution fusion | flops 402653184 | bytes 3407872 | tf_op jit(solution)/shard_map/dot_general | solution.py:72
  57.4 2.2 %convolution_bitcast_fusion.2 = f32[1,256,256]{2,1,0:T(8,128)S(1)} fusion(bf16[256,12,8,128]{3,0,2,1:T(8,128)(2,1)S(1)} %copy-done.1, bf16[256,4,8,128]{3,0,2,1:T(8,128)(2,1)} %collective-permute-done.1), kind=kOutput, calls=%fused_computation.83 | convolution fusion | flops 402653184 | bytes 3932160 | tf_op jit(solution)/shard_map/dot_general | solution.py:72
  61.7 2.3 %concatenate.47 = bf16[256,6,8,128]{3,0,2,1:T(8,128)(2,1)S(1)} pad(bf16[256,4,8,128]{3,0,2,1:T(8,128)(2,1)} %collective-permute-done.1, bf16[]{:T(256)} %constant.61.clone.1), padding=0_0x2_0x0_0x0_0 | pad | bytes 5242882 | tf_op jit(solution)/shard_map/concatenate | solution.py:269
  64.0 4.0 %slice_convert_fusion = f32[256,4,8,128]{3,0,2,1:T(8,128)} fusion(bf16[256,4,8,128]{3,0,2,1:T(8,128)(2,1)} %collective-permute-done.1), kind=kLoop, calls=%fused_computation.58 | loop fusion | flops 1048576 | bytes 6291456 | tf_op jit(solution)/shard_map/convert_element_type | solution.py:57
  68.4 1.6 %slice-done.2 = bf16[256,6,8,128]{3,0,2,1:T(8,128)(2,1)S(1)} async-done(((bf16[256,12,8,128]{3,0,2,1:T(8,128)(2,1)}), bf16[256,6,8,128]{3,0,2,1:T(8,128)(2,1)S(1)}, s32[]{:S(2)}) %slice-start.2) | async-done | bytes 3145752 | tf_op jit(solution)/shard_map/slice | solution.py:261
  70.0 7.1 %fusion.7 = (bf16[256,4,8,128]{3,0,2,1:T(8,128)(2,1)}, bf16[256,4,8,128]{3,0,2,1:T(8,128)(2,1)}) fusion(f32[256,4,8,128]{3,0,2,1:T(8,128)S(1)} %slice_convert_fusion.1, bf16[256,4,8,128]{3,0,2,1:T(8,128)(2,1)S(1)} %collective-permute-done, bf16[256,6,8,128]{3,0,2,1:T(8,128)(2,1)S(1)} %concatenate.41, bf16[256,6,1,128]{3,0,2,1:T(8,128)(2,1)S(1)} %get-tuple-element.12, ...), kind=kLoop, calls=%fused_computation.15 | loop fusion | flops 35651584 | bytes 28852224 | tf_op jit(solution)/shard_map/convert_element_type | solution.py:278
  77.1 2.9 %fusion.57 = f32[1,256,256]{2,1,0:T(8,128)S(1)} fusion(bf16[256,4,8,128]{3,0,2,1:T(8,128)(2,1)} %get-tuple-element.19, bf16[256,3,8,128]{3,0,2,1:T(8,128)(2,1)} %copy-done.8), kind=kOutput, calls=%fused_computation.74 | convolution fusion | flops 536870912 | bytes 3932160 | tf_op jit(solution)/shard_map/dot_general | solution.py:72
  80.8 0.8 copy-done.4
  83.6 1.4 copy-done.3
  85.0 4.5 %fusion.19 = bf16[256,4,8,128]{3,0,2,1:T(8,128)(2,1)S(1)} fusion(f32[256,4,8,128]{3,0,2,1:T(8,128)S(1)} %copy-done.3, bf16[256,4,8,128]{3,0,2,1:T(8,128)(2,1)} %collective-permute-done.1, bf16[256,6,8,128]{3,0,2,1:T(8,128)(2,1)S(1)} %concatenate.47, bf16[256,6,1,128]{3,0,2,1:T(8,128)(2,1)S(1)} %get-tuple-element.14, ...), kind=kLoop, calls=%fused_computation.27 | loop fusion | flops 17825792 | bytes 14434304 | tf_op jit(solution)/shard_map/convert_element_type | solution.py:278
  94.6 47.4 %shard_map.77 = f32[2,5,64,256]{3,2,1,0:T(8,128)S(1)} custom-call(f32[3,2,3,256,256]{4,3,2,1,0:T(8,128)S(1)} %pad_maximum_fusion.x_ref), custom_call_target="tpu_custom_call" | custom-call | tf_op jit(solution)/shard_map/pallas_call | solution.py:197
  142.0 1.1 bitcast_multiply_fusion
  (76 shorter events, 16.4 us)
Async XLA Ops:
  8.9 15.9 %copy-start = (bf16[256,12,8,128]{3,0,2,1:T(8,128)(2,1)}, bf16[256,12,8,128]{3,0,2,1:T(8,128)(2,1)S(1)}, u32[]{:S(2)}) copy-start(bf16[256,12,8,128]{3,0,2,1:T(8,128)(2,1)S(1)} %fusion.1) | copy-start | bytes 18874372
  12.9 31.7 %collective-permute-start = (bf16[256,4,8,128]{3,0,2,1:T(8,128)(2,1)}, bf16[256,4,8,128]{3,0,2,1:T(8,128)(2,1)S(1)}, u32[]{:S(2)}, u32[]{:S(2)}) collective-permute-start(bf16[256,4,8,128]{3,0,2,1:T(8,128)(2,1)} %get-tuple-element.6), channel_id=1, source_target_pairs={{252,0},{0,4},{4,8},{8,12},{12,16},{16,20},{20,24},{24,28},{28,32}... | collective-permute-start | bytes 6291464 | tf_op jit(solution)/shard_map/ppermute | solution.py:26
  12.9 35.8 %collective-permute-start.1 = (bf16[256,4,8,128]{3,0,2,1:T(8,128)(2,1)}, bf16[256,4,8,128]{3,0,2,1:T(8,128)(2,1)}, u32[]{:S(2)}, u32[]{:S(2)}) collective-permute-start(bf16[256,4,8,128]{3,0,2,1:T(8,128)(2,1)} %get-tuple-element.5), channel_id=1, source_target_pairs={{4,0},{8,4},{12,8},{16,12},{20,16},{24,20},{28,24},{32,28},{36,32}... | collective-permute-start | bytes 6291464 | tf_op jit(solution)/shard_map/ppermute | solution.py:26
  21.5 46.8 %collective-permute-start.4 = (bf16[256,6,128]{2,0,1:T(8,128)(2,1)}, bf16[256,6,128]{2,0,1:T(8,128)(2,1)S(1)}, u32[]{:S(2)}, u32[]{:S(2)}) collective-permute-start(bf16[256,6,128]{2,0,1:T(8,128)(2,1)} %get-tuple-element.2), channel_id=1, source_target_pairs={{1,0},{2,1},{3,2},{0,3},{5,4},{6,5},{7,6},{4,7},{9,8},{10,9},{11,1... | collective-permute-start | bytes 1179656 | tf_op jit(solution)/shard_map/ppermute | solution.py:248
  22.4 2.4 %copy-start.11 = (s32[2,5,2]{1,2,0:T(2,128)S(1)}, s32[2,5,2]{1,2,0:T(2,128)}, u32[]{:S(2)}) copy-start(s32[2,5,2]{1,2,0:T(2,128)} %param.11) | copy-start | bytes 244
  22.4 46.0 %collective-permute-start.5 = (bf16[256,6,128]{2,0,1:T(8,128)(2,1)}, bf16[256,6,128]{2,0,1:T(8,128)(2,1)S(1)}, u32[]{:S(2)}, u32[]{:S(2)}) collective-permute-start(bf16[256,6,128]{2,0,1:T(8,128)(2,1)} %get-tuple-element.3), channel_id=1, source_target_pairs={{0,1},{1,2},{2,3},{3,0},{4,5},{5,6},{6,7},{7,4},{8,9},{9,10},{10,1... | collective-permute-start | bytes 1179656 | tf_op jit(solution)/shard_map/ppermute | solution.py:247
  44.5 3.4 %copy-start.1 = (bf16[256,12,8,128]{3,0,2,1:T(8,128)(2,1)S(1)}, bf16[256,12,8,128]{3,0,2,1:T(8,128)(2,1)}, u32[]{:S(2)}) copy-start(bf16[256,12,8,128]{3,0,2,1:T(8,128)(2,1)} %copy-done) | copy-start | bytes 18874372
  44.6 10.6 %copy-start.8 = (bf16[256,3,8,128]{3,0,2,1:T(8,128)(2,1)}, bf16[256,3,8,128]{3,0,2,1:T(8,128)(2,1)S(1)}, u32[]{:S(2)}) copy-start(bf16[256,3,8,128]{3,0,2,1:T(8,128)(2,1)S(1)} %slice.158) | copy-start | bytes 4718596
  50.2 10.1 %copy-start.6 = (bf16[256,3,8,128]{3,0,2,1:T(8,128)(2,1)}, bf16[256,3,8,128]{3,0,2,1:T(8,128)(2,1)S(1)}, u32[]{:S(2)}) copy-start(bf16[256,3,8,128]{3,0,2,1:T(8,128)(2,1)S(1)} %slice.160) | copy-start | bytes 4718596
  52.7 15.3 %collective-permute-start.2 = (bf16[2,256,4,128]{3,1,2,0:T(8,128)(2,1)S(1)}, bf16[2,256,4,128]{3,1,2,0:T(8,128)(2,1)S(1)}, u32[]{:S(2)}, u32[]{:S(2)}) collective-permute-start(bf16[2,256,4,128]{3,1,2,0:T(8,128)(2,1)S(1)} %get-tuple-element.7), channel_id=1, source_target_pairs={{0,1},{1,2},{2,3},{3,0},{4,5},{5,6},{6,7},{7,4},{8,9},{9,10},{10,1... | collective-permute-start | bytes 1572872 | tf_op jit(solution)/shard_map/ppermute | solution.py:250
  53.3 14.8 %collective-permute-start.3 = (bf16[2,256,4,128]{3,1,2,0:T(8,128)(2,1)S(1)}, bf16[2,256,4,128]{3,1,2,0:T(8,128)(2,1)S(1)}, u32[]{:S(2)}, u32[]{:S(2)}) collective-permute-start(bf16[2,256,4,128]{3,1,2,0:T(8,128)(2,1)S(1)} %get-tuple-element.8), channel_id=1, source_target_pairs={{1,0},{2,1},{3,2},{0,3},{5,4},{6,5},{7,6},{4,7},{9,8},{10,9},{11,1... | collective-permute-start | bytes 1572872 | tf_op jit(solution)/shard_map/ppermute | solution.py:251
  61.7 6.7 %slice-start = ((s8[6291456]{0:T(1024)(128)(4,1)}), s8[4194304]{0:T(1024)(128)(4,1)S(1)}, s32[]{:S(2)}) async-start(s8[6291456]{0:T(1024)(128)(4,1)} %bitcast.188), calls=%async_computation | async-start | bytes 8388608
  63.9 4.4 %slice-start.1 = ((s8[6291456]{0:T(1024)(128)(4,1)}), s8[2097152]{0:T(1024)(128)(4,1)S(1)}, s32[]{:S(2)}) async-start(s8[6291456]{0:T(1024)(128)(4,1)} %bitcast.188), calls=%async_computation.1 | async-start | bytes 4194304
  63.9 4.4 %copy-start.2 = (f32[256,4,8,128]{3,0,2,1:T(8,128)S(1)}, f32[256,4,8,128]{3,0,2,1:T(8,128)}, u32[]{:S(2)}) copy-start(f32[256,4,8,128]{3,0,2,1:T(8,128)} %get-tuple-element.4) | copy-start | bytes 12582916
  68.1 1.9 %slice-start.2 = ((bf16[256,12,8,128]{3,0,2,1:T(8,128)(2,1)}), bf16[256,6,8,128]{3,0,2,1:T(8,128)(2,1)S(1)}, s32[]{:S(2)}) async-start(bf16[256,12,8,128]{3,0,2,1:T(8,128)(2,1)} %copy-done), calls=%async_computation.2 | async-start | bytes 6291456 | tf_op jit(solution)/shard_map/slice | solution.py:261
  68.1 1.9 %copy-start.10 = (f32[4,8,128]{2,1,0:T(8,128)S(1)}, f32[4,8,128]{2,1,0:T(8,128)}, u32[]{:S(2)}) copy-start(f32[4,8,128]{2,1,0:T(8,128)} %param.7) | copy-start | bytes 49156
  77.1 2.9 %copy-start.5 = (bf16[256,4,8,128]{3,0,2,1:T(8,128)(2,1)S(1)}, bf16[256,4,8,128]{3,0,2,1:T(8,128)(2,1)}, u32[]{:S(2)}) copy-start(bf16[256,4,8,128]{3,0,2,1:T(8,128)(2,1)} %get-tuple-element.19) | copy-start | bytes 6291460
  80.0 1.6 %copy-start.4 = (bf16[256,4,8,128]{3,0,2,1:T(8,128)(2,1)S(1)}, bf16[256,4,8,128]{3,0,2,1:T(8,128)(2,1)}, u32[]{:S(2)}) copy-start(bf16[256,4,8,128]{3,0,2,1:T(8,128)(2,1)} %get-tuple-element.20) | copy-start | bytes 6291460
  80.0 2.0 %copy-start.9 = (bf16[256,3,8,128]{3,0,2,1:T(8,128)(2,1)S(1)}, bf16[256,3,8,128]{3,0,2,1:T(8,128)(2,1)}, u32[]{:S(2)}) copy-start(bf16[256,3,8,128]{3,0,2,1:T(8,128)(2,1)} %copy-done.8) | copy-start | bytes 4718596
  82.8 2.2 %copy-start.3 = (f32[256,4,8,128]{3,0,2,1:T(8,128)S(1)}, f32[256,4,8,128]{3,0,2,1:T(8,128)}, u32[]{:S(2)}) copy-start(f32[256,4,8,128]{3,0,2,1:T(8,128)} %slice_convert_fusion) | copy-start | bytes 12582916
  90.3 1.4 copy-start.7

commit v9 on v7

--- a/solution.py
+++ b/solution.py
@@ -268,11 +268,20 @@
         jnp.concatenate([zero_plane, zero_plane, from_right], axis=1),
         jnp.concatenate([zero_rows, zero_rows, rows_from_right], axis=2),
     )
-    phi_slots = [
-        jnp.concatenate([from_left[:, 1:], zero_plane], axis=1),
-        masked[:, patch_cells:upper_start],
-        jnp.concatenate([zero_plane, from_right[:, :-1]], axis=1),
-    ]
+    phi_slots = [from_left[:, 1:], masked[:, patch_cells:upper_start], from_right[:, :-1]]
+    plane_ranges = [(0, patch_cells - 1), (0, patch_cells), (1, patch_cells)]
+
+    def overlap(a, b):
+        low = max(plane_ranges[a][0], plane_ranges[b][0])
+        high = min(plane_ranges[a][1], plane_ranges[b][1])
+        first = phi_slots[a][:, low - plane_ranges[a][0] : high - plane_ranges[a][0]]
+        second = phi_slots[b][:, low - plane_ranges[b][0] : high - plane_ranges[b][0]]
+        return pair_product(first, second)
+
+    def applied_overlap(a, b):
+        low, high = plane_ranges[b]
+        return pair_product(applied_slots[a][:, low:high], phi_slots[b])
+
     applied_slots = [
         stencil(ext, potential).astype(jnp.bfloat16) for ext in (left_ext, own_ext, right_ext)
     ]
@@ -280,8 +289,8 @@
         [
             jnp.stack(
                 [
-                    jnp.stack([pair_product(phi_slots[a], phi_slots[b]) for a in range(3)]),
-                    jnp.stack([pair_product(applied_slots[a], phi_slots[b]) for a in range(3)]),
+                    jnp.stack([overlap(a, b) for a in range(3)]),
+                    jnp.stack([applied_overlap(a, b) for a in range(3)]),
                 ]
             )
             for b in range(3)

time: 141 us -> 148 us (1.050)
  matrix products: 19.2 us -> 25.6 us
  Pallas kernels: 47.4 us -> 48.9 us
  local copies, waits for them, and re-layouts: 15.4 us -> 13.9 us
    dot_general x18, matrix products: 17.9 us -> 24.3 us  [pair_product(): lax.dot_general(left, right, (((1, 2, 3), (1, 2, 3)), ((), ())), preferre...]
    slice x2 -> x0, local copies, waits for them, and re-layouts: 1.65 us -> none  [the longest x1 1.55 us: on_device(): from_right[:, :-1]]
    pallas_call x1, Pallas kernels: 47.4 us -> 48.9 us  [exchange_and_sum(): pl.pallas_call(functools.partial(exchange_kernel, count, domains, share,...]
    unnamed x28 -> x20, local copies, waits for them, and re-layouts: 6.14 us -> 6.85 us
  transfers between devices with their start and end apart: 6 -> 6, of which waited for: 3 -> 3; matrix products, arithmetic and copies ran while one was open for 13% -> 16% of each run, Pallas kernels for 0% -> 0%
where the time goes in v9:
time: 148 us; the launch traced here: 147 us
  Pallas kernels  48.9 us (33%)
  other arithmetic  30.6 us (21%)
  matrix products  25.6 us (17%)
  waiting for transfers between devices  15.1 us (10%)
  local copies, waits for them, and re-layouts  13.9 us (9%)
  starting transfers between devices  11.9 us (8%)
    pallas_call x1, Pallas kernels, exchange_and_sum(): pl.pallas_call(functools.partial(exchange_kernel, count, domains, share,...  48.9 us
    dot_general x18, matrix products, pair_product(): lax.dot_general(left, right, (((1, 2, 3), (1, 2, 3)), ((), ())), preferre...  24.3 us
    convert_element_type x2, other arithmetic, on_device(): stencil(ext, potential).astype(jnp.bfloat16)  11.6 us
    convert_element_type x3, other arithmetic, stencil(): centre_cells = extended[:, 1:-1, 1:-1, :].astype(jnp.float32)  8.45 us
    ppermute x1, waiting for transfers between devices, on_device(): row_above = lax.ppermute(masked[:, :, second_cells - 1], 'mat', up)  8.26 us
    ppermute x2, starting transfers between devices, passed_along(): return lax.ppermute(block, axis, route)  7.75 us
    unnamed x20, local copies, waits for them, and re-layouts  6.85 us
    ppermute x2, waiting for transfers between devices, passed_along(): return lax.ppermute(block, axis, route)  6.41 us
  transfers between devices with their start and end apart: 6, of which 3 were waited for; matrix products, arithmetic and copies ran while one was open for 16% of the time, Pallas kernels for 0%

profile of v9, /device:TPU:6, one launch (start us, length us, event | category | flops | bytes accessed | tf_op | source)
XLA Modules:
  0.0 146.9 jit_solution(16677072762223111027)
XLA Ops:
  2.9 5.9 %fusion.1 = bf16[256,12,8,128]{3,0,2,1:T(8,128)(2,1)S(1)} fusion(bf16[256,12,8,128]{3,2,1,0:T(8,128)(2,1)} %param.6, s32[256,128]{1,0:T(8,128)S(1)} %subtract_multiply_fusion, s32[256,12,8]{0,2,1:T(8,128)S(1)} %broadcast_add_fusion, pred[12]{0:T(512)(128)(4,1)S(1)} %compare_and_fusion), kind=kLoop, calls=%fused_computation.2 | loop fusion | flops 12582912 | bytes 12812300 | tf_op jit(solution)/shard_map/jit(_where)/select_n | solution.py:237
  8.9 4.0 %slice_convert_fusion.2 = (f32[256,4,8,128]{3,0,2,1:T(8,128)}, bf16[256,4,8,128]{3,0,2,1:T(8,128)(2,1)}, bf16[256,4,8,128]{3,0,2,1:T(8,128)(2,1)}) fusion(bf16[256,12,8,128]{3,0,2,1:T(8,128)(2,1)S(1)} %fusion.1), kind=kLoop, calls=%fused_computation.72 | loop fusion | flops 1048576 | bytes 14680064 | tf_op jit(solution)/shard_map/convert_element_type | solution.py:57
  12.9 7.7 %collective-permute-start.1 = (bf16[256,4,8,128]{3,0,2,1:T(8,128)(2,1)}, bf16[256,4,8,128]{3,0,2,1:T(8,128)(2,1)}, u32[]{:S(2)}, u32[]{:S(2)}) collective-permute-start(bf16[256,4,8,128]{3,0,2,1:T(8,128)(2,1)} %get-tuple-element.5), channel_id=1, source_target_pairs={{4,0},{8,4},{12,8},{16,12},{20,16},{24,20},{28,24},{32,28},{36,32}... | collective-permute-start | bytes 6291464 | tf_op jit(solution)/shard_map/ppermute | solution.py:26
  22.1 1.5 %collective-permute-start.4 = (bf16[256,12,128]{2,0,1:T(8,128)(2,1)S(1)}, bf16[256,12,128]{2,0,1:T(8,128)(2,1)}, u32[]{:S(2)}, u32[]{:S(2)}) collective-permute-start(bf16[256,12,128]{2,0,1:T(8,128)(2,1)S(1)} %get-tuple-element.2), channel_id=1, source_target_pairs={{1,0},{2,1},{3,2},{0,3},{5,4},{6,5},{7,6},{4,7},{9,8},{10,9},{11,1... | collective-permute-start | bytes 2359304 | tf_op jit(solution)/shard_map/ppermute | solution.py:247
  23.9 2.8 %copy-done.1 = bf16[256,12,8,128]{3,0,2,1:T(8,128)(2,1)S(1)} copy-done((bf16[256,12,8,128]{3,0,2,1:T(8,128)(2,1)S(1)}, bf16[256,12,8,128]{3,0,2,1:T(8,128)(2,1)}, u32[]{:S(2)}) %copy-start.1) | copy-done | bytes 6291480
  27.4 8.3 %collective-permute-done.5 = bf16[256,12,128]{2,0,1:T(8,128)(2,1)} collective-permute-done((bf16[256,12,128]{2,0,1:T(8,128)(2,1)}, bf16[256,12,128]{2,0,1:T(8,128)(2,1)}, u32[]{:S(2)}, u32[]{:S(2)}) %collective-permute-start.5) | collective-permute-done | bytes 786464 | tf_op jit(solution)/shard_map/ppermute | solution.py:246
  38.1 6.4 %collective-permute-done = bf16[256,4,8,128]{3,0,2,1:T(8,128)(2,1)S(1)} collective-permute-done((bf16[256,4,8,128]{3,0,2,1:T(8,128)(2,1)}, bf16[256,4,8,128]{3,0,2,1:T(8,128)(2,1)S(1)}, u32[]{:S(2)}, u32[]{:S(2)}) %collective-permute-start) | collective-permute-done | bytes 2097184 | tf_op jit(solution)/shard_map/ppermute | solution.py:26
  46.2 1.5 %collective-permute-start.3 = (bf16[2,256,4,128]{3,1,2,0:T(8,128)(2,1)S(1)}, bf16[2,256,4,128]{3,1,2,0:T(8,128)(2,1)S(1)}, u32[]{:S(2)}, u32[]{:S(2)}) collective-permute-start(bf16[2,256,4,128]{3,1,2,0:T(8,128)(2,1)S(1)} %get-tuple-element.8), channel_id=1, source_target_pairs={{1,0},{2,1},{3,2},{0,3},{5,4},{6,5},{7,6},{4,7},{9,8},{10,9},{11,1... | collective-permute-start | bytes 1572872 | tf_op jit(solution)/shard_map/ppermute | solution.py:250
  47.8 1.7 %convolution_bitcast_fusion.5 = f32[1,256,256]{2,1,0:T(8,128)S(1)} fusion(bf16[256,4,8,128]{3,0,2,1:T(8,128)(2,1)} %collective-permute-done.1, bf16[256,4,8,128]{3,0,2,1:T(8,128)(2,1)S(1)} %collective-permute-done), kind=kOutput, calls=%fused_computation.54 | convolution fusion | flops 268435456 | bytes 3407872 | tf_op jit(solution)/shard_map/dot_general | solution.py:72
  51.7 2.0 %fusion.31 = f32[1,256,256]{2,1,0:T(8,128)S(1)} fusion(bf16[256,4,8,128]{3,0,2,1:T(8,128)(2,1)} %collective-permute-done.1, bf16[256,12,8,128]{3,0,2,1:T(8,128)(2,1)S(1)} %copy-done.1), kind=kOutput, calls=%fused_computation.56 | convolution fusion | flops 402653184 | bytes 3932160 | tf_op jit(solution)/shard_map/dot_general | solution.py:72
  53.8 1.7 %convolution_bitcast_fusion.4 = f32[1,256,256]{2,1,0:T(8,128)S(1)} fusion(bf16[256,4,8,128]{3,0,2,1:T(8,128)(2,1)S(1)} %collective-permute-done, bf16[256,4,8,128]{3,0,2,1:T(8,128)(2,1)} %collective-permute-done.1), kind=kOutput, calls=%fused_computation.53 | convolution fusion | flops 268435456 | bytes 3407872 | tf_op jit(solution)/shard_map/dot_general | solution.py:72
  55.5 2.0 %convolution_bitcast_fusion.1 = f32[1,256,256]{2,1,0:T(8,128)S(1)} fusion(bf16[256,12,8,128]{3,0,2,1:T(8,128)(2,1)S(1)} %copy-done.1, bf16[256,4,8,128]{3,0,2,1:T(8,128)(2,1)} %collective-permute-done.1), kind=kOutput, calls=%fused_computation.50 | convolution fusion | flops 402653184 | bytes 8126464 | tf_op jit(solution)/shard_map/dot_general | solution.py:72
  57.5 2.5 %convolution_bitcast_fusion.9 = f32[1,256,256]{2,1,0:T(8,128)S(1)} fusion(bf16[256,4,8,128]{3,0,2,1:T(8,128)(2,1)} %collective-permute-done.1), kind=kOutput, calls=%fused_computation.60 | convolution fusion | flops 402653184 | bytes 3932160 | tf_op jit(solution)/shard_map/dot_general | solution.py:72
  60.6 2.3 %concatenate.39 = bf16[256,6,8,128]{3,0,2,1:T(8,128)(2,1)S(1)} pad(bf16[256,4,8,128]{3,0,2,1:T(8,128)(2,1)} %collective-permute-done.1, bf16[]{:T(256)} %constant.60.clone.1), padding=0_0x2_0x0_0x0_0 | pad | bytes 5242882 | tf_op jit(solution)/shard_map/concatenate | solution.py:268
  62.9 4.0 %slice_convert_fusion = f32[256,4,8,128]{3,0,2,1:T(8,128)} fusion(bf16[256,4,8,128]{3,0,2,1:T(8,128)(2,1)} %collective-permute-done.1), kind=kLoop, calls=%fused_computation.34 | loop fusion | flops 1048576 | bytes 6291456 | tf_op jit(solution)/shard_map/convert_element_type | solution.py:57
  67.4 1.8 %copy-done.2 = f32[256,4,8,128]{3,0,2,1:T(8,128)S(1)} copy-done((f32[256,4,8,128]{3,0,2,1:T(8,128)S(1)}, f32[256,4,8,128]{3,0,2,1:T(8,128)}, u32[]{:S(2)}) %copy-start.2) | copy-done | bytes 4194328
  70.2 7.1 %fusion.7 = (bf16[256,4,8,128]{3,0,2,1:T(8,128)(2,1)}, bf16[256,4,8,128]{3,0,2,1:T(8,128)(2,1)}) fusion(f32[256,4,8,128]{3,0,2,1:T(8,128)S(1)} %slice_convert_fusion.1, bf16[256,4,8,128]{3,0,2,1:T(8,128)(2,1)S(1)} %collective-permute-done, bf16[256,6,8,128]{3,0,2,1:T(8,128)(2,1)S(1)} %concatenate.33, bf16[256,6,1,128]{3,0,2,1:T(8,128)(2,1)S(1)} %get-tuple-element.12, ...), kind=kLoop, calls=%fused_computation.15 | loop fusion | flops 35651584 | bytes 28852224 | tf_op jit(solution)/shard_map/convert_element_type | solution.py:286
  77.3 2.5 %convolution_bitcast_fusion.16 = f32[1,256,256]{2,1,0:T(8,128)S(1)} fusion(bf16[256,4,8,128]{3,0,2,1:T(8,128)(2,1)} %get-tuple-element.19, bf16[256,12,8,128]{3,0,2,1:T(8,128)(2,1)S(1)} %bitcast.195), kind=kOutput, calls=%fused_computation.67 | convolution fusion | flops 536870912 | bytes 4456448 | tf_op jit(solution)/shard_map/dot_general | solution.py:72
  80.6 1.4 copy-done.3
  82.0 4.5 %fusion.19 = bf16[256,4,8,128]{3,0,2,1:T(8,128)(2,1)S(1)} fusion(f32[256,4,8,128]{3,0,2,1:T(8,128)S(1)} %copy-done.3, bf16[256,4,8,128]{3,0,2,1:T(8,128)(2,1)} %collective-permute-done.1, bf16[256,6,8,128]{3,0,2,1:T(8,128)(2,1)S(1)} %concatenate.39, bf16[256,6,1,128]{3,0,2,1:T(8,128)(2,1)S(1)} %get-tuple-element.14, ...), kind=kLoop, calls=%fused_computation.27 | loop fusion | flops 17825792 | bytes 14434304 | tf_op jit(solution)/shard_map/convert_element_type | solution.py:286
  90.3 2.0 %convolution_bitcast_fusion.8 = f32[1,256,256]{2,1,0:T(8,128)S(1)} fusion(bf16[256,4,8,128]{3,0,2,1:T(8,128)(2,1)S(1)} %copy-done.5, bf16[256,4,8,128]{3,0,2,1:T(8,128)(2,1)} %collective-permute-done.1), kind=kOutput, calls=%fused_computation.59 | convolution fusion | flops 402653184 | bytes 3932160 | tf_op jit(solution)/shard_map/dot_general | solution.py:72
  92.3 2.0 %convolution_bitcast_fusion.7 = f32[1,256,256]{2,1,0:T(8,128)S(1)} fusion(bf16[256,4,8,128]{3,0,2,1:T(8,128)(2,1)S(1)} %copy-done.4, bf16[256,4,8,128]{3,0,2,1:T(8,128)(2,1)} %collective-permute-done.1), kind=kOutput, calls=%fused_computation.58 | convolution fusion | flops 402653184 | bytes 3932160 | tf_op jit(solution)/shard_map/dot_general | solution.py:72
  94.3 2.0 %convolution_bitcast_fusion.6 = f32[1,256,256]{2,1,0:T(8,128)S(1)} fusion(bf16[256,4,8,128]{3,0,2,1:T(8,128)(2,1)S(1)} %fusion.19, bf16[256,4,8,128]{3,0,2,1:T(8,128)(2,1)} %collective-permute-done.1), kind=kOutput, calls=%fused_computation.57 | convolution fusion | flops 402653184 | bytes 3932160 | tf_op jit(solution)/shard_map/dot_general | solution.py:72
  96.9 48.9 %shard_map.77 = f32[2,5,64,256]{3,2,1,0:T(8,128)S(1)} custom-call(f32[3,2,3,256,256]{4,3,2,1,0:T(8,128)S(1)} %pad_maximum_fusion.x_ref), custom_call_target="tpu_custom_call" | custom-call | tf_op jit(solution)/shard_map/pallas_call | solution.py:197
  (68 shorter events, 19.2 us)
Async XLA Ops:
  8.9 11.8 %copy-start = (bf16[256,12,8,128]{3,0,2,1:T(8,128)(2,1)}, bf16[256,12,8,128]{3,0,2,1:T(8,128)(2,1)S(1)}, u32[]{:S(2)}) copy-start(bf16[256,12,8,128]{3,0,2,1:T(8,128)(2,1)S(1)} %fusion.1) | copy-start | bytes 18874372
  12.9 10.8 %copy-start.7 = (s32[2,5,2]{1,2,0:T(2,128)S(1)}, s32[2,5,2]{1,2,0:T(2,128)}, u32[]{:S(2)}) copy-start(s32[2,5,2]{1,2,0:T(2,128)} %param.11) | copy-start | bytes 244
  12.9 31.7 %collective-permute-start = (bf16[256,4,8,128]{3,0,2,1:T(8,128)(2,1)}, bf16[256,4,8,128]{3,0,2,1:T(8,128)(2,1)S(1)}, u32[]{:S(2)}, u32[]{:S(2)}) collective-permute-start(bf16[256,4,8,128]{3,0,2,1:T(8,128)(2,1)} %get-tuple-element.6), channel_id=1, source_target_pairs={{252,0},{0,4},{4,8},{8,12},{12,16},{16,20},{20,24},{24,28},{28,32}... | collective-permute-start | bytes 6291464 | tf_op jit(solution)/shard_map/ppermute | solution.py:26
  12.9 31.7 %collective-permute-start.1 = (bf16[256,4,8,128]{3,0,2,1:T(8,128)(2,1)}, bf16[256,4,8,128]{3,0,2,1:T(8,128)(2,1)}, u32[]{:S(2)}, u32[]{:S(2)}) collective-permute-start(bf16[256,4,8,128]{3,0,2,1:T(8,128)(2,1)} %get-tuple-element.5), channel_id=1, source_target_pairs={{4,0},{8,4},{12,8},{16,12},{20,16},{24,20},{28,24},{32,28},{36,32}... | collective-permute-start | bytes 6291464 | tf_op jit(solution)/shard_map/ppermute | solution.py:26
  21.6 14.0 %collective-permute-start.5 = (bf16[256,12,128]{2,0,1:T(8,128)(2,1)}, bf16[256,12,128]{2,0,1:T(8,128)(2,1)}, u32[]{:S(2)}, u32[]{:S(2)}) collective-permute-start(bf16[256,12,128]{2,0,1:T(8,128)(2,1)} %get-tuple-element.3), channel_id=1, source_target_pairs={{0,1},{1,2},{2,3},{3,0},{4,5},{5,6},{6,7},{7,4},{8,9},{9,10},{10,1... | collective-permute-start | bytes 2359304 | tf_op jit(solution)/shard_map/ppermute | solution.py:246
  22.1 15.0 %collective-permute-start.4 = (bf16[256,12,128]{2,0,1:T(8,128)(2,1)S(1)}, bf16[256,12,128]{2,0,1:T(8,128)(2,1)}, u32[]{:S(2)}, u32[]{:S(2)}) collective-permute-start(bf16[256,12,128]{2,0,1:T(8,128)(2,1)S(1)} %get-tuple-element.2), channel_id=1, source_target_pairs={{1,0},{2,1},{3,2},{0,3},{5,4},{6,5},{7,6},{4,7},{9,8},{10,9},{11,1... | collective-permute-start | bytes 2359304 | tf_op jit(solution)/shard_map/ppermute | solution.py:247
  23.9 2.8 %copy-start.1 = (bf16[256,12,8,128]{3,0,2,1:T(8,128)(2,1)S(1)}, bf16[256,12,8,128]{3,0,2,1:T(8,128)(2,1)}, u32[]{:S(2)}) copy-start(bf16[256,12,8,128]{3,0,2,1:T(8,128)(2,1)} %copy-done) | copy-start | bytes 18874372
  45.7 21.3 %collective-permute-start.2 = (bf16[2,256,4,128]{3,1,2,0:T(8,128)(2,1)S(1)}, bf16[2,256,4,128]{3,1,2,0:T(8,128)(2,1)S(1)}, u32[]{:S(2)}, u32[]{:S(2)}) collective-permute-start(bf16[2,256,4,128]{3,1,2,0:T(8,128)(2,1)S(1)} %get-tuple-element.7), channel_id=1, source_target_pairs={{0,1},{1,2},{2,3},{3,0},{4,5},{5,6},{6,7},{7,4},{8,9},{9,10},{10,1... | collective-permute-start | bytes 1572872 | tf_op jit(solution)/shard_map/ppermute | solution.py:249
  46.2 20.8 %collective-permute-start.3 = (bf16[2,256,4,128]{3,1,2,0:T(8,128)(2,1)S(1)}, bf16[2,256,4,128]{3,1,2,0:T(8,128)(2,1)S(1)}, u32[]{:S(2)}, u32[]{:S(2)}) collective-permute-start(bf16[2,256,4,128]{3,1,2,0:T(8,128)(2,1)S(1)} %get-tuple-element.8), channel_id=1, source_target_pairs={{1,0},{2,1},{3,2},{0,3},{5,4},{6,5},{7,6},{4,7},{9,8},{10,9},{11,1... | collective-permute-start | bytes 1572872 | tf_op jit(solution)/shard_map/ppermute | solution.py:250
  60.6 6.7 %slice-start = ((s8[6291456]{0:T(1024)(128)(4,1)}), s8[4194304]{0:T(1024)(128)(4,1)S(1)}, s32[]{:S(2)}) async-start(s8[6291456]{0:T(1024)(128)(4,1)} %bitcast.194), calls=%async_computation | async-start | bytes 8388608
  62.9 4.5 %slice-start.1 = ((s8[6291456]{0:T(1024)(128)(4,1)}), s8[2097152]{0:T(1024)(128)(4,1)S(1)}, s32[]{:S(2)}) async-start(s8[6291456]{0:T(1024)(128)(4,1)} %bitcast.194), calls=%async_computation.1 | async-start | bytes 4194304
  67.0 2.2 %copy-start.2 = (f32[256,4,8,128]{3,0,2,1:T(8,128)S(1)}, f32[256,4,8,128]{3,0,2,1:T(8,128)}, u32[]{:S(2)}) copy-start(f32[256,4,8,128]{3,0,2,1:T(8,128)} %get-tuple-element.4) | copy-start | bytes 12582916
  67.0 2.1 %copy-start.6 = (f32[4,8,128]{2,1,0:T(8,128)S(1)}, f32[4,8,128]{2,1,0:T(8,128)}, u32[]{:S(2)}) copy-start(f32[4,8,128]{2,1,0:T(8,128)} %param.7) | copy-start | bytes 49156
  67.2 3.0 %slice-start.2 = ((bf16[256,12,8,128]{3,0,2,1:T(8,128)(2,1)}), bf16[256,6,8,128]{3,0,2,1:T(8,128)(2,1)S(1)}, s32[]{:S(2)}) async-start(bf16[256,12,8,128]{3,0,2,1:T(8,128)(2,1)} %copy-done), calls=%async_computation.2 | async-start | bytes 6291456 | tf_op jit(solution)/shard_map/slice | solution.py:260
  77.3 2.5 %copy-start.4 = (bf16[256,4,8,128]{3,0,2,1:T(8,128)(2,1)S(1)}, bf16[256,4,8,128]{3,0,2,1:T(8,128)(2,1)}, u32[]{:S(2)}) copy-start(bf16[256,4,8,128]{3,0,2,1:T(8,128)(2,1)} %get-tuple-element.20) | copy-start | bytes 6291460
  79.8 2.2 %copy-start.3 = (f32[256,4,8,128]{3,0,2,1:T(8,128)S(1)}, f32[256,4,8,128]{3,0,2,1:T(8,128)}, u32[]{:S(2)}) copy-start(f32[256,4,8,128]{3,0,2,1:T(8,128)} %slice_convert_fusion) | copy-start | bytes 12582916
  86.5 1.6 %copy-start.5 = (bf16[256,4,8,128]{3,0,2,1:T(8,128)(2,1)S(1)}, bf16[256,4,8,128]{3,0,2,1:T(8,128)(2,1)}, u32[]{:S(2)}) copy-start(bf16[256,4,8,128]{3,0,2,1:T(8,128)(2,1)} %get-tuple-element.19) | copy-start | bytes 6291460

commit v10 on v7

--- a/solution.py
+++ b/solution.py
@@ -276,11 +276,19 @@
     applied_slots = [
         stencil(ext, potential).astype(jnp.bfloat16) for ext in (left_ext, own_ext, right_ext)
     ]
+    gram_blocks = {}
+
+    def gram_block(a, b):
+        if (b, a) in gram_blocks:
+            return gram_blocks[(b, a)].T
+        gram_blocks[(a, b)] = pair_product(phi_slots[a], phi_slots[b])
+        return gram_blocks[(a, b)]
+
     full = jnp.stack(
         [
             jnp.stack(
                 [
-                    jnp.stack([pair_product(phi_slots[a], phi_slots[b]) for a in range(3)]),
+                    jnp.stack([gram_block(a, b) for a in range(3)]),
                     jnp.stack([pair_product(applied_slots[a], phi_slots[b]) for a in range(3)]),
                 ]
             )

time: 141 us -> 153 us (1.085)
  local copies, waits for them, and re-layouts: 15.4 us -> 23 us
  other arithmetic: 30.6 us -> 36.4 us
    dot_general x0 -> x3, local copies, waits for them, and re-layouts: none -> 3.71 us  [pair_product(): lax.dot_general(left, right, (((1, 2, 3), (1, 2, 3)), ((), ())), preferre...]
    convert_element_type x3, other arithmetic: 8.43 us -> 11 us  [stencil(): centre_cells = extended[:, 1:-1, 1:-1, :].astype(jnp.float32)]
    another operation x10, other arithmetic: 1.03 us -> 3.16 us  [the longest x6 2.45 us: on_device(): jnp.stack([jnp.stack([gram_block(a, b) for a in range(3)]), jnp.stack([pa...]
    slice x2, local copies, waits for them, and re-layouts: 0.07 us -> 2.13 us  [on_device(): rows_from_left = jnp.stack([arrived_above[0], arrived_below[0]])]
    unnamed x28 -> x34, local copies, waits for them, and re-layouts: 6.14 us -> 7.27 us
    dot_general x18 -> x15, matrix products: 17.9 us -> 18 us  [pair_product(): lax.dot_general(left, right, (((1, 2, 3), (1, 2, 3)), ((), ())), preferre...]
  transfers between devices with their start and end apart: 6 -> 6, of which waited for: 3 -> 3; matrix products, arithmetic and copies ran while one was open for 13% -> 21% of each run, Pallas kernels for 0% -> 0%
where the time goes in v10:
time: 153 us
  Pallas kernels  47.4 us (31%)
  other arithmetic  36.4 us (24%)
  local copies, waits for them, and re-layouts  23 us (15%)
  matrix products  19.3 us (13%)
  waiting for transfers between devices  13.6 us (9%)
  starting transfers between devices  11.8 us (8%)
    pallas_call x1, Pallas kernels, exchange_and_sum(): pl.pallas_call(functools.partial(exchange_kernel, count, domains, share,...  47.4 us
    dot_general x15, matrix products, pair_product(): lax.dot_general(left, right, (((1, 2, 3), (1, 2, 3)), ((), ())), preferre...  18 us
    convert_element_type x2, other arithmetic, on_device(): stencil(ext, potential).astype(jnp.bfloat16)  11.7 us
    convert_element_type x3, other arithmetic, stencil(): centre_cells = extended[:, 1:-1, 1:-1, :].astype(jnp.float32)  11 us
    ppermute x2, starting transfers between devices, passed_along(): return lax.ppermute(block, axis, route)  7.75 us
    ppermute x1, waiting for transfers between devices, on_device(): row_above = lax.ppermute(masked[:, :, second_cells - 1], 'mat', up)  7.54 us
    unnamed x34, local copies, waits for them, and re-layouts  7.27 us
    select_n x1, other arithmetic, on_device(): masked = jnp.where(inside, orbitals, jnp.zeros_like(orbitals))  5.94 us
  transfers between devices with their start and end apart: 6, of which 3 were waited for; matrix products, arithmetic and copies ran while one was open for 21% of the time, Pallas kernels for 0%

profile of v10, /device:TPU:6, one launch (start us, length us, event | category | flops | bytes accessed | tf_op | source)
XLA Modules:
  0.0 152.6 jit_solution(4889763736141886438)
XLA Ops:
  2.9 5.9 %fusion.1 = bf16[256,12,8,128]{3,0,2,1:T(8,128)(2,1)S(1)} fusion(bf16[256,12,8,128]{3,2,1,0:T(8,128)(2,1)} %param.6, s32[256,128]{1,0:T(8,128)S(1)} %subtract_multiply_fusion, s32[256,12,8]{0,2,1:T(8,128)S(1)} %broadcast_add_fusion, pred[12]{0:T(512)(128)(4,1)S(1)} %compare_and_fusion), kind=kLoop, calls=%fused_computation.2 | loop fusion | flops 12582912 | bytes 12812300 | tf_op jit(solution)/shard_map/jit(_where)/select_n | solution.py:237
  8.9 4.0 %slice_convert_fusion.2 = (f32[256,4,8,128]{3,0,2,1:T(8,128)}, bf16[256,4,8,128]{3,0,2,1:T(8,128)(2,1)}, bf16[256,4,8,128]{3,0,2,1:T(8,128)(2,1)}) fusion(bf16[256,12,8,128]{3,0,2,1:T(8,128)(2,1)S(1)} %fusion.1), kind=kLoop, calls=%fused_computation.83 | loop fusion | flops 1048576 | bytes 14680064 | tf_op jit(solution)/shard_map/convert_element_type | solution.py:57
  12.9 7.7 %collective-permute-start.1 = (bf16[256,4,8,128]{3,0,2,1:T(8,128)(2,1)}, bf16[256,4,8,128]{3,0,2,1:T(8,128)(2,1)}, u32[]{:S(2)}, u32[]{:S(2)}) collective-permute-start(bf16[256,4,8,128]{3,0,2,1:T(8,128)(2,1)} %get-tuple-element.5), channel_id=1, source_target_pairs={{4,0},{8,4},{12,8},{16,12},{20,16},{24,20},{28,24},{32,28},{36,32}... | collective-permute-start | bytes 6291464 | tf_op jit(solution)/shard_map/ppermute | solution.py:26
  22.1 1.5 %collective-permute-start.4 = (bf16[256,12,128]{2,0,1:T(8,128)(2,1)S(1)}, bf16[256,12,128]{2,0,1:T(8,128)(2,1)}, u32[]{:S(2)}, u32[]{:S(2)}) collective-permute-start(bf16[256,12,128]{2,0,1:T(8,128)(2,1)S(1)} %get-tuple-element.2), channel_id=1, source_target_pairs={{1,0},{2,1},{3,2},{0,3},{5,4},{6,5},{7,6},{4,7},{9,8},{10,9},{11,1... | collective-permute-start | bytes 2359304 | tf_op jit(solution)/shard_map/ppermute | solution.py:247
  23.9 2.8 %copy-done.1 = bf16[256,12,8,128]{3,0,2,1:T(8,128)(2,1)S(1)} copy-done((bf16[256,12,8,128]{3,0,2,1:T(8,128)(2,1)S(1)}, bf16[256,12,8,128]{3,0,2,1:T(8,128)(2,1)}, u32[]{:S(2)}) %copy-start.1) | copy-done | bytes 6291480
  26.7 1.5 convolution_bitcast_fusion.1
  28.2 7.5 %collective-permute-done.5 = bf16[256,12,128]{2,0,1:T(8,128)(2,1)} collective-permute-done((bf16[256,12,128]{2,0,1:T(8,128)(2,1)}, bf16[256,12,128]{2,0,1:T(8,128)(2,1)}, u32[]{:S(2)}, u32[]{:S(2)}) %collective-permute-start.5) | collective-permute-done | bytes 786464 | tf_op jit(solution)/shard_map/ppermute | solution.py:246
  37.1 1.8 %slice_bitcast_fusion.5 = bf16[256,6,1,128]{3,0,2,1:T(8,128)(2,1)} fusion(bf16[256,12,128]{2,0,1:T(8,128)(2,1)} %collective-permute-done.4), kind=kLoop, calls=%fused_computation.101 | loop fusion | bytes 786432 | tf_op jit(solution)/shard_map/broadcast_in_dim;squeeze;stack | solution.py:255
  38.9 5.7 %collective-permute-done = bf16[256,4,8,128]{3,0,2,1:T(8,128)(2,1)S(1)} collective-permute-done((bf16[256,4,8,128]{3,0,2,1:T(8,128)(2,1)}, bf16[256,4,8,128]{3,0,2,1:T(8,128)(2,1)S(1)}, u32[]{:S(2)}, u32[]{:S(2)}) %collective-permute-start) | collective-permute-done | bytes 2097184 | tf_op jit(solution)/shard_map/ppermute | solution.py:26
  46.1 2.2 %maximum_bitcast_fusion.9 = (bf16[2,256,4,128]{3,1,2,0:T(8,128)(2,1)}, bf16[2,256,4,128]{3,1,2,0:T(8,128)(2,1)}) fusion(bf16[1,256,4,8,128]{4,1,3,2,0:T(8,128)(2,1)} %bitcast.11, bf16[1,256,4,8,128]{4,1,3,2,0:T(8,128)(2,1)S(1)} %bitcast.179), kind=kLoop, calls=%fused_computation.97 | loop fusion | flops 524288 | bytes 5242880 | tf_op jit(solution)/shard_map/squeeze | solution.py:249
  48.8 1.5 %collective-permute-start.3 = (bf16[2,256,4,128]{3,1,2,0:T(8,128)(2,1)}, bf16[2,256,4,128]{3,1,2,0:T(8,128)(2,1)}, u32[]{:S(2)}, u32[]{:S(2)}) collective-permute-start(bf16[2,256,4,128]{3,1,2,0:T(8,128)(2,1)} %get-tuple-element.8), channel_id=1, source_target_pairs={{1,0},{2,1},{3,2},{0,3},{5,4},{6,5},{7,6},{4,7},{9,8},{10,9},{11,1... | collective-permute-start | bytes 1572872 | tf_op jit(solution)/shard_map/ppermute | solution.py:250
  50.3 1.5 slice.165
  53.0 1.4 fusion.50
  54.4 2.4 %slice_convert_fusion.1 = f32[256,4,8,128]{3,0,2,1:T(8,128)} fusion(bf16[256,4,8,128]{3,0,2,1:T(8,128)(2,1)S(1)} %collective-permute-done), kind=kLoop, calls=%fused_computation.55 | loop fusion | flops 1048576 | bytes 6291456 | tf_op jit(solution)/shard_map/convert_element_type | solution.py:57
  56.8 2.1 %fusion.26 = f32[256,256,1,1]{1,0,3,2:T(8,128)S(1)} fusion(bf16[256,3,8,128]{3,0,2,1:T(8,128)(2,1)S(1)} %slice.163, bf16[256,4,8,128]{3,0,2,1:T(8,128)(2,1)} %collective-permute-done.1), kind=kOutput, calls=%fused_computation.34 | convolution fusion | flops 402653184 | bytes 3407872 | tf_op jit(solution)/shard_map/dot_general | solution.py:72
  58.9 3.0 %fusion.70 = f32[256,256,1,1]{1,0,3,2:T(8,128)} fusion(bf16[256,12,8,128]{3,0,2,1:T(8,128)(2,1)S(1)} %copy-done.1, bf16[256,4,8,128]{3,0,2,1:T(8,128)(2,1)} %collective-permute-done.1), kind=kOutput, calls=%fused_computation.80 | convolution fusion | flops 402653184 | bytes 3932160 | tf_op jit(solution)/shard_map/dot_general | solution.py:72
  63.9 1.8 %copy.18 = f32[256,256]{0,1:T(8,128)} copy(f32[256,256]{1,0:T(8,128)} %bitcast.182) | data formatting | bytes 524288 | tf_op jit(solution)/shard_map/dot_general | solution.py:72
  68.4 2.3 %concatenate.47 = bf16[256,6,8,128]{3,0,2,1:T(8,128)(2,1)S(1)} pad(bf16[256,4,8,128]{3,0,2,1:T(8,128)(2,1)} %collective-permute-done.1, bf16[]{:T(256)} %constant.61.clone.1), padding=0_0x2_0x0_0x0_0 | pad | bytes 5242882 | tf_op jit(solution)/shard_map/concatenate | solution.py:268
  70.7 4.6 %slice_convert_fusion = f32[256,4,8,128]{3,0,2,1:T(8,128)} fusion(bf16[256,4,8,128]{3,0,2,1:T(8,128)(2,1)} %collective-permute-done.1), kind=kLoop, calls=%fused_computation.54 | loop fusion | flops 1048576 | bytes 6291456 | tf_op jit(solution)/shard_map/convert_element_type | solution.py:57
  77.8 1.6 %slice-done.2 = bf16[256,6,8,128]{3,0,2,1:T(8,128)(2,1)S(1)} async-done(((bf16[256,12,8,128]{3,0,2,1:T(8,128)(2,1)}), bf16[256,6,8,128]{3,0,2,1:T(8,128)(2,1)S(1)}, s32[]{:S(2)}) %slice-start.2) | async-done | bytes 3145752 | tf_op jit(solution)/shard_map/slice | solution.py:260
  79.4 7.1 %fusion.7 = (bf16[256,4,8,128]{3,0,2,1:T(8,128)(2,1)}, bf16[256,4,8,128]{3,0,2,1:T(8,128)(2,1)}) fusion(f32[256,4,8,128]{3,0,2,1:T(8,128)S(1)} %copy-done.3, bf16[256,4,8,128]{3,0,2,1:T(8,128)(2,1)S(1)} %collective-permute-done, bf16[256,6,8,128]{3,0,2,1:T(8,128)(2,1)S(1)} %concatenate.41, bf16[256,6,1,128]{3,0,2,1:T(8,128)(2,1)S(1)} %get-tuple-element.12, ...), kind=kLoop, calls=%fused_computation.15 | loop fusion | flops 35651584 | bytes 28852224 | tf_op jit(solution)/shard_map/convert_element_type | solution.py:277
  86.5 2.9 %fusion.62 = f32[1,256,256]{2,1,0:T(8,128)S(1)} fusion(bf16[256,4,8,128]{3,0,2,1:T(8,128)(2,1)} %get-tuple-element.20, bf16[256,3,8,128]{3,0,2,1:T(8,128)(2,1)} %copy-done.8), kind=kOutput, calls=%fused_computation.73 | convolution fusion | flops 536870912 | bytes 3932160 | tf_op jit(solution)/shard_map/dot_general | solution.py:72
  94.4 4.5 %fusion.19 = bf16[256,4,8,128]{3,0,2,1:T(8,128)(2,1)S(1)} fusion(f32[256,4,8,128]{3,0,2,1:T(8,128)S(1)} %copy-done.4, bf16[256,4,8,128]{3,0,2,1:T(8,128)(2,1)} %collective-permute-done.1, bf16[256,6,8,128]{3,0,2,1:T(8,128)(2,1)S(1)} %concatenate.47, bf16[256,6,1,128]{3,0,2,1:T(8,128)(2,1)S(1)} %get-tuple-element.14, ...), kind=kLoop, calls=%fused_computation.27 | loop fusion | flops 17825792 | bytes 14434304 | tf_op jit(solution)/shard_map/convert_element_type | solution.py:277
  104.1 47.4 %shard_map.77 = f32[2,5,64,256]{3,2,1,0:T(8,128)S(1)} custom-call(f32[3,2,3,256,256]{4,3,2,1,0:T(8,128)S(1)} %pad_maximum_fusion.x_ref), custom_call_target="tpu_custom_call" | custom-call | tf_op jit(solution)/shard_map/pallas_call | solution.py:197
  (84 shorter events, 26.6 us)
Async XLA Ops:
  8.9 11.8 %copy-start = (bf16[256,12,8,128]{3,0,2,1:T(8,128)(2,1)}, bf16[256,12,8,128]{3,0,2,1:T(8,128)(2,1)S(1)}, u32[]{:S(2)}) copy-start(bf16[256,12,8,128]{3,0,2,1:T(8,128)(2,1)S(1)} %fusion.1) | copy-start | bytes 18874372
  12.9 10.8 %copy-start.14 = (s32[2,5,2]{1,2,0:T(2,128)S(1)}, s32[2,5,2]{1,2,0:T(2,128)}, u32[]{:S(2)}) copy-start(s32[2,5,2]{1,2,0:T(2,128)} %param.11) | copy-start | bytes 244
  12.9 31.7 %collective-permute-start = (bf16[256,4,8,128]{3,0,2,1:T(8,128)(2,1)}, bf16[256,4,8,128]{3,0,2,1:T(8,128)(2,1)S(1)}, u32[]{:S(2)}, u32[]{:S(2)}) collective-permute-start(bf16[256,4,8,128]{3,0,2,1:T(8,128)(2,1)} %get-tuple-element.6), channel_id=1, source_target_pairs={{252,0},{0,4},{4,8},{8,12},{12,16},{16,20},{20,24},{24,28},{28,32}... | collective-permute-start | bytes 6291464 | tf_op jit(solution)/shard_map/ppermute | solution.py:26
  12.9 33.2 %collective-permute-start.1 = (bf16[256,4,8,128]{3,0,2,1:T(8,128)(2,1)}, bf16[256,4,8,128]{3,0,2,1:T(8,128)(2,1)}, u32[]{:S(2)}, u32[]{:S(2)}) collective-permute-start(bf16[256,4,8,128]{3,0,2,1:T(8,128)(2,1)} %get-tuple-element.5), channel_id=1, source_target_pairs={{4,0},{8,4},{12,8},{16,12},{20,16},{24,20},{28,24},{32,28},{36,32}... | collective-permute-start | bytes 6291464 | tf_op jit(solution)/shard_map/ppermute | solution.py:26
  21.7 14.0 %collective-permute-start.5 = (bf16[256,12,128]{2,0,1:T(8,128)(2,1)}, bf16[256,12,128]{2,0,1:T(8,128)(2,1)}, u32[]{:S(2)}, u32[]{:S(2)}) collective-permute-start(bf16[256,12,128]{2,0,1:T(8,128)(2,1)} %get-tuple-element.3), channel_id=1, source_target_pairs={{0,1},{1,2},{2,3},{3,0},{4,5},{5,6},{6,7},{7,4},{8,9},{9,10},{10,1... | collective-permute-start | bytes 2359304 | tf_op jit(solution)/shard_map/ppermute | solution.py:246
  22.1 15.0 %collective-permute-start.4 = (bf16[256,12,128]{2,0,1:T(8,128)(2,1)S(1)}, bf16[256,12,128]{2,0,1:T(8,128)(2,1)}, u32[]{:S(2)}, u32[]{:S(2)}) collective-permute-start(bf16[256,12,128]{2,0,1:T(8,128)(2,1)S(1)} %get-tuple-element.2), channel_id=1, source_target_pairs={{1,0},{2,1},{3,2},{0,3},{5,4},{6,5},{7,6},{4,7},{9,8},{10,9},{11,1... | collective-permute-start | bytes 2359304 | tf_op jit(solution)/shard_map/ppermute | solution.py:247
  23.9 2.8 %copy-start.1 = (bf16[256,12,8,128]{3,0,2,1:T(8,128)(2,1)S(1)}, bf16[256,12,8,128]{3,0,2,1:T(8,128)(2,1)}, u32[]{:S(2)}) copy-start(bf16[256,12,8,128]{3,0,2,1:T(8,128)(2,1)} %copy-done) | copy-start | bytes 18874372
  44.7 12.1 %copy-start.8 = (bf16[256,3,8,128]{3,0,2,1:T(8,128)(2,1)}, bf16[256,3,8,128]{3,0,2,1:T(8,128)(2,1)S(1)}, u32[]{:S(2)}) copy-start(bf16[256,3,8,128]{3,0,2,1:T(8,128)(2,1)S(1)} %slice.163) | copy-start | bytes 4718596
  48.3 27.0 %collective-permute-start.2 = (bf16[2,256,4,128]{3,1,2,0:T(8,128)(2,1)}, bf16[2,256,4,128]{3,1,2,0:T(8,128)(2,1)}, u32[]{:S(2)}, u32[]{:S(2)}) collective-permute-start(bf16[2,256,4,128]{3,1,2,0:T(8,128)(2,1)} %get-tuple-element.7), channel_id=1, source_target_pairs={{0,1},{1,2},{2,3},{3,0},{4,5},{5,6},{6,7},{7,4},{8,9},{9,10},{10,1... | collective-permute-start | bytes 1572872 | tf_op jit(solution)/shard_map/ppermute | solution.py:249
  48.8 27.6 %collective-permute-start.3 = (bf16[2,256,4,128]{3,1,2,0:T(8,128)(2,1)}, bf16[2,256,4,128]{3,1,2,0:T(8,128)(2,1)}, u32[]{:S(2)}, u32[]{:S(2)}) collective-permute-start(bf16[2,256,4,128]{3,1,2,0:T(8,128)(2,1)} %get-tuple-element.8), channel_id=1, source_target_pairs={{1,0},{2,1},{3,2},{0,3},{5,4},{6,5},{7,6},{4,7},{9,8},{10,9},{11,1... | collective-permute-start | bytes 1572872 | tf_op jit(solution)/shard_map/ppermute | solution.py:250
  51.9 1.1 copy-start.10
  58.9 3.0 %copy-start.12 = (f32[256,256,1,1]{1,0,3,2:T(8,128)}, f32[256,256,1,1]{1,0,3,2:T(8,128)S(1)}, u32[]{:S(2)}) copy-start(f32[256,256,1,1]{1,0,3,2:T(8,128)S(1)} %fusion.26) | copy-start | bytes 786436
  67.9 9.8 %copy-start.7 = (bf16[256,6,1,128]{3,0,2,1:T(8,128)(2,1)S(1)}, bf16[256,6,1,128]{3,0,2,1:T(8,128)(2,1)}, u32[]{:S(2)}) copy-start(bf16[256,6,1,128]{3,0,2,1:T(8,128)(2,1)} %slice_bitcast_fusion.5) | copy-start | bytes 1179652
  67.9 9.8 %copy-start.13 = (f32[4,8,128]{2,1,0:T(8,128)S(1)}, f32[4,8,128]{2,1,0:T(8,128)}, u32[]{:S(2)}) copy-start(f32[4,8,128]{2,1,0:T(8,128)} %param.7) | copy-start | bytes 49156
  68.4 9.3 %slice-start = ((s8[6291456]{0:T(1024)(128)(4,1)}), s8[4194304]{0:T(1024)(128)(4,1)S(1)}, s32[]{:S(2)}) async-start(s8[6291456]{0:T(1024)(128)(4,1)} %bitcast.177), calls=%async_computation | async-start | bytes 8388608
  68.4 9.3 %copy-start.3 = (f32[256,4,8,128]{3,0,2,1:T(8,128)S(1)}, f32[256,4,8,128]{3,0,2,1:T(8,128)}, u32[]{:S(2)}) copy-start(f32[256,4,8,128]{3,0,2,1:T(8,128)} %slice_convert_fusion.1) | copy-start | bytes 12582916
  70.7 7.1 %slice-start.1 = ((s8[6291456]{0:T(1024)(128)(4,1)}), s8[2097152]{0:T(1024)(128)(4,1)S(1)}, s32[]{:S(2)}) async-start(s8[6291456]{0:T(1024)(128)(4,1)} %bitcast.177), calls=%async_computation.1 | async-start | bytes 4194304
  70.7 7.1 %copy-start.2 = (f32[256,4,8,128]{3,0,2,1:T(8,128)S(1)}, f32[256,4,8,128]{3,0,2,1:T(8,128)}, u32[]{:S(2)}) copy-start(f32[256,4,8,128]{3,0,2,1:T(8,128)} %get-tuple-element.4) | copy-start | bytes 12582916
  77.5 1.9 %slice-start.2 = ((bf16[256,12,8,128]{3,0,2,1:T(8,128)(2,1)}), bf16[256,6,8,128]{3,0,2,1:T(8,128)(2,1)S(1)}, s32[]{:S(2)}) async-start(bf16[256,12,8,128]{3,0,2,1:T(8,128)(2,1)} %copy-done), calls=%async_computation.2 | async-start | bytes 6291456 | tf_op jit(solution)/shard_map/slice | solution.py:260
  86.5 2.9 %copy-start.5 = (bf16[256,4,8,128]{3,0,2,1:T(8,128)(2,1)S(1)}, bf16[256,4,8,128]{3,0,2,1:T(8,128)(2,1)}, u32[]{:S(2)}) copy-start(bf16[256,4,8,128]{3,0,2,1:T(8,128)(2,1)} %get-tuple-element.20) | copy-start | bytes 6291460
  89.5 1.6 %copy-start.6 = (bf16[256,4,8,128]{3,0,2,1:T(8,128)(2,1)S(1)}, bf16[256,4,8,128]{3,0,2,1:T(8,128)(2,1)}, u32[]{:S(2)}) copy-start(bf16[256,4,8,128]{3,0,2,1:T(8,128)(2,1)} %get-tuple-element.19) | copy-start | bytes 6291460
  89.5 2.0 %copy-start.9 = (bf16[256,3,8,128]{3,0,2,1:T(8,128)(2,1)S(1)}, bf16[256,3,8,128]{3,0,2,1:T(8,128)(2,1)}, u32[]{:S(2)}) copy-start(bf16[256,3,8,128]{3,0,2,1:T(8,128)(2,1)} %copy-done.8) | copy-start | bytes 4718596
  92.3 2.2 %copy-start.4 = (f32[256,4,8,128]{3,0,2,1:T(8,128)S(1)}, f32[256,4,8,128]{3,0,2,1:T(8,128)}, u32[]{:S(2)}) copy-start(f32[256,4,8,128]{3,0,2,1:T(8,128)} %slice_convert_fusion) | copy-start | bytes 12582916
  99.7 1.4 copy-start.11
